TPU v7x, 32 devices: a whole 2x2x4 slice. The times are simulated.
32 devices in a mesh: rows: 8 (over z, y), sub: 4 (over x, core).
Axes of the slice: x: 2, y: 2, z: 4, core: 2. Of those that a mesh axis runs over, the one named last changes fastest.
Arguments:
- snaps_box: bfloat16 [8, 262144], P(None, ('rows', 'sub')), may hold values from -64 to 64
- box_order: int32 [8, 4, 4], P('rows'), may hold values from 0 to 3, as said below
- basis: bfloat16 [262144, 256], P(('rows', 'sub')), may hold values from -20 to 20
Outputs:
- new_modes: bfloat16 [8, 262144], P(None, ('rows', 'sub'))
- coeffs: float32 [8, 256], replicated
- r_factor: float32 [8, 8], replicated
Inputs may be any that keep to these rules, and one draw needn't show every extreme that they name: Each box_order[r, t, :] is a permutation of 0 to 3.
All inputs are finite; a program needn't handle non-finite values.
Results may differ from a plain program's by a relative error of at most 0.001.
The roundings to bfloat16 on the way count: a program that leaves them out, or rounds other values in their place, can miss the bound.
Values may be sent and summed in bfloat16 or wider, within the bound.
No kernel may reach another device: no remote copies, remote signals or barrier semaphores. Data moves between devices by JAX's collectives and lax.ppermute only.
A program may use at most 64 MiB of HBM per device.

v0:
```python
import jax
import jax.numpy as jnp
from jax import lax
from jax.sharding import PartitionSpec as P


def local(snaps_box, box_order, basis):
    snapcount = snaps_box.shape[0]
    local_cells = snaps_box.shape[1]
    groups = lax.axis_size("sub")
    block_len = local_cells // groups
    cell_total = local_cells * lax.axis_size("rows") * groups
    position = lax.axis_index("sub")
    order_row = lax.dynamic_index_in_dim(box_order[0], position, 0, keepdims=False)
    placing = (order_row[:, None] == jnp.arange(groups, dtype=jnp.int32)[None, :]).astype(
        jnp.bfloat16
    )
    blocks = snaps_box.reshape(snapcount, groups, block_len)
    received = lax.all_to_all(blocks, "sub", split_axis=1, concat_axis=1, tiled=True)
    placed = jnp.einsum("sp,asb->apb", placing, received, preferred_element_type=jnp.float32)
    snapshots = placed.astype(jnp.bfloat16).reshape(received.shape[0], local_cells)
    partial_value = jnp.dot(snapshots, basis, preferred_element_type=jnp.float32)
    raw_sums = lax.psum(partial_value, ("rows", "sub"))
    coeffs = raw_sums / cell_total
    rounded = coeffs.astype(jnp.bfloat16)
    fitted = lax.dot_general(
        rounded, basis, (((1,), (1,)), ((), ())), preferred_element_type=jnp.float32
    )
    residual, rounded = (snapshots.astype(jnp.float32) - fitted, rounded)
    local_gram = jnp.dot(residual, residual.T, precision=lax.Precision.HIGHEST) / cell_total
    wgram = lax.psum(local_gram, ("rows", "sub"))
    lower_tri = jnp.linalg.cholesky(wgram)
    r_factor = lower_tri.T
    modes = jax.scipy.linalg.solve_triangular(lower_tri, residual, lower=True)
    return (modes.astype(jnp.bfloat16), coeffs, r_factor)


def solution(mesh):
    return jax.shard_map(
        local,
        mesh=mesh,
        in_specs=(P(None, ("rows", "sub")), P("rows", None, None), P(("rows", "sub"), None)),
        out_specs=(P(None, ("rows", "sub")), P(), P()),
        check_vma=False,
    )
```

profile of v0, /device:TPU:0, one launch (start us, length us, event | category | flops | bytes accessed | tf_op | source)
XLA Modules:
  0.0 102.2 jit_solution(13893098348373837003)
XLA Ops:
  0.6 0.0 copy-start
  0.6 4.2 %all-to-all-start = ((bf16[8,4,2048]{2,0,1:T(8,128)(2,1)}), bf16[8,4,2048]{2,0,1:T(8,128)(2,1)S(1)}, u32[]{:S(2)}, u32[]{:S(2)}) async-start(bf16[8,4,2048]{2,0,1:T(8,128)(2,1)} %bitcast.30), calls=%async_computation | async-start | bytes 262144 | tf_op jit(solution)/shard_map/all_to_all | solution.py:19
  4.9 0.0 copy-done
  4.9 4.6 %all-to-all-done = bf16[8,4,2048]{2,0,1:T(8,128)(2,1)S(1)} async-done(((bf16[8,4,2048]{2,0,1:T(8,128)(2,1)}), bf16[8,4,2048]{2,0,1:T(8,128)(2,1)S(1)}, u32[]{:S(2)}, u32[]{:S(2)}) %all-to-all-start) | async-done | bytes 131104 | tf_op jit(solution)/shard_map/all_to_all | solution.py:19
  9.5 0.2 fusion
  9.7 0.1 copy.16
  9.8 2.8 %fusion.9 = f32[8,256]{1,0:T(8,128)S(1)} fusion(bf16[8,8192]{1,0:T(8,128)(2,1)S(1)} %bitcast.28, bf16[8192,256]{1,0:T(8,128)(2,1)} %param.5), kind=kOutput, calls=%fused_computation.22 | convolution fusion | flops 33554432 | bytes 4333568 | tf_op jit(solution)/shard_map/dot_general | solution.py:22
  12.6 40.1 %psum.14 = f32[8,256]{1,0:T(8,128)S(1)} all-reduce(f32[8,256]{1,0:T(8,128)S(1)} %fusion.9), channel_id=1, replica_groups=mesh['rows'=8,'sub'=4] {'rows','sub'}, use_global_device_ids=true, to_apply=%region_0.1 | all-reduce | flops 2048 | bytes 16384 | tf_op jit(solution)/shard_map/psum | solution.py:23
  52.7 0.0 copy-start.1
  52.7 3.4 %convolution_subtract_fusion = f32[8,8192]{1,0:T(8,128)S(1)} fusion(bf16[8192,256]{1,0:T(8,128)(2,1)} %param.5, bf16[8,8192]{1,0:T(8,128)(2,1)S(1)} %bitcast.29, f32[8,256]{1,0:T(8,128)S(1)} %broadcast_multiply_fusion), kind=kOutput, calls=%fused_computation | convolution fusion | flops 33687552 | bytes 4595712 | tf_op jit(solution)/shard_map/dot_general | solution.py:26
  56.1 0.7 convolution_multiply_fusion
  56.7 41.0 %psum.15 = f32[8,8]{0,1:T(8,128)S(1)} all-reduce(f32[8,8]{0,1:T(8,128)S(1)} %convolution_multiply_fusion), channel_id=1, replica_groups=mesh['rows'=8,'sub'=4] {'rows','sub'}, use_global_device_ids=true, to_apply=%region_1.2 | all-reduce | flops 64 | bytes 512 | tf_op jit(solution)/shard_map/psum | solution.py:31
  97.7 0.1 copy.12
  97.8 0.7 cholesky.16
  98.5 0.6 compare_reduce_fusion
  99.2 0.6 fusion.5
  99.8 0.7 copy.14
  100.5 0.6 custom-call.7
  101.1 1.1 %convolution_convert_fusion = bf16[8,8192]{1,0:T(8,128)(2,1)} fusion(f32[8,8192]{1,0:T(8,128)S(1)} %convolution_subtract_fusion, f32[1,8,8]{1,2,0:T(8,128)S(1)} %custom-call.7), kind=kOutput, calls=%fused_computation.1 | convolution fusion | flops 6356992 | bytes 393472 | tf_op jit(solution)/shard_map/jit(_solve_triangular)/triangular_solve | solution.py:34
  102.2 0.0 copy-done.1
  (4 shorter events, 0.1 us)
Async XLA Ops:
  0.6 4.3 %copy-start = (s32[1,4,4]{2,1,0:T(4,128)S(1)}, s32[1,4,4]{2,1,0:T(4,128)}, u32[]{:S(2)}) copy-start(s32[1,4,4]{2,1,0:T(4,128)} %param.4) | copy-start | bytes 196
  0.6 8.8 %all-to-all-start = ((bf16[8,4,2048]{2,0,1:T(8,128)(2,1)}), bf16[8,4,2048]{2,0,1:T(8,128)(2,1)S(1)}, u32[]{:S(2)}, u32[]{:S(2)}) async-start(bf16[8,4,2048]{2,0,1:T(8,128)(2,1)} %bitcast.30), calls=%async_computation | async-start | bytes 262144 | tf_op jit(solution)/shard_map/all_to_all | solution.py:19
  52.7 49.5 %copy-start.1 = (f32[8,256]{1,0:T(8,128)}, f32[8,256]{1,0:T(8,128)S(1)}, u32[]{:S(2)}) copy-start(f32[8,256]{1,0:T(8,128)S(1)} %broadcast_multiply_fusion) | copy-start | bytes 24580
where the time goes:
time: 103 us; the launch traced here: 102 us
  blocking collectives  81 us (79%)
  matrix products  8.17 us (8%)
  waiting for transfers between devices  4.59 us (4%)
  starting transfers between devices  4.25 us (4%)
  other arithmetic  2.68 us (3%)
    psum x1, blocking collectives, local(): wgram = lax.psum(local_gram, ('rows', 'sub'))  41 us
    psum x1, blocking collectives, local(): raw_sums = lax.psum(partial_value, ('rows', 'sub'))  40.1 us
    all_to_all x1, waiting for transfers between devices, local(): lax.all_to_all(blocks, 'sub', split_axis=1, concat_axis=1, tiled=True)  4.59 us
    all_to_all x1, starting transfers between devices, local(): lax.all_to_all(blocks, 'sub', split_axis=1, concat_axis=1, tiled=True)  4.25 us
    dot_general x1, matrix products, local(): lax.dot_general(rounded, basis, (((1,), (1,)), ((), ())), preferred_eleme...  3.38 us
    dot_general x1, matrix products, local(): jnp.dot(snapshots, basis, preferred_element_type=jnp.float32)  2.84 us
  transfers between devices with their start and end apart: 1, of which 1 were waited for; matrix products, arithmetic and copies ran while one was open for 0% of the time, Pallas kernels for 0%

commit v1 on v0

v1 whole, which is shorter than its diff:
```python
import jax
import jax.numpy as jnp
from jax import lax
from jax.experimental import pallas as pl
from jax.experimental.pallas import tpu as pltpu
from jax.sharding import PartitionSpec as P

AXES = ("rows", "sub")
HIGH = lax.Precision.HIGHEST
LANES = 128
GUARD = 1.0 / 64.0
VMEM = pl.BlockSpec(memory_space=pltpu.VMEM)
SMEM = pl.BlockSpec(memory_space=pltpu.SMEM)
F32 = jnp.float32
MB = 1 << 20


def nt(a, b, precision=None):
    return lax.dot_general(
        a, b, (((1,), (1,)), ((), ())), precision=precision, preferred_element_type=F32
    )


def lane_at_least(shape, bound):
    return lax.broadcasted_iota(jnp.int32, shape, len(shape) - 1) >= bound


def gram_kernel(basis_ref, fold_ref):
    rank = basis_ref.shape[1]
    half, quarter = rank // 2, rank // 4
    total = lax.dot_general(
        basis_ref[...], basis_ref[...], (((0,), (0,)), ((), ())), preferred_element_type=F32
    )
    upper = lane_at_least((quarter, half), quarter)
    fold_ref[0:quarter] = jnp.where(upper, 2.0, 1.0) * total[0:quarter, 0:half]
    fold_ref[quarter : 2 * quarter] = jnp.where(
        upper, total[quarter:half, 0:half], total[half : 3 * quarter, half:]
    )
    fold_ref[2 * quarter : 3 * quarter] = jnp.where(upper, 1.0, 2.0) * total[3 * quarter :, half:]
    fold_ref[3 * quarter : 3 * quarter + half] = 2.0 * total[0:half, half:]


def project_kernel(order_ref, snaps_ref, basis_ref, fold_ref, out_ref):
    groups, snapcount, block_len = snaps_ref.shape
    fold_rows = fold_ref.shape[0]
    rank = basis_ref.shape[1]
    raw = jnp.zeros((snapcount, rank), F32)
    own = jnp.zeros((snapcount, snapcount), F32)
    for source in range(groups):
        start = pl.multiple_of(order_ref[source] * block_len, block_len)
        block = snaps_ref[source]
        raw += jnp.dot(block, basis_ref[pl.ds(start, block_len), :], preferred_element_type=F32)
        own += nt(block, block)
    out_ref[0:fold_rows] = fold_ref[...]
    at = fold_rows
    for part in range(rank // LANES):
        out_ref[at : at + snapcount] = raw[:, part * LANES : (part + 1) * LANES]
        at += snapcount
    out_ref[at:] = jnp.zeros((out_ref.shape[0] - at, LANES), F32)
    out_ref[at : at + snapcount, 0:snapcount] = own


def column(matrix, index):
    return matrix[:, index : index + 1]


def factor(gram, scale):
    count = gram.shape[0]
    row_id = lax.broadcasted_iota(jnp.int32, (count, count), 0)
    col_id = lax.broadcasted_iota(jnp.int32, (count, count), 1)
    eye = (row_id == col_id).astype(F32)
    both = jnp.concatenate([gram, eye], axis=1)
    rows = lax.broadcasted_iota(jnp.int32, both.shape, 0)
    for step in range(count - 1):
        factors = column(both, step)
        ratio = factors / factors[step : step + 1]
        both -= jnp.where(rows > step, ratio * both[step : step + 1], 0.0)
    pivots = jnp.sum(both[:, 0:count] * eye, axis=1, keepdims=True)
    weak = jnp.sum(jnp.where(pivots >= GUARD * scale, 0.0, 1.0))
    both = both / jnp.sqrt(pivots)
    return jnp.where(row_id <= col_id, both[:, 0:count], 0.0), both[:, count:], weak


def finish_kernel(
    cell_total,
    order_ref,
    side_ref,
    mine_ref,
    other_ref,
    snaps_ref,
    basis_ref,
    modes_ref,
    coeffs_ref,
    upper_ref,
    weak_ref,
    sums_ref,
    resid_ref,
):
    groups, snapcount, block_len = snaps_ref.shape
    rank = basis_ref.shape[1]
    half, quarter = rank // 2, rank // 4
    share = mine_ref.shape[0]
    first = side_ref[0] == 0
    sums_ref[0:share] = jnp.where(first, mine_ref[...], other_ref[...])
    sums_ref[share:] = jnp.where(first, other_ref[...], mine_ref[...])
    fold_rows = 3 * quarter + half
    parts = rank // LANES
    raw = jnp.concatenate(
        [sums_ref[fold_rows + k * snapcount : fold_rows + (k + 1) * snapcount] for k in range(parts)],
        axis=1,
    )
    at = fold_rows + parts * snapcount
    own = sums_ref[at : at + snapcount, 0:snapcount]
    coeffs = raw / cell_total
    coeffs_ref[...] = coeffs
    narrow = coeffs.astype(jnp.bfloat16)
    rounded = narrow.astype(F32)

    for source in range(groups):
        start = pl.multiple_of(order_ref[source] * block_len, block_len)
        fitted = nt(narrow, basis_ref[pl.ds(start, block_len), :])
        resid_ref[source] = snaps_ref[source].astype(F32) - fitted

    upper = lane_at_least((quarter, half), quarter)
    middle = sums_ref[quarter : 2 * quarter]
    left = jnp.concatenate([sums_ref[0:quarter], jnp.where(upper, middle, 0.0)], axis=0)
    right = jnp.concatenate(
        [
            sums_ref[3 * quarter : fold_rows],
            jnp.where(upper, 0.0, middle),
            sums_ref[2 * quarter : 3 * quarter],
        ],
        axis=0,
    )
    spread = jnp.concatenate(
        [
            jnp.dot(rounded[:, 0:half], left, precision=HIGH, preferred_element_type=F32),
            jnp.dot(rounded, right, precision=HIGH, preferred_element_type=F32),
        ],
        axis=1,
    )
    cross = nt(raw, rounded, HIGH)
    quad = nt(spread, rounded, HIGH)
    gram = (own - (cross + cross.T) + 0.5 * (quad + quad.T)) / cell_total
    size = own + 2.0 * jnp.abs(cross) + jnp.abs(quad)
    eye = lax.broadcasted_iota(jnp.int32, size.shape, 0) == lax.broadcasted_iota(
        jnp.int32, size.shape, 1
    )
    scale = jnp.sum(jnp.where(eye, size, 0.0), axis=1, keepdims=True) / cell_total
    upper_factor, inverse, weak = factor(gram, scale)
    upper_ref[...] = upper_factor
    weak_ref[0] = weak

    for source in range(groups):
        start = pl.multiple_of(order_ref[source] * block_len, block_len)
        modes = column(inverse, 0) * resid_ref[source, 0:1, :]
        for row in range(1, snapcount):
            modes += column(inverse, row) * resid_ref[source, row : row + 1, :]
        modes_ref[:, pl.ds(start, block_len)] = modes.astype(jnp.bfloat16)


def exchange(value, total, masks):
    def partner(index):
        return index ^ masks[bin(index).count("1") % 2]

    return lax.ppermute(value, AXES, [(index, partner(index)) for index in range(total)])


def all_sum(value, total):
    value = value + exchange(value, total, (1, 1))
    for bit in range(1, total.bit_length() - 1):
        mask = (1 << bit) | 1
        value = value + exchange(value, total, (mask, mask))
    return value


def local(snaps_box, box_order, basis):
    snapcount = snaps_box.shape[0]
    local_cells, rank = basis.shape
    groups = lax.axis_size("sub")
    total = lax.axis_size("rows") * groups
    block_len = local_cells // groups
    cell_total = local_cells * total
    position = lax.axis_index("sub")
    order_row = lax.dynamic_index_in_dim(box_order[0], position, 0, keepdims=False)
    device = lax.axis_index("rows") * groups + position
    side = lax.population_count(device) % 2

    blocks = snaps_box.reshape(snapcount, groups, block_len).transpose(1, 0, 2)
    received = lax.all_to_all(blocks, "sub", split_axis=0, concat_axis=0, tiled=True)

    half, quarter = rank // 2, rank // 4
    fold_rows = 3 * quarter + half
    fold = pl.pallas_call(
        gram_kernel,
        out_shape=jax.ShapeDtypeStruct((fold_rows, half), F32),
        in_specs=[VMEM],
        out_specs=VMEM,
        compiler_params=pltpu.CompilerParams(vmem_limit_bytes=24 * MB),
        cost_estimate=pl.CostEstimate(
            flops=2 * local_cells * rank * rank,
            bytes_accessed=2 * local_cells * rank,
            transcendentals=0,
        ),
    )(basis)
    used = fold_rows + (rank // LANES + 1) * snapcount
    share = -(-used // 16) * 8
    packed = pl.pallas_call(
        project_kernel,
        out_shape=jax.ShapeDtypeStruct((2 * share, LANES), F32),
        in_specs=[SMEM, VMEM, VMEM, VMEM],
        out_specs=VMEM,
        compiler_params=pltpu.CompilerParams(vmem_limit_bytes=24 * MB),
    )(order_row, received, basis, fold)

    packed = packed + exchange(packed, total, (1, 1))
    mine = lax.dynamic_slice_in_dim(packed, side * share, share, 0)
    masks = [(1 << bit) | 1 for bit in range(1, total.bit_length() - 1)]
    swapped = list(masks)
    for index in range(0, len(masks) - 1, 2):
        swapped[index], swapped[index + 1] = masks[index + 1], masks[index]
    for pair in zip(masks, swapped):
        mine = mine + exchange(mine, total, pair)
    other = exchange(mine, total, (1, 1))

    modes, coeffs, r_factor, weak = pl.pallas_call(
        lambda *refs: finish_kernel(cell_total, *refs),
        out_shape=(
            jax.ShapeDtypeStruct((snapcount, local_cells), jnp.bfloat16),
            jax.ShapeDtypeStruct((snapcount, rank), F32),
            jax.ShapeDtypeStruct((snapcount, snapcount), F32),
            jax.ShapeDtypeStruct((1,), F32),
        ),
        in_specs=[SMEM, SMEM, VMEM, VMEM, VMEM, VMEM],
        out_specs=(VMEM, VMEM, VMEM, SMEM),
        scratch_shapes=[
            pltpu.VMEM((2 * share, LANES), F32),
            pltpu.VMEM((groups, snapcount, block_len), F32),
        ],
        compiler_params=pltpu.CompilerParams(vmem_limit_bytes=24 * MB),
    )(order_row, side.reshape(1), mine, other, received, basis)

    def direct(_):
        ordered = jnp.argsort(order_row)
        snapshots = jnp.take(received, ordered, axis=0).transpose(1, 0, 2)
        snapshots = snapshots.reshape(snapcount, local_cells).astype(F32)
        residual = snapshots - nt(coeffs.astype(jnp.bfloat16), basis)
        wgram = all_sum(jnp.dot(residual, residual.T, precision=HIGH) / cell_total, total)
        lower = jnp.linalg.cholesky(wgram)
        solved = jax.scipy.linalg.solve_triangular(lower, residual, lower=True)
        return solved.astype(jnp.bfloat16), lower.T

    modes, r_factor = lax.cond(weak[0] > 0.0, direct, lambda ready: ready, (modes, r_factor))
    return modes, coeffs, r_factor


def solution(mesh):
    return jax.shard_map(
        local,
        mesh=mesh,
        in_specs=(P(None, AXES), P("rows", None, None), P(AXES, None)),
        out_specs=(P(None, AXES), P(), P()),
        check_vma=False,
    )
```

time: 103 us -> 40.5 us (0.39)
  blocking collectives: 81 us -> 0 us
  Pallas kernels: 0 us -> 11.5 us
  waiting for transfers between devices: 4.59 us -> 13.5 us
  starting transfers between devices: 4.25 us -> 13.1 us
  matrix products: 8.17 us -> 0 us
  other arithmetic: 2.68 us -> 0.06 us
    psum x2 -> x0, blocking collectives: 81 us -> none  [the longest x1 41 us: local(): wgram = lax.psum(local_gram, ('rows', 'sub'))]
    ppermute x0 -> x6, waiting for transfers between devices: none -> 12.4 us  [exchange(): lax.ppermute(value, AXES, [(index, partner(index)) for index in range(tot...]
    pallas_call x0 -> x3, Pallas kernels: none -> 11.5 us  [the longest x1 5 us: local(): pl.pallas_call(lambda *refs: finish_kernel(cell_total, *refs), out_shape=...]
    ppermute x0 -> x6, starting transfers between devices: none -> 8.85 us  [exchange(): lax.ppermute(value, AXES, [(index, partner(index)) for index in range(tot...]
    dot_general x4 -> x0, matrix products: 7.09 us -> none  [the longest x1 3.38 us: local(): lax.dot_general(rounded, basis, (((1,), (1,)), ((), ())), preferred_eleme...]
    all_to_all x1, waiting for transfers between devices: 4.59 us -> 1.1 us  [local(): lax.all_to_all(blocks, 'sub', split_axis=0, concat_axis=0, tiled=True)]
    another operation x4 -> x0, other arithmetic: 2.02 us -> none  [the longest x3 1.39 us: local(): lower_tri = jnp.linalg.cholesky(wgram)]
    another operation x1 -> x0, matrix products: 1.09 us -> none  [local(): modes = jax.scipy.linalg.solve_triangular(lower_tri, residual, lower=True)]
  transfers between devices with their start and end apart: 1 -> 7, of which waited for: 1 -> 7; matrix products, arithmetic and copies ran while one was open for 0% -> 0% of each run, Pallas kernels for 0% -> 9%
where the time goes in v1:
time: 40.5 us; the launch traced here: 40.1 us
  waiting for transfers between devices  13.5 us (33%)
  starting transfers between devices  13.1 us (32%)
  Pallas kernels  11.5 us (28%)
  between operations  1.36 us (3%)
  local copies, waits for them, and re-layouts  0.66 us (2%)
    ppermute x6, waiting for transfers between devices, exchange(): lax.ppermute(value, AXES, [(index, partner(index)) for index in range(tot...  12.4 us
    ppermute x6, starting transfers between devices, exchange(): lax.ppermute(value, AXES, [(index, partner(index)) for index in range(tot...  8.85 us
    pallas_call x1, Pallas kernels, local(): pl.pallas_call(lambda *refs: finish_kernel(cell_total, *refs), out_shape=...  5 us
    all_to_all x1, starting transfers between devices, local(): lax.all_to_all(blocks, 'sub', split_axis=0, concat_axis=0, tiled=True)  4.25 us
    pallas_call x1, Pallas kernels, local(): pl.pallas_call(gram_kernel, out_shape=jax.ShapeDtypeStruct((fold_rows, ha...  3.49 us
    pallas_call x1, Pallas kernels, local(): pl.pallas_call(project_kernel, out_shape=jax.ShapeDtypeStruct((2 * share,...  2.97 us
    all_to_all x1, waiting for transfers between devices, local(): lax.all_to_all(blocks, 'sub', split_axis=0, concat_axis=0, tiled=True)  1.1 us
  transfers between devices with their start and end apart: 7, of which 7 were waited for; matrix products, arithmetic and copies ran while one was open for 0% of the time, Pallas kernels for 9%

profile of v1, /device:TPU:0, one launch (start us, length us, event | category | flops | bytes accessed | tf_op | source)
XLA Modules:
  0.0 40.1 jit_solution(6399631276989697115)
XLA Ops:
  0.6 0.0 copy-start
  0.6 4.2 %all-to-all-start = ((bf16[4,8,2048]{2,1,0:T(8,128)(2,1)}), bf16[4,8,2048]{2,1,0:T(8,128)(2,1)S(1)}, u32[]{:S(2)}, u32[]{:S(2)}) async-start(bf16[4,8,2048]{2,1,0:T(8,128)(2,1)} %bitcast.27), calls=%async_computation | async-start | bytes 262144 | tf_op jit(solution)/shard_map/all_to_all | solution.py:190
  4.9 0.0 copy-done
  4.9 3.5 %shard_map.58.fold_ref = f32[320,128]{1,0:T(8,128)S(1)} custom-call(bf16[8192,256]{1,0:T(8,128)(2,1)} %refs_5_.1), custom_call_target="tpu_custom_call" | custom-call | flops 1073741824 | bytes 4194304 | tf_op jit(solution)/shard_map/pallas_call | solution.py:194
  8.4 1.1 %all-to-all-done.snaps_ref.refs_4_ = bf16[4,8,2048]{2,1,0:T(8,128)(2,1)S(1)} async-done(((bf16[4,8,2048]{2,1,0:T(8,128)(2,1)}), bf16[4,8,2048]{2,1,0:T(8,128)(2,1)S(1)}, u32[]{:S(2)}, u32[]{:S(2)}) %all-to-all-start) | async-done | bytes 131104 | tf_op jit(solution)/shard_map/all_to_all | solution.py:190
  9.5 3.0 %shard_map.59 = f32[352,128]{1,0:T(8,128)S(1)} custom-call(s32[4]{0:T(128)S(1)} %fusion.4.order_ref.refs_0_, bf16[4,8,2048]{2,1,0:T(8,128)(2,1)S(1)} %all-to-all-done.snaps_ref.refs_4_, bf16[8192,256]{1,0:T(8,128)(2,1)} %refs_5_.1, f32[320,128]{1,0:T(8,128)S(1)} %shard_map.58.fold_ref), custom_call_target="tpu_custom_call" | custom-call | tf_op jit(solution)/shard_map/pallas_call | solution.py:208
  12.5 0.0 collective-permute-start.5
  12.5 1.4 %collective-permute-done.5 = f32[352,128]{1,0:T(8,128)S(1)} collective-permute-done((f32[352,128]{1,0:T(8,128)S(1)}, f32[352,128]{1,0:T(8,128)S(1)}, u32[]{:S(2)}, u32[]{:S(2)}) %collective-permute-start.5) | collective-permute-done | bytes 180256 | tf_op jit(solution)/shard_map/ppermute | solution.py:166
  13.9 0.8 %collective-permute-start.6 = (f32[176,128]{1,0:T(8,128)S(1)}, f32[176,128]{1,0:T(8,128)S(1)}, u32[]{:S(2)}, u32[]{:S(2)}) collective-permute-start(f32[176,128]{1,0:T(8,128)S(1)} %dynamic-slice_add_fusion), channel_id=1, source_target_pairs={{0,3},{1,4},{2,7},{3,0},{4,1},{5,6},{6,5},{7,2},{8,13},{9,10},{10,... | collective-permute-start | bytes 270344 | tf_op jit(solution)/shard_map/ppermute | solution.py:166
  14.7 3.2 %collective-permute-done.6 = f32[176,128]{1,0:T(8,128)S(1)} collective-permute-done((f32[176,128]{1,0:T(8,128)S(1)}, f32[176,128]{1,0:T(8,128)S(1)}, u32[]{:S(2)}, u32[]{:S(2)}) %collective-permute-start.6) | collective-permute-done | bytes 90144 | tf_op jit(solution)/shard_map/ppermute | solution.py:166
  18.0 1.9 %collective-permute-start.7 = (f32[176,128]{1,0:T(8,128)S(1)}, f32[176,128]{1,0:T(8,128)S(1)}, u32[]{:S(2)}, u32[]{:S(2)}) collective-permute-start(f32[176,128]{1,0:T(8,128)S(1)} %add.65), channel_id=1, source_target_pairs={{0,5},{1,2},{2,1},{3,6},{4,7},{5,0},{6,3},{7,4},{8,11},{9,12},{10,... | collective-permute-start | bytes 270344 | tf_op jit(solution)/shard_map/ppermute | solution.py:166
  19.8 2.2 %collective-permute-done.7 = f32[176,128]{1,0:T(8,128)S(1)} collective-permute-done((f32[176,128]{1,0:T(8,128)S(1)}, f32[176,128]{1,0:T(8,128)S(1)}, u32[]{:S(2)}, u32[]{:S(2)}) %collective-permute-start.7) | collective-permute-done | bytes 90144 | tf_op jit(solution)/shard_map/ppermute | solution.py:166
  22.1 1.9 %collective-permute-start.8 = (f32[176,128]{1,0:T(8,128)S(1)}, f32[176,128]{1,0:T(8,128)S(1)}, u32[]{:S(2)}, u32[]{:S(2)}) collective-permute-start(f32[176,128]{1,0:T(8,128)S(1)} %add.66), channel_id=1, source_target_pairs={{0,9},{1,16},{2,19},{3,10},{4,21},{5,12},{6,15},{7,22},{8,25},{9,0... | collective-permute-start | bytes 270344 | tf_op jit(solution)/shard_map/ppermute | solution.py:166
  23.9 2.3 %collective-permute-done.8 = f32[176,128]{1,0:T(8,128)S(1)} collective-permute-done((f32[176,128]{1,0:T(8,128)S(1)}, f32[176,128]{1,0:T(8,128)S(1)}, u32[]{:S(2)}, u32[]{:S(2)}) %collective-permute-start.8) | collective-permute-done | bytes 90144 | tf_op jit(solution)/shard_map/ppermute | solution.py:166
  26.3 3.5 %collective-permute-start.9 = (f32[176,128]{1,0:T(8,128)S(1)}, f32[176,128]{1,0:T(8,128)S(1)}, u32[]{:S(2)}, u32[]{:S(2)}) collective-permute-start(f32[176,128]{1,0:T(8,128)S(1)} %add.67), channel_id=1, source_target_pairs={{0,17},{1,8},{2,11},{3,18},{4,13},{5,20},{6,23},{7,14},{8,1},{9,24... | collective-permute-start | bytes 270344 | tf_op jit(solution)/shard_map/ppermute | solution.py:166
  29.8 2.3 %collective-permute-done.9 = f32[176,128]{1,0:T(8,128)S(1)} collective-permute-done((f32[176,128]{1,0:T(8,128)S(1)}, f32[176,128]{1,0:T(8,128)S(1)}, u32[]{:S(2)}, u32[]{:S(2)}) %collective-permute-start.9) | collective-permute-done | bytes 90144 | tf_op jit(solution)/shard_map/ppermute | solution.py:166
  32.1 0.8 %collective-permute-start.10 = (f32[176,128]{1,0:T(8,128)S(1)}, f32[176,128]{1,0:T(8,128)S(1)}, u32[]{:S(2)}, u32[]{:S(2)}) collective-permute-start(f32[176,128]{1,0:T(8,128)S(1)} %add.68.refs_2_), channel_id=1, source_target_pairs={{0,1},{1,0},{2,3},{3,2},{4,5},{5,4},{6,7},{7,6},{8,9},{9,8},{10,11... | collective-permute-start | bytes 270344 | tf_op jit(solution)/shard_map/ppermute | solution.py:166
  32.9 0.9 %collective-permute-done.10.refs_3_ = f32[176,128]{1,0:T(8,128)S(1)} collective-permute-done((f32[176,128]{1,0:T(8,128)S(1)}, f32[176,128]{1,0:T(8,128)S(1)}, u32[]{:S(2)}, u32[]{:S(2)}) %collective-permute-start.10) | collective-permute-done | bytes 90144 | tf_op jit(solution)/shard_map/ppermute | solution.py:166
  33.8 5.0 %shard_map.60 = (bf16[8,8192]{1,0:T(8,128)(2,1)S(1)}, f32[8,256]{1,0:T(8,128)}, f32[8,8]{1,0:T(8,128)S(1)}, f32[1]{0:T(128)}) custom-call(s32[4]{0:T(128)S(1)} %fusion.4.order_ref.refs_0_, s32[1]{0:T(128)} %bitcast.7.refs_1_, f32[176,128]{1,0:T(8,128)S(1)} %add.68.refs_2_, f32[176,128]{1,0:T(8,128)S(1)} %collective-permute-done.10.refs_3_, ...), custom_call_target="tpu_custom_call" | custom-call | tf_op jit(solution)/shard_map/pallas_call | solution.py:226
  39.5 0.0 copy-start.1
  39.5 0.0 copy-start.2
  39.5 0.6 %copy-done.1 = bf16[8,8192]{1,0:T(8,128)(2,1)} copy-done((bf16[8,8192]{1,0:T(8,128)(2,1)}, bf16[8,8192]{1,0:T(8,128)(2,1)S(1)}, u32[]{:S(2)}) %copy-start.1) | copy-done | bytes 131096
  40.1 0.0 copy-done.2
  (7 shorter events, 0.1 us)
Async XLA Ops:
  0.6 4.3 %copy-start = (s32[1,4,4]{2,1,0:T(4,128)S(1)}, s32[1,4,4]{2,1,0:T(4,128)}, u32[]{:S(2)}) copy-start(s32[1,4,4]{2,1,0:T(4,128)} %param.6) | copy-start | bytes 196
  0.6 8.8 %all-to-all-start = ((bf16[4,8,2048]{2,1,0:T(8,128)(2,1)}), bf16[4,8,2048]{2,1,0:T(8,128)(2,1)S(1)}, u32[]{:S(2)}, u32[]{:S(2)}) async-start(bf16[4,8,2048]{2,1,0:T(8,128)(2,1)} %bitcast.27), calls=%async_computation | async-start | bytes 262144 | tf_op jit(solution)/shard_map/all_to_all | solution.py:190
  12.5 1.5 %collective-permute-start.5 = (f32[352,128]{1,0:T(8,128)S(1)}, f32[352,128]{1,0:T(8,128)S(1)}, u32[]{:S(2)}, u32[]{:S(2)}) collective-permute-start(f32[352,128]{1,0:T(8,128)S(1)} %shard_map.59), channel_id=1, source_target_pairs={{0,1},{1,0},{2,3},{3,2},{4,5},{5,4},{6,7},{7,6},{8,9},{9,8},{10,11... | collective-permute-start | bytes 540680 | tf_op jit(solution)/shard_map/ppermute | solution.py:166
  13.9 4.0 %collective-permute-start.6 = (f32[176,128]{1,0:T(8,128)S(1)}, f32[176,128]{1,0:T(8,128)S(1)}, u32[]{:S(2)}, u32[]{:S(2)}) collective-permute-start(f32[176,128]{1,0:T(8,128)S(1)} %dynamic-slice_add_fusion), channel_id=1, source_target_pairs={{0,3},{1,4},{2,7},{3,0},{4,1},{5,6},{6,5},{7,2},{8,13},{9,10},{10,... | collective-permute-start | bytes 270344 | tf_op jit(solution)/shard_map/ppermute | solution.py:166
  18.0 4.1 %collective-permute-start.7 = (f32[176,128]{1,0:T(8,128)S(1)}, f32[176,128]{1,0:T(8,128)S(1)}, u32[]{:S(2)}, u32[]{:S(2)}) collective-permute-start(f32[176,128]{1,0:T(8,128)S(1)} %add.65), channel_id=1, source_target_pairs={{0,5},{1,2},{2,1},{3,6},{4,7},{5,0},{6,3},{7,4},{8,11},{9,12},{10,... | collective-permute-start | bytes 270344 | tf_op jit(solution)/shard_map/ppermute | solution.py:166
  22.1 4.2 %collective-permute-start.8 = (f32[176,128]{1,0:T(8,128)S(1)}, f32[176,128]{1,0:T(8,128)S(1)}, u32[]{:S(2)}, u32[]{:S(2)}) collective-permute-start(f32[176,128]{1,0:T(8,128)S(1)} %add.66), channel_id=1, source_target_pairs={{0,9},{1,16},{2,19},{3,10},{4,21},{5,12},{6,15},{7,22},{8,25},{9,0... | collective-permute-start | bytes 270344 | tf_op jit(solution)/shard_map/ppermute | solution.py:166
  26.3 5.8 %collective-permute-start.9 = (f32[176,128]{1,0:T(8,128)S(1)}, f32[176,128]{1,0:T(8,128)S(1)}, u32[]{:S(2)}, u32[]{:S(2)}) collective-permute-start(f32[176,128]{1,0:T(8,128)S(1)} %add.67), channel_id=1, source_target_pairs={{0,17},{1,8},{2,11},{3,18},{4,13},{5,20},{6,23},{7,14},{8,1},{9,24... | collective-permute-start | bytes 270344 | tf_op jit(solution)/shard_map/ppermute | solution.py:166
  32.1 1.7 %collective-permute-start.10 = (f32[176,128]{1,0:T(8,128)S(1)}, f32[176,128]{1,0:T(8,128)S(1)}, u32[]{:S(2)}, u32[]{:S(2)}) collective-permute-start(f32[176,128]{1,0:T(8,128)S(1)} %add.68.refs_2_), channel_id=1, source_target_pairs={{0,1},{1,0},{2,3},{3,2},{4,5},{5,4},{6,7},{7,6},{8,9},{9,8},{10,11... | collective-permute-start | bytes 270344 | tf_op jit(solution)/shard_map/ppermute | solution.py:166
  39.5 0.7 %copy-start.1 = (bf16[8,8192]{1,0:T(8,128)(2,1)}, bf16[8,8192]{1,0:T(8,128)(2,1)S(1)}, u32[]{:S(2)}) copy-start(bf16[8,8192]{1,0:T(8,128)(2,1)S(1)} %get-tuple-element.34) | copy-start | bytes 393220
  39.5 0.6 %copy-start.2 = (f32[8,8]{1,0:T(8,128)}, f32[8,8]{1,0:T(8,128)S(1)}, u32[]{:S(2)}) copy-start(f32[8,8]{1,0:T(8,128)S(1)} %get-tuple-element.37) | copy-start | bytes 772

commit v2 on v1

v2 whole, which is shorter than its diff:
```python
import jax
import jax.numpy as jnp
from jax import lax
from jax.experimental import pallas as pl
from jax.experimental.pallas import tpu as pltpu
from jax.sharding import PartitionSpec as P

AXES = ("rows", "sub")
HIGH = lax.Precision.HIGHEST
LANES = 128
GUARD = 1.0 / 64.0
CHUNKS = 8
LIMIT = 16 * 1048576
VMEM = pl.BlockSpec(memory_space=pltpu.VMEM)
SMEM = pl.BlockSpec(memory_space=pltpu.SMEM)
F32 = jnp.float32


def nt(a, b, precision=None):
    return lax.dot_general(
        a, b, (((1,), (1,)), ((), ())), precision=precision, preferred_element_type=F32
    )


def lane_at_least(shape, bound):
    return lax.broadcasted_iota(jnp.int32, shape, len(shape) - 1) >= bound


def gram_kernel(basis_ref, fold_ref, near_ref, sems):
    cells, rank = near_ref.shape
    half, quarter = rank // 2, rank // 4
    chunk = cells // CHUNKS

    def load(index):
        part = pl.ds(index * chunk, chunk)
        return pltpu.make_async_copy(basis_ref.at[part], near_ref.at[part], sems.at[index])

    for index in range(CHUNKS):
        load(index).start()
    total = jnp.zeros((rank, rank), F32)
    for index in range(CHUNKS):
        load(index).wait()
        part = near_ref[index * chunk : (index + 1) * chunk]
        total += lax.dot_general(
            part, part, (((0,), (0,)), ((), ())), preferred_element_type=F32
        )
    upper = lane_at_least((quarter, half), quarter)
    fold_ref[0:quarter] = jnp.where(upper, 2.0, 1.0) * total[0:quarter, 0:half]
    fold_ref[quarter : 2 * quarter] = jnp.where(
        upper, total[quarter:half, 0:half], total[half : 3 * quarter, half:]
    )
    fold_ref[2 * quarter : 3 * quarter] = jnp.where(upper, 1.0, 2.0) * total[3 * quarter :, half:]
    fold_ref[3 * quarter : 3 * quarter + half] = 2.0 * total[0:half, half:]


def device_index():
    return lax.axis_index("rows") * lax.axis_size("sub") + lax.axis_index("sub")


def parity(device, total):
    value = device
    for bit in range(1, (total - 1).bit_length()):
        value = value ^ (device >> bit)
    return value & 1


def fetch_kernel(far_ref, near_ref, sem):
    copy = pltpu.make_async_copy(far_ref, near_ref, sem)
    copy.start()
    copy.wait()


def pack_kernel(kept, own_ref, peer_ref, keep_ref, send_ref):
    position = lax.axis_index("sub")
    half = len(kept) // 2
    for source, ref in enumerate((own_ref, peer_ref)):
        for index, offset in enumerate(kept):
            out = keep_ref if index < half else send_ref
            out[source, index % half] = ref[position ^ offset]


def starts(order_ref, sources, block_len):
    position = lax.axis_index("sub")
    return [
        pl.multiple_of(order_ref[0, position, position ^ source] * block_len, block_len)
        for source in sources
    ]


def project_kernel(sources, total, order_ref, keep_ref, far_ref, basis_ref, fold_ref, mine_ref, send_ref, out_ref):
    near, snapcount, block_len = keep_ref.shape
    share = mine_ref.shape[0]
    fold_rows = fold_ref.shape[0]
    rank = basis_ref.shape[1]
    raw = jnp.zeros((snapcount, rank), F32)
    own = jnp.zeros((snapcount, snapcount), F32)
    for index, start in enumerate(starts(order_ref, sources, block_len)):
        block = keep_ref[index] if index < near else far_ref[index - near]
        raw += jnp.dot(block, basis_ref[pl.ds(start, block_len), :], preferred_element_type=F32)
        own += nt(block, block)
    out_ref[0:fold_rows] = fold_ref[...]
    at = fold_rows
    for part in range(rank // LANES):
        out_ref[at : at + snapcount] = raw[:, part * LANES : (part + 1) * LANES]
        at += snapcount
    out_ref[at:] = jnp.zeros((out_ref.shape[0] - at, LANES), F32)
    out_ref[at : at + snapcount, 0:snapcount] = own
    side = parity(device_index(), total)
    mine_ref[...] = out_ref[pl.ds(pl.multiple_of(side * share, 8), share)]
    send_ref[...] = out_ref[pl.ds(pl.multiple_of((1 - side) * share, 8), share)]


def column(matrix, index):
    return matrix[:, index : index + 1]


def factor(gram, scale):
    count = gram.shape[0]
    row_id = lax.broadcasted_iota(jnp.int32, (count, count), 0)
    col_id = lax.broadcasted_iota(jnp.int32, (count, count), 1)
    eye = (row_id == col_id).astype(F32)
    both = jnp.concatenate([gram, eye], axis=1)
    rows = lax.broadcasted_iota(jnp.int32, both.shape, 0)
    for step in range(count - 1):
        factors = column(both, step)
        ratio = factors / factors[step : step + 1]
        both -= jnp.where(rows > step, ratio * both[step : step + 1], 0.0)
    pivots = jnp.sum(both[:, 0:count] * eye, axis=1, keepdims=True)
    weak = jnp.sum(jnp.where(pivots >= GUARD * scale, 0.0, 1.0))
    both = both / jnp.sqrt(pivots)
    return jnp.where(row_id <= col_id, both[:, 0:count], 0.0), both[:, count:], weak


def finish_kernel(
    sources,
    total,
    order_ref,
    mine_ref,
    other_ref,
    keep_ref,
    far_ref,
    basis_ref,
    modes_ref,
    coeffs_ref,
    upper_ref,
    weak_ref,
    sums_ref,
    resid_ref,
):
    near, snapcount, block_len = keep_ref.shape
    cells, rank = basis_ref.shape
    cell_total = cells * total
    half, quarter = rank // 2, rank // 4
    share = mine_ref.shape[0]
    first = parity(device_index(), total) == 0
    places = starts(order_ref, sources, block_len)
    sums_ref[0:share] = jnp.where(first, mine_ref[...], other_ref[...])
    sums_ref[share:] = jnp.where(first, other_ref[...], mine_ref[...])
    fold_rows = 3 * quarter + half
    parts = rank // LANES
    raw = jnp.concatenate(
        [sums_ref[fold_rows + k * snapcount : fold_rows + (k + 1) * snapcount] for k in range(parts)],
        axis=1,
    )
    at = fold_rows + parts * snapcount
    own = sums_ref[at : at + snapcount, 0:snapcount]
    coeffs = raw / cell_total
    coeffs_ref[...] = coeffs
    narrow = coeffs.astype(jnp.bfloat16)
    rounded = narrow.astype(F32)

    for index, start in enumerate(places):
        fitted = nt(narrow, basis_ref[pl.ds(start, block_len), :])
        block = keep_ref[index] if index < near else far_ref[index - near]
        resid_ref[index] = block.astype(F32) - fitted

    upper = lane_at_least((quarter, half), quarter)
    middle = sums_ref[quarter : 2 * quarter]
    left = jnp.concatenate([sums_ref[0:quarter], jnp.where(upper, middle, 0.0)], axis=0)
    right = jnp.concatenate(
        [
            sums_ref[3 * quarter : fold_rows],
            jnp.where(upper, 0.0, middle),
            sums_ref[2 * quarter : 3 * quarter],
        ],
        axis=0,
    )
    spread = jnp.concatenate(
        [
            jnp.dot(rounded[:, 0:half], left, precision=HIGH, preferred_element_type=F32),
            jnp.dot(rounded, right, precision=HIGH, preferred_element_type=F32),
        ],
        axis=1,
    )
    cross = nt(raw, rounded, HIGH)
    quad = nt(spread, rounded, HIGH)
    gram = (own - (cross + cross.T) + 0.5 * (quad + quad.T)) / cell_total
    size = own + 2.0 * jnp.abs(cross) + jnp.abs(quad)
    eye = lax.broadcasted_iota(jnp.int32, size.shape, 0) == lax.broadcasted_iota(
        jnp.int32, size.shape, 1
    )
    scale = jnp.sum(jnp.where(eye, size, 0.0), axis=1, keepdims=True) / cell_total
    upper_factor, inverse, weak = factor(gram, scale)
    upper_ref[...] = upper_factor
    weak_ref[0] = weak

    for index, start in enumerate(places):
        modes = column(inverse, 0) * resid_ref[index, 0:1, :]
        for row in range(1, snapcount):
            modes += column(inverse, row) * resid_ref[index, row : row + 1, :]
        modes_ref[:, pl.ds(start, block_len)] = modes.astype(jnp.bfloat16)


def exchange(value, total, masks):
    def partner(index):
        return index ^ masks[bin(index).count("1") % 2]

    return lax.ppermute(value, AXES, [(index, partner(index)) for index in range(total)])


def flips(count):
    return [(1 << bit) | 1 for bit in range(1, count.bit_length() - 1)]


def all_sum(value, total):
    for mask in [1] + flips(total):
        value = value + exchange(value, total, (mask, mask))
    return value


def kernel_call(kernel, outputs, in_specs, out_specs, scratch=(), **options):
    return pl.pallas_call(
        kernel,
        out_shape=outputs,
        in_specs=in_specs,
        out_specs=out_specs,
        scratch_shapes=scratch,
        compiler_params=pltpu.CompilerParams(vmem_limit_bytes=LIMIT),
        **options,
    )


def spread_boxes(boxes, groups, total):
    like = jax.ShapeDtypeStruct
    peer = exchange(boxes, total, (1, 1))
    own = kernel_call(
        fetch_kernel,
        like(boxes.shape, boxes.dtype),
        [pl.BlockSpec(memory_space=pltpu.HBM)],
        VMEM,
        [pltpu.SemaphoreType.DMA(())],
        cost_estimate=pl.CostEstimate(
            flops=0, bytes_accessed=2 * boxes.size, transcendentals=0
        ),
    )(boxes)
    kept, sources = [0], [0, 1]
    for mask in flips(groups):
        kept = kept + [offset ^ mask for offset in kept]
    half = len(kept) // 2
    shape = like((2, half) + boxes.shape[1:], boxes.dtype)
    keep, send = kernel_call(
        lambda *refs: pack_kernel(kept, *refs), (shape, shape), [VMEM, VMEM], (VMEM, VMEM)
    )(own, peer)
    for mask in reversed(flips(groups)):
        far = exchange(send, total, (mask, mask))
        sources = sources + [source ^ mask for source in sources]
        if half == 1:
            return keep[:, 0], far[:, 0], sources
        both = jnp.concatenate([keep, far], axis=0)
        half //= 2
        keep, send = both[:, :half], both[:, half:]


def local(snaps_box, box_order, basis):
    like = jax.ShapeDtypeStruct
    snapcount = snaps_box.shape[0]
    local_cells, rank = basis.shape
    groups = lax.axis_size("sub")
    total = lax.axis_size("rows") * groups
    block_len = local_cells // groups
    cell_total = local_cells * total

    boxes = snaps_box.reshape(snapcount, groups, block_len).transpose(1, 0, 2)
    keep, far, sources = spread_boxes(boxes, groups, total)

    half, quarter = rank // 2, rank // 4
    fold_rows = 3 * quarter + half
    fold, near = kernel_call(
        gram_kernel,
        (like((fold_rows, half), F32), like(basis.shape, basis.dtype)),
        [pl.BlockSpec(memory_space=pltpu.HBM)],
        (VMEM, VMEM),
        [pltpu.SemaphoreType.DMA((CHUNKS,))],
        cost_estimate=pl.CostEstimate(
            flops=2 * local_cells * rank * rank,
            bytes_accessed=2 * local_cells * rank,
            transcendentals=0,
        ),
    )(basis)
    used = fold_rows + (rank // LANES + 1) * snapcount
    share = -(-used // 16) * 8
    part = like((share, LANES), F32)
    mine, send = kernel_call(
        lambda *refs: project_kernel(sources, total, *refs),
        (part, part),
        [SMEM, VMEM, VMEM, VMEM, VMEM],
        (VMEM, VMEM),
        [pltpu.VMEM((2 * share, LANES), F32)],
    )(box_order, keep, far, near, fold)

    mine = mine + exchange(send, total, (1, 1))
    masks = flips(total)
    swapped = list(masks)
    for index in range(0, len(masks) - 1, 2):
        swapped[index], swapped[index + 1] = masks[index + 1], masks[index]
    for pair in zip(masks, swapped):
        mine = mine + exchange(mine, total, pair)
    other = exchange(mine, total, (1, 1))

    modes, coeffs, r_factor, weak = kernel_call(
        lambda *refs: finish_kernel(sources, total, *refs),
        (
            like((snapcount, local_cells), jnp.bfloat16),
            like((snapcount, rank), F32),
            like((snapcount, snapcount), F32),
            like((1,), F32),
        ),
        [SMEM, VMEM, VMEM, VMEM, VMEM, VMEM],
        (VMEM, VMEM, VMEM, SMEM),
        [
            pltpu.VMEM((2 * share, LANES), F32),
            pltpu.VMEM((groups, snapcount, block_len), F32),
        ],
    )(box_order, mine, other, keep, far, near)

    def direct(_):
        position = lax.axis_index("sub")
        order_row = lax.dynamic_index_in_dim(box_order[0], position, 0, keepdims=False)
        held = position ^ jnp.array(sources, dtype=jnp.int32)
        ordered = jnp.argsort(order_row[held])
        snapshots = jnp.take(jnp.concatenate([keep, far]), ordered, axis=0).transpose(1, 0, 2)
        snapshots = snapshots.reshape(snapcount, local_cells).astype(F32)
        residual = snapshots - nt(coeffs.astype(jnp.bfloat16), basis)
        wgram = all_sum(jnp.dot(residual, residual.T, precision=HIGH) / cell_total, total)
        lower = jnp.linalg.cholesky(wgram)
        solved = jax.scipy.linalg.solve_triangular(lower, residual, lower=True)
        return solved.astype(jnp.bfloat16), lower.T

    modes, r_factor = lax.cond(weak[0] > 0.0, direct, lambda ready: ready, (modes, r_factor))
    return modes, coeffs, r_factor


def solution(mesh):
    return jax.shard_map(
        local,
        mesh=mesh,
        in_specs=(P(None, AXES), P("rows", None, None), P(AXES, None)),
        out_specs=(P(None, AXES), P(), P()),
        check_vma=False,
    )
```

time: 40.5 us -> 36.1 us (0.89)
  Pallas kernels: 11.5 us -> 8.95 us
  starting transfers between devices: 13.1 us -> 10.8 us
  local copies, waits for them, and re-layouts: 0.66 us -> 1.55 us
    all_to_all x1 -> x0, starting transfers between devices: 4.25 us -> none  [local(): lax.all_to_all(blocks, 'sub', split_axis=0, concat_axis=0, tiled=True)]
    pallas_call x3 -> x5, Pallas kernels: 11.5 us -> 8.95 us  [the longest x1 4.05 us: local(): kernel_call(gram_kernel, (like((fold_rows, half), F32), like(basis.shape,...]
    ppermute x6 -> x8, starting transfers between devices: 8.85 us -> 10.8 us  [exchange(): lax.ppermute(value, AXES, [(index, partner(index)) for index in range(tot...]
    all_to_all x1 -> x0, waiting for transfers between devices: 1.1 us -> none  [local(): lax.all_to_all(blocks, 'sub', split_axis=0, concat_axis=0, tiled=True)]
    unnamed x6 -> x8, local copies, waits for them, and re-layouts: 0.65 us -> 1.55 us
    ppermute x6 -> x8, waiting for transfers between devices: 12.4 us -> 13.2 us  [exchange(): lax.ppermute(value, AXES, [(index, partner(index)) for index in range(tot...]
  transfers between devices with their start and end apart: 7 -> 8, of which waited for: 7 -> 7; matrix products, arithmetic and copies ran while one was open for 0% -> 0% of each run, Pallas kernels for 9% -> 12%
where the time goes in v2:
time: 36.1 us; the launch traced here: 35.9 us
  waiting for transfers between devices  13.2 us (37%)
  starting transfers between devices  10.8 us (30%)
  Pallas kernels  8.95 us (25%)
  local copies, waits for them, and re-layouts  1.55 us (4%)
  between operations  1.36 us (4%)
    ppermute x8, waiting for transfers between devices, exchange(): lax.ppermute(value, AXES, [(index, partner(index)) for index in range(tot...  13.2 us
    ppermute x8, starting transfers between devices, exchange(): lax.ppermute(value, AXES, [(index, partner(index)) for index in range(tot...  10.8 us
    pallas_call x1, Pallas kernels, local(): kernel_call(gram_kernel, (like((fold_rows, half), F32), like(basis.shape,...  4.05 us
    pallas_call x1, Pallas kernels, local(): kernel_call(lambda *refs: finish_kernel(sources, total, *refs), (like((sn...  3.38 us
    unnamed x8, local copies, waits for them, and re-layouts  1.55 us
    pallas_call x1, Pallas kernels, local(): kernel_call(lambda *refs: project_kernel(sources, total, *refs), (part, p...  1.36 us
  transfers between devices with their start and end apart: 8, of which 7 were waited for; matrix products, arithmetic and copies ran while one was open for 0% of the time, Pallas kernels for 12%

profile of v2, /device:TPU:0, one launch (start us, length us, event | category | flops | bytes accessed | tf_op | source)
XLA Modules:
  0.0 35.9 jit_solution(10727629315851659885)
XLA Ops:
  0.6 0.6 %collective-permute-start.5 = (bf16[4,8,2048]{2,1,0:T(8,128)(2,1)}, bf16[4,8,2048]{2,1,0:T(8,128)(2,1)S(1)}, u32[]{:S(2)}, u32[]{:S(2)}) collective-permute-start(bf16[4,8,2048]{2,1,0:T(8,128)(2,1)} %bitcast.28), channel_id=1, source_target_pairs={{0,1},{1,0},{2,3},{3,2},{4,5},{5,4},{6,7},{7,6},{8,9},{9,8},{10,11... | collective-permute-start | bytes 393224 | tf_op jit(solution)/shard_map/ppermute | solution.py:218
  1.2 0.0 copy-start
  1.2 0.9 %copy-done = bf16[8,8192]{1,0:T(8,128)(2,1)S(1)} copy-done((bf16[8,8192]{1,0:T(8,128)(2,1)S(1)}, bf16[8,8192]{1,0:T(8,128)(2,1)}, u32[]{:S(2)}) %copy-start) | copy-done | bytes 131096
  2.1 0.0 copy-start.1
  2.1 0.2 shard_map.68.refs_0_
  2.3 0.1 collective-permute-done.5.refs_1_
  2.4 2.7 %collective-permute-start.6 = (bf16[2,1,8,2048]{3,2,0,1:T(8,128)(2,1)S(1)}, bf16[2,1,8,2048]{3,2,0,1:T(8,128)(2,1)S(1)}, u32[]{:S(2)}, u32[]{:S(2)}) collective-permute-start(bf16[2,1,8,2048]{3,2,0,1:T(8,128)(2,1)S(1)} %bitcast.30), channel_id=1, source_target_pairs={{0,3},{1,2},{2,1},{3,0},{4,7},{5,6},{6,5},{7,4},{8,11},{9,10},{10,... | collective-permute-start | bytes 196616 | tf_op jit(solution)/shard_map/ppermute | solution.py:218
  5.1 4.0 %shard_map.70 = (f32[320,128]{1,0:T(8,128)S(1)}, bf16[8192,256]{1,0:T(8,128)(2,1)S(1)}) custom-call(bf16[8192,256]{1,0:T(8,128)(2,1)} %basis_ref.1), custom_call_target="tpu_custom_call" | custom-call | flops 1073741824 | bytes 4194304 | tf_op jit(solution)/shard_map/pallas_call | solution.py:288
  9.1 0.0 collective-permute-done.6
  9.1 0.0 copy-done.1
  9.1 1.4 %shard_map.71 = (f32[176,128]{1,0:T(8,128)S(1)}, f32[176,128]{1,0:T(8,128)S(1)}) custom-call(s32[1,4,4]{2,1,0:T(4,128)S(1)} %copy-done.1, bf16[2,8,2048]{2,1,0:T(8,128)(2,1)S(1)} %bitcast.32, bf16[2,8,2048]{2,1,0:T(8,128)(2,1)S(1)} %bitcast.35, bf16[8192,256]{1,0:T(8,128)(2,1)S(1)} %get-tuple-element.40.refs_3_.refs_5_, f32[320,128]{1,0:T(8,128)S(1)} %get-tuple-element.41.refs_4_), custom_call_target="tpu_custom_call" | custom-call | tf_op jit(solution)/shard_map/pallas_call | solution.py:303
  10.5 0.4 %collective-permute-start.7 = (f32[176,128]{1,0:T(8,128)S(1)}, f32[176,128]{1,0:T(8,128)S(1)}, u32[]{:S(2)}, u32[]{:S(2)}) collective-permute-start(f32[176,128]{1,0:T(8,128)S(1)} %get-tuple-element.43), channel_id=1, source_target_pairs={{0,1},{1,0},{2,3},{3,2},{4,5},{5,4},{6,7},{7,6},{8,9},{9,8},{10,11... | collective-permute-start | bytes 270344 | tf_op jit(solution)/shard_map/ppermute | solution.py:218
  10.9 0.9 %collective-permute-done.7 = f32[176,128]{1,0:T(8,128)S(1)} collective-permute-done((f32[176,128]{1,0:T(8,128)S(1)}, f32[176,128]{1,0:T(8,128)S(1)}, u32[]{:S(2)}, u32[]{:S(2)}) %collective-permute-start.7) | collective-permute-done | bytes 90144 | tf_op jit(solution)/shard_map/ppermute | solution.py:218
  11.8 0.1 collective-permute-start.8
  11.9 3.9 %collective-permute-done.8 = f32[176,128]{1,0:T(8,128)S(1)} collective-permute-done((f32[176,128]{1,0:T(8,128)S(1)}, f32[176,128]{1,0:T(8,128)S(1)}, u32[]{:S(2)}, u32[]{:S(2)}) %collective-permute-start.8) | collective-permute-done | bytes 90144 | tf_op jit(solution)/shard_map/ppermute | solution.py:218
  15.9 1.5 %collective-permute-start.9 = (f32[176,128]{1,0:T(8,128)S(1)}, f32[176,128]{1,0:T(8,128)S(1)}, u32[]{:S(2)}, u32[]{:S(2)}) collective-permute-start(f32[176,128]{1,0:T(8,128)S(1)} %add.54), channel_id=1, source_target_pairs={{0,5},{1,2},{2,1},{3,6},{4,7},{5,0},{6,3},{7,4},{8,11},{9,12},{10,... | collective-permute-start | bytes 270344 | tf_op jit(solution)/shard_map/ppermute | solution.py:218
  17.4 2.5 %collective-permute-done.9 = f32[176,128]{1,0:T(8,128)S(1)} collective-permute-done((f32[176,128]{1,0:T(8,128)S(1)}, f32[176,128]{1,0:T(8,128)S(1)}, u32[]{:S(2)}, u32[]{:S(2)}) %collective-permute-start.9) | collective-permute-done | bytes 90144 | tf_op jit(solution)/shard_map/ppermute | solution.py:218
  19.9 1.6 %collective-permute-start.10 = (f32[176,128]{1,0:T(8,128)S(1)}, f32[176,128]{1,0:T(8,128)S(1)}, u32[]{:S(2)}, u32[]{:S(2)}) collective-permute-start(f32[176,128]{1,0:T(8,128)S(1)} %add.55), channel_id=1, source_target_pairs={{0,9},{1,16},{2,19},{3,10},{4,21},{5,12},{6,15},{7,22},{8,25},{9,0... | collective-permute-start | bytes 270344 | tf_op jit(solution)/shard_map/ppermute | solution.py:218
  21.5 2.5 %collective-permute-done.10 = f32[176,128]{1,0:T(8,128)S(1)} collective-permute-done((f32[176,128]{1,0:T(8,128)S(1)}, f32[176,128]{1,0:T(8,128)S(1)}, u32[]{:S(2)}, u32[]{:S(2)}) %collective-permute-start.10) | collective-permute-done | bytes 90144 | tf_op jit(solution)/shard_map/ppermute | solution.py:218
  24.1 3.1 %collective-permute-start.11 = (f32[176,128]{1,0:T(8,128)S(1)}, f32[176,128]{1,0:T(8,128)S(1)}, u32[]{:S(2)}, u32[]{:S(2)}) collective-permute-start(f32[176,128]{1,0:T(8,128)S(1)} %add.56), channel_id=1, source_target_pairs={{0,17},{1,8},{2,11},{3,18},{4,13},{5,20},{6,23},{7,14},{8,1},{9,24... | collective-permute-start | bytes 270344 | tf_op jit(solution)/shard_map/ppermute | solution.py:218
  27.2 2.2 %collective-permute-done.11 = f32[176,128]{1,0:T(8,128)S(1)} collective-permute-done((f32[176,128]{1,0:T(8,128)S(1)}, f32[176,128]{1,0:T(8,128)S(1)}, u32[]{:S(2)}, u32[]{:S(2)}) %collective-permute-start.11) | collective-permute-done | bytes 90144 | tf_op jit(solution)/shard_map/ppermute | solution.py:218
  29.4 0.9 %collective-permute-start.12 = (f32[176,128]{1,0:T(8,128)S(1)}, f32[176,128]{1,0:T(8,128)S(1)}, u32[]{:S(2)}, u32[]{:S(2)}) collective-permute-start(f32[176,128]{1,0:T(8,128)S(1)} %add.57.refs_1_), channel_id=1, source_target_pairs={{0,1},{1,0},{2,3},{3,2},{4,5},{5,4},{6,7},{7,6},{8,9},{9,8},{10,11... | collective-permute-start | bytes 270344 | tf_op jit(solution)/shard_map/ppermute | solution.py:218
  30.3 0.9 %collective-permute-done.12.refs_2_ = f32[176,128]{1,0:T(8,128)S(1)} collective-permute-done((f32[176,128]{1,0:T(8,128)S(1)}, f32[176,128]{1,0:T(8,128)S(1)}, u32[]{:S(2)}, u32[]{:S(2)}) %collective-permute-start.12) | collective-permute-done | bytes 90144 | tf_op jit(solution)/shard_map/ppermute | solution.py:218
  31.2 3.4 %shard_map.72 = (bf16[8,8192]{1,0:T(8,128)(2,1)S(1)}, f32[8,256]{1,0:T(8,128)}, f32[8,8]{1,0:T(8,128)S(1)}, f32[1]{0:T(128)}) custom-call(s32[1,4,4]{2,1,0:T(4,128)S(1)} %copy-done.1, f32[176,128]{1,0:T(8,128)S(1)} %add.57.refs_1_, f32[176,128]{1,0:T(8,128)S(1)} %collective-permute-done.12.refs_2_, bf16[2,8,2048]{2,1,0:T(8,128)(2,1)S(1)} %bitcast.33, ...), custom_call_target="tpu_custom_call" | custom-call | tf_op jit(solution)/shard_map/pallas_call | solution.py:320
  35.2 0.0 copy-start.2
  35.3 0.0 copy-start.3
  35.3 0.6 %copy-done.2 = bf16[8,8192]{1,0:T(8,128)(2,1)} copy-done((bf16[8,8192]{1,0:T(8,128)(2,1)}, bf16[8,8192]{1,0:T(8,128)(2,1)S(1)}, u32[]{:S(2)}) %copy-start.2) | copy-done | bytes 131096
  35.9 0.0 copy-done.3
  (7 shorter events, 0.1 us)
Async XLA Ops:
  0.6 1.8 %collective-permute-start.5 = (bf16[4,8,2048]{2,1,0:T(8,128)(2,1)}, bf16[4,8,2048]{2,1,0:T(8,128)(2,1)S(1)}, u32[]{:S(2)}, u32[]{:S(2)}) collective-permute-start(bf16[4,8,2048]{2,1,0:T(8,128)(2,1)} %bitcast.28), channel_id=1, source_target_pairs={{0,1},{1,0},{2,3},{3,2},{4,5},{5,4},{6,7},{7,6},{8,9},{9,8},{10,11... | collective-permute-start | bytes 393224 | tf_op jit(solution)/shard_map/ppermute | solution.py:218
  1.2 0.9 %copy-start = (bf16[8,8192]{1,0:T(8,128)(2,1)S(1)}, bf16[8,8192]{1,0:T(8,128)(2,1)}, u32[]{:S(2)}) copy-start(bf16[8,8192]{1,0:T(8,128)(2,1)} %param.6) | copy-start | bytes 393220
  2.1 7.0 %copy-start.1 = (s32[1,4,4]{2,1,0:T(4,128)S(1)}, s32[1,4,4]{2,1,0:T(4,128)}, u32[]{:S(2)}) copy-start(s32[1,4,4]{2,1,0:T(4,128)} %refs_0_.3) | copy-start | bytes 196
  2.4 6.7 %collective-permute-start.6 = (bf16[2,1,8,2048]{3,2,0,1:T(8,128)(2,1)S(1)}, bf16[2,1,8,2048]{3,2,0,1:T(8,128)(2,1)S(1)}, u32[]{:S(2)}, u32[]{:S(2)}) collective-permute-start(bf16[2,1,8,2048]{3,2,0,1:T(8,128)(2,1)S(1)} %bitcast.30), channel_id=1, source_target_pairs={{0,3},{1,2},{2,1},{3,0},{4,7},{5,6},{6,5},{7,4},{8,11},{9,10},{10,... | collective-permute-start | bytes 196616 | tf_op jit(solution)/shard_map/ppermute | solution.py:218
  10.5 1.3 %collective-permute-start.7 = (f32[176,128]{1,0:T(8,128)S(1)}, f32[176,128]{1,0:T(8,128)S(1)}, u32[]{:S(2)}, u32[]{:S(2)}) collective-permute-start(f32[176,128]{1,0:T(8,128)S(1)} %get-tuple-element.43), channel_id=1, source_target_pairs={{0,1},{1,0},{2,3},{3,2},{4,5},{5,4},{6,7},{7,6},{8,9},{9,8},{10,11... | collective-permute-start | bytes 270344 | tf_op jit(solution)/shard_map/ppermute | solution.py:218
  11.8 4.0 %collective-permute-start.8 = (f32[176,128]{1,0:T(8,128)S(1)}, f32[176,128]{1,0:T(8,128)S(1)}, u32[]{:S(2)}, u32[]{:S(2)}) collective-permute-start(f32[176,128]{1,0:T(8,128)S(1)} %add.53), channel_id=1, source_target_pairs={{0,3},{1,4},{2,7},{3,0},{4,1},{5,6},{6,5},{7,2},{8,13},{9,10},{10,... | collective-permute-start | bytes 270344 | tf_op jit(solution)/shard_map/ppermute | solution.py:218
  15.9 4.0 %collective-permute-start.9 = (f32[176,128]{1,0:T(8,128)S(1)}, f32[176,128]{1,0:T(8,128)S(1)}, u32[]{:S(2)}, u32[]{:S(2)}) collective-permute-start(f32[176,128]{1,0:T(8,128)S(1)} %add.54), channel_id=1, source_target_pairs={{0,5},{1,2},{2,1},{3,6},{4,7},{5,0},{6,3},{7,4},{8,11},{9,12},{10,... | collective-permute-start | bytes 270344 | tf_op jit(solution)/shard_map/ppermute | solution.py:218
  19.9 4.1 %collective-permute-start.10 = (f32[176,128]{1,0:T(8,128)S(1)}, f32[176,128]{1,0:T(8,128)S(1)}, u32[]{:S(2)}, u32[]{:S(2)}) collective-permute-start(f32[176,128]{1,0:T(8,128)S(1)} %add.55), channel_id=1, source_target_pairs={{0,9},{1,16},{2,19},{3,10},{4,21},{5,12},{6,15},{7,22},{8,25},{9,0... | collective-permute-start | bytes 270344 | tf_op jit(solution)/shard_map/ppermute | solution.py:218
  24.1 5.3 %collective-permute-start.11 = (f32[176,128]{1,0:T(8,128)S(1)}, f32[176,128]{1,0:T(8,128)S(1)}, u32[]{:S(2)}, u32[]{:S(2)}) collective-permute-start(f32[176,128]{1,0:T(8,128)S(1)} %add.56), channel_id=1, source_target_pairs={{0,17},{1,8},{2,11},{3,18},{4,13},{5,20},{6,23},{7,14},{8,1},{9,24... | collective-permute-start | bytes 270344 | tf_op jit(solution)/shard_map/ppermute | solution.py:218
  29.4 1.8 %collective-permute-start.12 = (f32[176,128]{1,0:T(8,128)S(1)}, f32[176,128]{1,0:T(8,128)S(1)}, u32[]{:S(2)}, u32[]{:S(2)}) collective-permute-start(f32[176,128]{1,0:T(8,128)S(1)} %add.57.refs_1_), channel_id=1, source_target_pairs={{0,1},{1,0},{2,3},{3,2},{4,5},{5,4},{6,7},{7,6},{8,9},{9,8},{10,11... | collective-permute-start | bytes 270344 | tf_op jit(solution)/shard_map/ppermute | solution.py:218
  35.2 0.7 %copy-start.2 = (bf16[8,8192]{1,0:T(8,128)(2,1)}, bf16[8,8192]{1,0:T(8,128)(2,1)S(1)}, u32[]{:S(2)}) copy-start(bf16[8,8192]{1,0:T(8,128)(2,1)S(1)} %get-tuple-element.59) | copy-start | bytes 393220
  35.3 0.6 %copy-start.3 = (f32[8,8]{1,0:T(8,128)}, f32[8,8]{1,0:T(8,128)S(1)}, u32[]{:S(2)}) copy-start(f32[8,8]{1,0:T(8,128)S(1)} %get-tuple-element.62) | copy-start | bytes 772

commit v3 on v2

--- a/solution.py
+++ b/solution.py
@@ -9,7 +9,10 @@
 HIGH = lax.Precision.HIGHEST
 LANES = 128
 GUARD = 1.0 / 64.0
-CHUNKS = 8
+STRETCHES = 8
+HBM = pl.BlockSpec(memory_space=pltpu.HBM)
+ANY = pl.BlockSpec(memory_space=pl.ANY)
+DMA = pltpu.SemaphoreType.DMA
 LIMIT = 16 * 1048576
 VMEM = pl.BlockSpec(memory_space=pltpu.VMEM)
 SMEM = pl.BlockSpec(memory_space=pltpu.SMEM)
@@ -26,24 +29,37 @@
     return lax.broadcasted_iota(jnp.int32, shape, len(shape) - 1) >= bound
 
 
-def gram_kernel(basis_ref, fold_ref, near_ref, sems):
-    cells, rank = near_ref.shape
+def gram_of(part):
+    return lax.dot_general(part, part, (((0,), (0,)), ((), ())), preferred_element_type=F32)
+
+
+def copies(source_ref, target_ref, bounds, sems):
+    made = []
+    for index, (low, high) in enumerate(bounds):
+        part = pl.ds(low, high - low)
+        made.append(
+            pltpu.make_async_copy(source_ref.at[part], target_ref.at[part], sems.at[index])
+        )
+        made[index].start()
+    return made
+
+
+def open_kernel(done, boxes_ref, basis_ref, own_ref, near_ref, total_ref, box_sem, sems):
+    box = pltpu.make_async_copy(boxes_ref, own_ref, box_sem)
+    box.start()
+    (rows,) = copies(basis_ref, near_ref, [(0, done)], sems)
+    rows.wait()
+    total_ref[...] = gram_of(near_ref[0:done])
+    box.wait()
+
+
+def gram_kernel(bounds, basis_ref, held_ref, total_ref, fold_ref, near_ref, sems):
+    rank = near_ref.shape[1]
     half, quarter = rank // 2, rank // 4
-    chunk = cells // CHUNKS
-
-    def load(index):
-        part = pl.ds(index * chunk, chunk)
-        return pltpu.make_async_copy(basis_ref.at[part], near_ref.at[part], sems.at[index])
-
-    for index in range(CHUNKS):
-        load(index).start()
-    total = jnp.zeros((rank, rank), F32)
-    for index in range(CHUNKS):
-        load(index).wait()
-        part = near_ref[index * chunk : (index + 1) * chunk]
-        total += lax.dot_general(
-            part, part, (((0,), (0,)), ((), ())), preferred_element_type=F32
-        )
+    total = total_ref[...]
+    for copy, (low, high) in zip(copies(basis_ref, near_ref, bounds, sems), bounds):
+        copy.wait()
+        total += gram_of(near_ref[low:high])
     upper = lane_at_least((quarter, half), quarter)
     fold_ref[0:quarter] = jnp.where(upper, 2.0, 1.0) * total[0:quarter, 0:half]
     fold_ref[quarter : 2 * quarter] = jnp.where(
@@ -62,12 +78,6 @@
     for bit in range(1, (total - 1).bit_length()):
         value = value ^ (device >> bit)
     return value & 1
-
-
-def fetch_kernel(far_ref, near_ref, sem):
-    copy = pltpu.make_async_copy(far_ref, near_ref, sem)
-    copy.start()
-    copy.wait()
 
 
 def pack_kernel(kept, own_ref, peer_ref, keep_ref, send_ref):
@@ -79,26 +89,41 @@
             out[source, index % half] = ref[position ^ offset]
 
 
-def starts(order_ref, sources, block_len):
-    position = lax.axis_index("sub")
-    return [
-        pl.multiple_of(order_ref[0, position, position ^ source] * block_len, block_len)
-        for source in sources
-    ]
-
-
-def project_kernel(sources, total, order_ref, keep_ref, far_ref, basis_ref, fold_ref, mine_ref, send_ref, out_ref):
+def project_kernel(
+    sources,
+    total,
+    order_hbm,
+    keep_ref,
+    far_ref,
+    basis_ref,
+    fold_ref,
+    mine_ref,
+    send_ref,
+    placed_ref,
+    out_ref,
+    order_ref,
+    sem,
+):
+    table = pltpu.make_async_copy(order_hbm, order_ref, sem)
+    table.start()
     near, snapcount, block_len = keep_ref.shape
     share = mine_ref.shape[0]
     fold_rows = fold_ref.shape[0]
     rank = basis_ref.shape[1]
+    blocks = [keep_ref[index] for index in range(near)]
+    blocks += [far_ref[index] for index in range(len(sources) - near)]
+    out_ref[0:fold_rows] = fold_ref[...]
+    own = nt(blocks[0], blocks[0])
+    for block in blocks[1:]:
+        own += nt(block, block)
+    table.wait()
+    position = lax.axis_index("sub")
     raw = jnp.zeros((snapcount, rank), F32)
-    own = jnp.zeros((snapcount, snapcount), F32)
-    for index, start in enumerate(starts(order_ref, sources, block_len)):
-        block = keep_ref[index] if index < near else far_ref[index - near]
+    for source, block in zip(sources, blocks):
+        start = order_ref[0, position, position ^ source] * block_len
+        start = pl.multiple_of(start, block_len)
         raw += jnp.dot(block, basis_ref[pl.ds(start, block_len), :], preferred_element_type=F32)
-        own += nt(block, block)
-    out_ref[0:fold_rows] = fold_ref[...]
+        placed_ref[:, pl.ds(start, block_len)] = block
     at = fold_rows
     for part in range(rank // LANES):
         out_ref[at : at + snapcount] = raw[:, part * LANES : (part + 1) * LANES]
@@ -132,28 +157,28 @@
 
 
 def finish_kernel(
-    sources,
     total,
-    order_ref,
     mine_ref,
     other_ref,
-    keep_ref,
-    far_ref,
+    placed_ref,
     basis_ref,
-    modes_ref,
-    coeffs_ref,
+    modes_hbm,
+    coeffs_hbm,
     upper_ref,
     weak_ref,
     sums_ref,
+    coeffs_ref,
     resid_ref,
+    modes_ref,
+    coeffs_sem,
+    modes_sems,
 ):
-    near, snapcount, block_len = keep_ref.shape
-    cells, rank = basis_ref.shape
+    snapcount, cells = placed_ref.shape
+    rank = basis_ref.shape[1]
     cell_total = cells * total
     half, quarter = rank // 2, rank // 4
     share = mine_ref.shape[0]
     first = parity(device_index(), total) == 0
-    places = starts(order_ref, sources, block_len)
     sums_ref[0:share] = jnp.where(first, mine_ref[...], other_ref[...])
     sums_ref[share:] = jnp.where(first, other_ref[...], mine_ref[...])
     fold_rows = 3 * quarter + half
@@ -166,13 +191,10 @@
     own = sums_ref[at : at + snapcount, 0:snapcount]
     coeffs = raw / cell_total
     coeffs_ref[...] = coeffs
+    coeffs_copy = pltpu.make_async_copy(coeffs_ref, coeffs_hbm, coeffs_sem)
+    coeffs_copy.start()
     narrow = coeffs.astype(jnp.bfloat16)
     rounded = narrow.astype(F32)
-
-    for index, start in enumerate(places):
-        fitted = nt(narrow, basis_ref[pl.ds(start, block_len), :])
-        block = keep_ref[index] if index < near else far_ref[index - near]
-        resid_ref[index] = block.astype(F32) - fitted
 
     upper = lane_at_least((quarter, half), quarter)
     middle = sums_ref[quarter : 2 * quarter]
@@ -203,12 +225,29 @@
     upper_factor, inverse, weak = factor(gram, scale)
     upper_ref[...] = upper_factor
     weak_ref[0] = weak
-
-    for index, start in enumerate(places):
-        modes = column(inverse, 0) * resid_ref[index, 0:1, :]
-        for row in range(1, snapcount):
-            modes += column(inverse, row) * resid_ref[index, row : row + 1, :]
-        modes_ref[:, pl.ds(start, block_len)] = modes.astype(jnp.bfloat16)
+    columns = [jnp.broadcast_to(column(inverse, row), (snapcount, LANES)) for row in range(snapcount)]
+
+    stretch = cells // STRETCHES
+    outgoing = []
+    for index in range(STRETCHES):
+        low = index * stretch
+        fitted = nt(narrow, basis_ref[low : low + stretch])
+        resid_ref[:, low : low + stretch] = (
+            placed_ref[:, low : low + stretch].astype(F32) - fitted
+        )
+        for lane in range(low, low + stretch, LANES):
+            modes = columns[0] * resid_ref[0:1, lane : lane + LANES]
+            for row in range(1, snapcount):
+                modes += columns[row] * resid_ref[row : row + 1, lane : lane + LANES]
+            modes_ref[:, lane : lane + LANES] = modes.astype(jnp.bfloat16)
+        part = pl.ds(low, stretch)
+        outgoing.append(
+            pltpu.make_async_copy(modes_ref.at[:, part], modes_hbm.at[:, part], modes_sems.at[index])
+        )
+        outgoing[index].start()
+    coeffs_copy.wait()
+    for copy in outgoing:
+        copy.wait()
 
 
 def exchange(value, total, masks):
@@ -240,24 +279,13 @@
     )
 
 
-def spread_boxes(boxes, groups, total):
+def spread_boxes(own, peer, groups, total):
     like = jax.ShapeDtypeStruct
-    peer = exchange(boxes, total, (1, 1))
-    own = kernel_call(
-        fetch_kernel,
-        like(boxes.shape, boxes.dtype),
-        [pl.BlockSpec(memory_space=pltpu.HBM)],
-        VMEM,
-        [pltpu.SemaphoreType.DMA(())],
-        cost_estimate=pl.CostEstimate(
-            flops=0, bytes_accessed=2 * boxes.size, transcendentals=0
-        ),
-    )(boxes)
     kept, sources = [0], [0, 1]
     for mask in flips(groups):
         kept = kept + [offset ^ mask for offset in kept]
     half = len(kept) // 2
-    shape = like((2, half) + boxes.shape[1:], boxes.dtype)
+    shape = like((2, half) + own.shape[1:], own.dtype)
     keep, send = kernel_call(
         lambda *refs: pack_kernel(kept, *refs), (shape, shape), [VMEM, VMEM], (VMEM, VMEM)
     )(own, peer)
@@ -271,6 +299,12 @@
         keep, send = both[:, :half], both[:, half:]
 
 
+def gram_cost(rows, rank):
+    return pl.CostEstimate(
+        flops=2 * rows * rank * rank, bytes_accessed=2 * rows * rank, transcendentals=0
+    )
+
+
 def local(snaps_box, box_order, basis):
     like = jax.ShapeDtypeStruct
     snapcount = snaps_box.shape[0]
@@ -281,31 +315,45 @@
     cell_total = local_cells * total
 
     boxes = snaps_box.reshape(snapcount, groups, block_len).transpose(1, 0, 2)
-    keep, far, sources = spread_boxes(boxes, groups, total)
+    peer = exchange(boxes, total, (1, 1))
+    eighth = local_cells // 8
+    done = 2 * eighth
+    rest = [(done, 3 * eighth), (3 * eighth, 5 * eighth), (5 * eighth, local_cells)]
+    held = like(basis.shape, basis.dtype)
+    own, near, total_gram = kernel_call(
+        lambda *refs: open_kernel(done, *refs),
+        (like(boxes.shape, boxes.dtype), held, like((rank, rank), F32)),
+        [HBM, HBM],
+        (VMEM, VMEM, VMEM),
+        [DMA(()), DMA((1,))],
+        cost_estimate=gram_cost(done, rank),
+    )(boxes, basis)
+    keep, far, sources = spread_boxes(own, peer, groups, total)
 
     half, quarter = rank // 2, rank // 4
     fold_rows = 3 * quarter + half
     fold, near = kernel_call(
-        gram_kernel,
-        (like((fold_rows, half), F32), like(basis.shape, basis.dtype)),
-        [pl.BlockSpec(memory_space=pltpu.HBM)],
+        lambda *refs: gram_kernel(rest, *refs),
+        (like((fold_rows, half), F32), held),
+        [HBM, VMEM, VMEM],
         (VMEM, VMEM),
-        [pltpu.SemaphoreType.DMA((CHUNKS,))],
-        cost_estimate=pl.CostEstimate(
-            flops=2 * local_cells * rank * rank,
-            bytes_accessed=2 * local_cells * rank,
-            transcendentals=0,
-        ),
-    )(basis)
+        [DMA((len(rest),))],
+        input_output_aliases={1: 1},
+        cost_estimate=gram_cost(local_cells - done, rank),
+    )(basis, near, total_gram)
     used = fold_rows + (rank // LANES + 1) * snapcount
     share = -(-used // 16) * 8
     part = like((share, LANES), F32)
-    mine, send = kernel_call(
+    mine, send, placed = kernel_call(
         lambda *refs: project_kernel(sources, total, *refs),
-        (part, part),
-        [SMEM, VMEM, VMEM, VMEM, VMEM],
-        (VMEM, VMEM),
-        [pltpu.VMEM((2 * share, LANES), F32)],
+        (part, part, like((snapcount, local_cells), snaps_box.dtype)),
+        [ANY, VMEM, VMEM, VMEM, VMEM],
+        (VMEM, VMEM, VMEM),
+        [
+            pltpu.VMEM((2 * share, LANES), F32),
+            pltpu.SMEM(box_order.shape, box_order.dtype),
+            DMA(()),
+        ],
     )(box_order, keep, far, near, fold)
 
     mine = mine + exchange(send, total, (1, 1))
@@ -318,29 +366,27 @@
     other = exchange(mine, total, (1, 1))
 
     modes, coeffs, r_factor, weak = kernel_call(
-        lambda *refs: finish_kernel(sources, total, *refs),
+        lambda *refs: finish_kernel(total, *refs),
         (
             like((snapcount, local_cells), jnp.bfloat16),
             like((snapcount, rank), F32),
             like((snapcount, snapcount), F32),
             like((1,), F32),
         ),
-        [SMEM, VMEM, VMEM, VMEM, VMEM, VMEM],
-        (VMEM, VMEM, VMEM, SMEM),
+        [VMEM, VMEM, VMEM, VMEM],
+        (HBM, HBM, VMEM, SMEM),
         [
             pltpu.VMEM((2 * share, LANES), F32),
-            pltpu.VMEM((groups, snapcount, block_len), F32),
+            pltpu.VMEM((snapcount, rank), F32),
+            pltpu.VMEM((snapcount, local_cells), F32),
+            pltpu.VMEM((snapcount, local_cells), jnp.bfloat16),
+            DMA(()),
+            DMA((STRETCHES,)),
         ],
-    )(box_order, mine, other, keep, far, near)
+    )(mine, other, placed, near)
 
     def direct(_):
-        position = lax.axis_index("sub")
-        order_row = lax.dynamic_index_in_dim(box_order[0], position, 0, keepdims=False)
-        held = position ^ jnp.array(sources, dtype=jnp.int32)
-        ordered = jnp.argsort(order_row[held])
-        snapshots = jnp.take(jnp.concatenate([keep, far]), ordered, axis=0).transpose(1, 0, 2)
-        snapshots = snapshots.reshape(snapcount, local_cells).astype(F32)
-        residual = snapshots - nt(coeffs.astype(jnp.bfloat16), basis)
+        residual = placed.astype(F32) - nt(coeffs.astype(jnp.bfloat16), basis)
         wgram = all_sum(jnp.dot(residual, residual.T, precision=HIGH) / cell_total, total)
         lower = jnp.linalg.cholesky(wgram)
         solved = jax.scipy.linalg.solve_triangular(lower, residual, lower=True)

time: 36.1 us -> 36.5 us (1.011)
  waiting for transfers between devices: 13.2 us -> 12.5 us
  starting transfers between devices: 10.8 us -> 11.4 us
  Pallas kernels: 8.95 us -> 9.44 us
    ppermute x8, waiting for transfers between devices: 13.2 us -> 12.5 us  [exchange(): lax.ppermute(value, AXES, [(index, partner(index)) for index in range(tot...]
    ppermute x8, starting transfers between devices: 10.8 us -> 11.4 us  [exchange(): lax.ppermute(value, AXES, [(index, partner(index)) for index in range(tot...]
    pallas_call x3, Pallas kernels: 7.58 us -> 8.1 us  [the longest x1 3.81 us: local(): kernel_call(lambda *refs: finish_kernel(total, *refs), (like((snapcount,...]
    unnamed x8 -> x10, local copies, waits for them, and re-layouts: 1.55 us -> 1.56 us
where the time goes in v3:
time: 36.5 us; the launch traced here: 36.3 us
  waiting for transfers between devices  12.5 us (34%)
  starting transfers between devices  11.4 us (31%)
  Pallas kernels  9.44 us (26%)
  local copies, waits for them, and re-layouts  1.56 us (4%)
  between operations  1.37 us (4%)
    ppermute x8, waiting for transfers between devices, exchange(): lax.ppermute(value, AXES, [(index, partner(index)) for index in range(tot...  12.5 us
    ppermute x8, starting transfers between devices, exchange(): lax.ppermute(value, AXES, [(index, partner(index)) for index in range(tot...  11.4 us
    pallas_call x1, Pallas kernels, local(): kernel_call(lambda *refs: finish_kernel(total, *refs), (like((snapcount,...  3.81 us
    pallas_call x1, Pallas kernels, local(): kernel_call(lambda *refs: gram_kernel(rest, *refs), (like((fold_rows, hal...  2.27 us
    pallas_call x1, Pallas kernels, local(): kernel_call(lambda *refs: open_kernel(done, *refs), (like(boxes.shape, bo...  2.02 us
    unnamed x10, local copies, waits for them, and re-layouts  1.56 us
    pallas_call x1, Pallas kernels, local(): kernel_call(lambda *refs: project_kernel(sources, total, *refs), (part, p...  1.32 us
  transfers between devices with their start and end apart: 8, of which 7 were waited for; matrix products, arithmetic and copies ran while one was open for 0% of the time, Pallas kernels for 12%

profile of v3, /device:TPU:0, one launch (start us, length us, event | category | flops | bytes accessed | tf_op | source)
XLA Modules:
  0.0 36.3 jit_solution(4558891205838139718)
XLA Ops:
  0.6 0.6 %collective-permute-start.5 = (bf16[4,8,2048]{2,1,0:T(8,128)(2,1)}, bf16[4,8,2048]{2,1,0:T(8,128)(2,1)S(1)}, u32[]{:S(2)}, u32[]{:S(2)}) collective-permute-start(bf16[4,8,2048]{2,1,0:T(8,128)(2,1)} %bitcast.23), channel_id=1, source_target_pairs={{0,1},{1,0},{2,3},{3,2},{4,5},{5,4},{6,7},{7,6},{8,9},{9,8},{10,11... | collective-permute-start | bytes 393224 | tf_op jit(solution)/shard_map/ppermute | solution.py:257
  1.2 0.0 copy-start
  1.2 0.9 %copy-done = bf16[8,8192]{1,0:T(8,128)(2,1)S(1)} copy-done((bf16[8,8192]{1,0:T(8,128)(2,1)S(1)}, bf16[8,8192]{1,0:T(8,128)(2,1)}, u32[]{:S(2)}) %copy-start) | copy-done | bytes 131096
  2.1 0.0 copy-start.2
  2.1 2.0 %shard_map.58 = (bf16[4,8,2048]{2,1,0:T(8,128)(2,1)S(1)}, bf16[8192,256]{1,0:T(8,128)(2,1)S(1)}, f32[256,256]{1,0:T(8,128)S(1)}) custom-call(bf16[4,8,2048]{2,1,0:T(8,128)(2,1)S(1)} %bitcast.24, bf16[8192,256]{1,0:T(8,128)(2,1)} %refs_0_.2), custom_call_target="tpu_custom_call" | custom-call | flops 268435456 | bytes 1048576 | tf_op jit(solution)/shard_map/pallas_call | solution.py:323
  4.1 0.0 collective-permute-done.5.refs_1_
  4.2 2.7 %collective-permute-start.6 = (bf16[2,1,8,2048]{3,2,0,1:T(8,128)(2,1)S(1)}, bf16[2,1,8,2048]{3,2,0,1:T(8,128)(2,1)S(1)}, u32[]{:S(2)}, u32[]{:S(2)}) collective-permute-start(bf16[2,1,8,2048]{3,2,0,1:T(8,128)(2,1)S(1)} %bitcast.27), channel_id=1, source_target_pairs={{0,3},{1,2},{2,1},{3,0},{4,7},{5,6},{6,5},{7,4},{8,11},{9,10},{10,... | collective-permute-start | bytes 196616 | tf_op jit(solution)/shard_map/ppermute | solution.py:257
  6.8 0.0 copy-done.2
  6.8 0.0 copy-start.1
  6.8 2.3 %shard_map.60 = (f32[320,128]{1,0:T(8,128)S(1)}, bf16[8192,256]{1,0:T(8,128)(2,1)S(1)}) custom-call(bf16[8192,256]{1,0:T(8,128)(2,1)S(1)} %copy-done.2, bf16[8192,256]{1,0:T(8,128)(2,1)S(1)} %get-tuple-element.35.refs_1_, f32[256,256]{1,0:T(8,128)S(1)} %get-tuple-element.36.refs_2_), custom_call_target="tpu_custom_call", output_to_operand_aliasing={{1}: (1, {})} | custom-call | flops 805306368 | bytes 3145728 | tf_op jit(solution)/shard_map/pallas_call | solution.py:335
  9.1 0.2 collective-permute-done.6
  9.3 0.0 copy-done.1
  9.3 1.3 %shard_map.61 = (f32[176,128]{1,0:T(8,128)S(1)}, f32[176,128]{1,0:T(8,128)S(1)}, bf16[8,8192]{1,0:T(8,128)(2,1)S(1)}) custom-call(s32[1,4,4]{2,1,0:T(4,128)S(1)} %copy-done.1, bf16[2,8,2048]{2,1,0:T(8,128)(2,1)S(1)} %bitcast.25, bf16[2,8,2048]{2,1,0:T(8,128)(2,1)S(1)} %bitcast.26, bf16[8192,256]{1,0:T(8,128)(2,1)S(1)} %get-tuple-element.37.refs_3_, ...), custom_call_target="tpu_custom_call" | custom-call | tf_op jit(solution)/shard_map/pallas_call | solution.py:347
  10.6 0.2 collective-permute-start.7
  10.8 1.2 %collective-permute-done.7 = f32[176,128]{1,0:T(8,128)S(1)} collective-permute-done((f32[176,128]{1,0:T(8,128)S(1)}, f32[176,128]{1,0:T(8,128)S(1)}, u32[]{:S(2)}, u32[]{:S(2)}) %collective-permute-start.7) | collective-permute-done | bytes 90144 | tf_op jit(solution)/shard_map/ppermute | solution.py:257
  12.0 1.3 %collective-permute-start.8 = (f32[176,128]{1,0:T(8,128)S(1)}, f32[176,128]{1,0:T(8,128)S(1)}, u32[]{:S(2)}, u32[]{:S(2)}) collective-permute-start(f32[176,128]{1,0:T(8,128)S(1)} %add.42), channel_id=1, source_target_pairs={{0,3},{1,4},{2,7},{3,0},{4,1},{5,6},{6,5},{7,2},{8,13},{9,10},{10,... | collective-permute-start | bytes 270344 | tf_op jit(solution)/shard_map/ppermute | solution.py:257
  13.3 2.7 %collective-permute-done.8 = f32[176,128]{1,0:T(8,128)S(1)} collective-permute-done((f32[176,128]{1,0:T(8,128)S(1)}, f32[176,128]{1,0:T(8,128)S(1)}, u32[]{:S(2)}, u32[]{:S(2)}) %collective-permute-start.8) | collective-permute-done | bytes 90144 | tf_op jit(solution)/shard_map/ppermute | solution.py:257
  16.0 1.4 %collective-permute-start.9 = (f32[176,128]{1,0:T(8,128)S(1)}, f32[176,128]{1,0:T(8,128)S(1)}, u32[]{:S(2)}, u32[]{:S(2)}) collective-permute-start(f32[176,128]{1,0:T(8,128)S(1)} %add.43), channel_id=1, source_target_pairs={{0,5},{1,2},{2,1},{3,6},{4,7},{5,0},{6,3},{7,4},{8,11},{9,12},{10,... | collective-permute-start | bytes 270344 | tf_op jit(solution)/shard_map/ppermute | solution.py:257
  17.4 2.7 %collective-permute-done.9 = f32[176,128]{1,0:T(8,128)S(1)} collective-permute-done((f32[176,128]{1,0:T(8,128)S(1)}, f32[176,128]{1,0:T(8,128)S(1)}, u32[]{:S(2)}, u32[]{:S(2)}) %collective-permute-start.9) | collective-permute-done | bytes 90144 | tf_op jit(solution)/shard_map/ppermute | solution.py:257
  20.0 1.4 %collective-permute-start.10 = (f32[176,128]{1,0:T(8,128)S(1)}, f32[176,128]{1,0:T(8,128)S(1)}, u32[]{:S(2)}, u32[]{:S(2)}) collective-permute-start(f32[176,128]{1,0:T(8,128)S(1)} %add.44), channel_id=1, source_target_pairs={{0,9},{1,16},{2,19},{3,10},{4,21},{5,12},{6,15},{7,22},{8,25},{9,0... | collective-permute-start | bytes 270344 | tf_op jit(solution)/shard_map/ppermute | solution.py:257
  21.4 2.6 %collective-permute-done.10 = f32[176,128]{1,0:T(8,128)S(1)} collective-permute-done((f32[176,128]{1,0:T(8,128)S(1)}, f32[176,128]{1,0:T(8,128)S(1)}, u32[]{:S(2)}, u32[]{:S(2)}) %collective-permute-start.10) | collective-permute-done | bytes 90144 | tf_op jit(solution)/shard_map/ppermute | solution.py:257
  24.1 3.1 %collective-permute-start.11 = (f32[176,128]{1,0:T(8,128)S(1)}, f32[176,128]{1,0:T(8,128)S(1)}, u32[]{:S(2)}, u32[]{:S(2)}) collective-permute-start(f32[176,128]{1,0:T(8,128)S(1)} %add.45), channel_id=1, source_target_pairs={{0,17},{1,8},{2,11},{3,18},{4,13},{5,20},{6,23},{7,14},{8,1},{9,24... | collective-permute-start | bytes 270344 | tf_op jit(solution)/shard_map/ppermute | solution.py:257
  27.1 2.2 %collective-permute-done.11 = f32[176,128]{1,0:T(8,128)S(1)} collective-permute-done((f32[176,128]{1,0:T(8,128)S(1)}, f32[176,128]{1,0:T(8,128)S(1)}, u32[]{:S(2)}, u32[]{:S(2)}) %collective-permute-start.11) | collective-permute-done | bytes 90144 | tf_op jit(solution)/shard_map/ppermute | solution.py:257
  29.4 0.9 %collective-permute-start.12 = (f32[176,128]{1,0:T(8,128)S(1)}, f32[176,128]{1,0:T(8,128)S(1)}, u32[]{:S(2)}, u32[]{:S(2)}) collective-permute-start(f32[176,128]{1,0:T(8,128)S(1)} %add.46.refs_0_), channel_id=1, source_target_pairs={{0,1},{1,0},{2,3},{3,2},{4,5},{5,4},{6,7},{7,6},{8,9},{9,8},{10,11... | collective-permute-start | bytes 270344 | tf_op jit(solution)/shard_map/ppermute | solution.py:257
  30.2 0.9 %collective-permute-done.12.refs_1_ = f32[176,128]{1,0:T(8,128)S(1)} collective-permute-done((f32[176,128]{1,0:T(8,128)S(1)}, f32[176,128]{1,0:T(8,128)S(1)}, u32[]{:S(2)}, u32[]{:S(2)}) %collective-permute-start.12) | collective-permute-done | bytes 90144 | tf_op jit(solution)/shard_map/ppermute | solution.py:257
  31.2 3.8 %shard_map.62 = (bf16[8,8192]{1,0:T(8,128)(2,1)S(1)}, f32[8,256]{1,0:T(8,128)}, f32[8,8]{1,0:T(8,128)S(1)}, f32[1]{0:T(128)}) custom-call(f32[176,128]{1,0:T(8,128)S(1)} %add.46.refs_0_, f32[176,128]{1,0:T(8,128)S(1)} %collective-permute-done.12.refs_1_, bf16[8,8192]{1,0:T(8,128)(2,1)S(1)} %get-tuple-element.41.refs_2_, ...), custom_call_target="tpu_custom_call" | custom-call | tf_op jit(solution)/shard_map/pallas_call | solution.py:368
  35.6 0.0 copy-start.3
  35.7 0.0 copy-start.4
  35.7 0.6 %copy-done.3 = bf16[8,8192]{1,0:T(8,128)(2,1)} copy-done((bf16[8,8192]{1,0:T(8,128)(2,1)}, bf16[8,8192]{1,0:T(8,128)(2,1)S(1)}, u32[]{:S(2)}) %copy-start.3) | copy-done | bytes 131096
  36.3 0.0 copy-done.4
  (7 shorter events, 0.1 us)
Async XLA Ops:
  0.6 3.5 %collective-permute-start.5 = (bf16[4,8,2048]{2,1,0:T(8,128)(2,1)}, bf16[4,8,2048]{2,1,0:T(8,128)(2,1)S(1)}, u32[]{:S(2)}, u32[]{:S(2)}) collective-permute-start(bf16[4,8,2048]{2,1,0:T(8,128)(2,1)} %bitcast.23), channel_id=1, source_target_pairs={{0,1},{1,0},{2,3},{3,2},{4,5},{5,4},{6,7},{7,6},{8,9},{9,8},{10,11... | collective-permute-start | bytes 393224 | tf_op jit(solution)/shard_map/ppermute | solution.py:257
  1.2 0.9 %copy-start = (bf16[8,8192]{1,0:T(8,128)(2,1)S(1)}, bf16[8,8192]{1,0:T(8,128)(2,1)}, u32[]{:S(2)}) copy-start(bf16[8,8192]{1,0:T(8,128)(2,1)} %param.5) | copy-start | bytes 393220
  2.1 4.7 %copy-start.2 = (bf16[8192,256]{1,0:T(8,128)(2,1)S(1)}, bf16[8192,256]{1,0:T(8,128)(2,1)}, u32[]{:S(2)}) copy-start(bf16[8192,256]{1,0:T(8,128)(2,1)} %refs_0_.2) | copy-start | bytes 12582916
  4.2 5.1 %collective-permute-start.6 = (bf16[2,1,8,2048]{3,2,0,1:T(8,128)(2,1)S(1)}, bf16[2,1,8,2048]{3,2,0,1:T(8,128)(2,1)S(1)}, u32[]{:S(2)}, u32[]{:S(2)}) collective-permute-start(bf16[2,1,8,2048]{3,2,0,1:T(8,128)(2,1)S(1)} %bitcast.27), channel_id=1, source_target_pairs={{0,3},{1,2},{2,1},{3,0},{4,7},{5,6},{6,5},{7,4},{8,11},{9,10},{10,... | collective-permute-start | bytes 196616 | tf_op jit(solution)/shard_map/ppermute | solution.py:257
  6.8 2.5 %copy-start.1 = (s32[1,4,4]{2,1,0:T(4,128)S(1)}, s32[1,4,4]{2,1,0:T(4,128)}, u32[]{:S(2)}) copy-start(s32[1,4,4]{2,1,0:T(4,128)} %refs_0_.3) | copy-start | bytes 196
  10.6 1.4 %collective-permute-start.7 = (f32[176,128]{1,0:T(8,128)S(1)}, f32[176,128]{1,0:T(8,128)S(1)}, u32[]{:S(2)}, u32[]{:S(2)}) collective-permute-start(f32[176,128]{1,0:T(8,128)S(1)} %get-tuple-element.40), channel_id=1, source_target_pairs={{0,1},{1,0},{2,3},{3,2},{4,5},{5,4},{6,7},{7,6},{8,9},{9,8},{10,11... | collective-permute-start | bytes 270344 | tf_op jit(solution)/shard_map/ppermute | solution.py:257
  12.0 4.0 %collective-permute-start.8 = (f32[176,128]{1,0:T(8,128)S(1)}, f32[176,128]{1,0:T(8,128)S(1)}, u32[]{:S(2)}, u32[]{:S(2)}) collective-permute-start(f32[176,128]{1,0:T(8,128)S(1)} %add.42), channel_id=1, source_target_pairs={{0,3},{1,4},{2,7},{3,0},{4,1},{5,6},{6,5},{7,2},{8,13},{9,10},{10,... | collective-permute-start | bytes 270344 | tf_op jit(solution)/shard_map/ppermute | solution.py:257
  16.0 4.0 %collective-permute-start.9 = (f32[176,128]{1,0:T(8,128)S(1)}, f32[176,128]{1,0:T(8,128)S(1)}, u32[]{:S(2)}, u32[]{:S(2)}) collective-permute-start(f32[176,128]{1,0:T(8,128)S(1)} %add.43), channel_id=1, source_target_pairs={{0,5},{1,2},{2,1},{3,6},{4,7},{5,0},{6,3},{7,4},{8,11},{9,12},{10,... | collective-permute-start | bytes 270344 | tf_op jit(solution)/shard_map/ppermute | solution.py:257
  20.0 4.0 %collective-permute-start.10 = (f32[176,128]{1,0:T(8,128)S(1)}, f32[176,128]{1,0:T(8,128)S(1)}, u32[]{:S(2)}, u32[]{:S(2)}) collective-permute-start(f32[176,128]{1,0:T(8,128)S(1)} %add.44), channel_id=1, source_target_pairs={{0,9},{1,16},{2,19},{3,10},{4,21},{5,12},{6,15},{7,22},{8,25},{9,0... | collective-permute-start | bytes 270344 | tf_op jit(solution)/shard_map/ppermute | solution.py:257
  24.1 5.3 %collective-permute-start.11 = (f32[176,128]{1,0:T(8,128)S(1)}, f32[176,128]{1,0:T(8,128)S(1)}, u32[]{:S(2)}, u32[]{:S(2)}) collective-permute-start(f32[176,128]{1,0:T(8,128)S(1)} %add.45), channel_id=1, source_target_pairs={{0,17},{1,8},{2,11},{3,18},{4,13},{5,20},{6,23},{7,14},{8,1},{9,24... | collective-permute-start | bytes 270344 | tf_op jit(solution)/shard_map/ppermute | solution.py:257
  29.4 1.8 %collective-permute-start.12 = (f32[176,128]{1,0:T(8,128)S(1)}, f32[176,128]{1,0:T(8,128)S(1)}, u32[]{:S(2)}, u32[]{:S(2)}) collective-permute-start(f32[176,128]{1,0:T(8,128)S(1)} %add.46.refs_0_), channel_id=1, source_target_pairs={{0,1},{1,0},{2,3},{3,2},{4,5},{5,4},{6,7},{7,6},{8,9},{9,8},{10,11... | collective-permute-start | bytes 270344 | tf_op jit(solution)/shard_map/ppermute | solution.py:257
  35.6 0.7 %copy-start.3 = (bf16[8,8192]{1,0:T(8,128)(2,1)}, bf16[8,8192]{1,0:T(8,128)(2,1)S(1)}, u32[]{:S(2)}) copy-start(bf16[8,8192]{1,0:T(8,128)(2,1)S(1)} %get-tuple-element.50) | copy-start | bytes 393220
  35.7 0.6 %copy-start.4 = (f32[8,8]{1,0:T(8,128)}, f32[8,8]{1,0:T(8,128)S(1)}, u32[]{:S(2)}) copy-start(f32[8,8]{1,0:T(8,128)S(1)} %get-tuple-element.53) | copy-start | bytes 772

commit v4 on v3

--- a/solution.py
+++ b/solution.py
@@ -33,32 +33,25 @@
     return lax.dot_general(part, part, (((0,), (0,)), ((), ())), preferred_element_type=F32)
 
 
-def copies(source_ref, target_ref, bounds, sems):
-    made = []
+def fetch_kernel(far_ref, near_ref, sem):
+    copy = pltpu.make_async_copy(far_ref, near_ref, sem)
+    copy.start()
+    copy.wait()
+
+
+def gram_kernel(bounds, basis_ref, fold_ref, near_ref, sems):
+    rank = near_ref.shape[1]
+    half, quarter = rank // 2, rank // 4
+    moves = []
     for index, (low, high) in enumerate(bounds):
         part = pl.ds(low, high - low)
-        made.append(
-            pltpu.make_async_copy(source_ref.at[part], target_ref.at[part], sems.at[index])
+        moves.append(
+            pltpu.make_async_copy(basis_ref.at[part], near_ref.at[part], sems.at[index])
         )
-        made[index].start()
-    return made
-
-
-def open_kernel(done, boxes_ref, basis_ref, own_ref, near_ref, total_ref, box_sem, sems):
-    box = pltpu.make_async_copy(boxes_ref, own_ref, box_sem)
-    box.start()
-    (rows,) = copies(basis_ref, near_ref, [(0, done)], sems)
-    rows.wait()
-    total_ref[...] = gram_of(near_ref[0:done])
-    box.wait()
-
-
-def gram_kernel(bounds, basis_ref, held_ref, total_ref, fold_ref, near_ref, sems):
-    rank = near_ref.shape[1]
-    half, quarter = rank // 2, rank // 4
-    total = total_ref[...]
-    for copy, (low, high) in zip(copies(basis_ref, near_ref, bounds, sems), bounds):
-        copy.wait()
+        moves[index].start()
+    total = jnp.zeros((rank, rank), F32)
+    for move, (low, high) in zip(moves, bounds):
+        move.wait()
         total += gram_of(near_ref[low:high])
     upper = lane_at_least((quarter, half), quarter)
     fold_ref[0:quarter] = jnp.where(upper, 2.0, 1.0) * total[0:quarter, 0:half]
@@ -316,31 +309,28 @@
 
     boxes = snaps_box.reshape(snapcount, groups, block_len).transpose(1, 0, 2)
     peer = exchange(boxes, total, (1, 1))
-    eighth = local_cells // 8
-    done = 2 * eighth
-    rest = [(done, 3 * eighth), (3 * eighth, 5 * eighth), (5 * eighth, local_cells)]
-    held = like(basis.shape, basis.dtype)
-    own, near, total_gram = kernel_call(
-        lambda *refs: open_kernel(done, *refs),
-        (like(boxes.shape, boxes.dtype), held, like((rank, rank), F32)),
-        [HBM, HBM],
-        (VMEM, VMEM, VMEM),
-        [DMA(()), DMA((1,))],
-        cost_estimate=gram_cost(done, rank),
-    )(boxes, basis)
+    own = kernel_call(
+        fetch_kernel,
+        like(boxes.shape, boxes.dtype),
+        [HBM],
+        VMEM,
+        [DMA(())],
+        cost_estimate=gram_cost(local_cells, rank),
+    )(boxes)
     keep, far, sources = spread_boxes(own, peer, groups, total)
 
     half, quarter = rank // 2, rank // 4
     fold_rows = 3 * quarter + half
+    eighth = local_cells // 8
+    bounds = [(0, eighth), (eighth, 3 * eighth), (3 * eighth, local_cells)]
     fold, near = kernel_call(
-        lambda *refs: gram_kernel(rest, *refs),
-        (like((fold_rows, half), F32), held),
-        [HBM, VMEM, VMEM],
+        lambda *refs: gram_kernel(bounds, *refs),
+        (like((fold_rows, half), F32), like(basis.shape, basis.dtype)),
+        [HBM],
         (VMEM, VMEM),
-        [DMA((len(rest),))],
-        input_output_aliases={1: 1},
-        cost_estimate=gram_cost(local_cells - done, rank),
-    )(basis, near, total_gram)
+        [DMA((len(bounds),))],
+        cost_estimate=gram_cost(local_cells, rank),
+    )(basis)
     used = fold_rows + (rank // LANES + 1) * snapcount
     share = -(-used // 16) * 8
     part = like((share, LANES), F32)

time: 36.5 us -> 35.3 us (0.967)
  starting transfers between devices: 11.4 us -> 13.1 us
  Pallas kernels: 9.44 us -> 7.76 us
  waiting for transfers between devices: 12.5 us -> 11.2 us
    ppermute x8, starting transfers between devices: 11.4 us -> 13.1 us  [exchange(): lax.ppermute(value, AXES, [(index, partner(index)) for index in range(tot...]
    pallas_call x2, Pallas kernels: 4.29 us -> 2.62 us  [the longest x1 2.46 us: local(): kernel_call(lambda *refs: gram_kernel(bounds, *refs), (like((fold_rows, h...]
    ppermute x8, waiting for transfers between devices: 12.5 us -> 11.2 us  [exchange(): lax.ppermute(value, AXES, [(index, partner(index)) for index in range(tot...]
  transfers between devices with their start and end apart: 8 -> 8, of which waited for: 7 -> 7; matrix products, arithmetic and copies ran while one was open for 0% -> 0% of each run, Pallas kernels for 12% -> 7%
where the time goes in v4:
time: 35.3 us; the launch traced here: 35.1 us
  starting transfers between devices  13.1 us (37%)
  waiting for transfers between devices  11.2 us (32%)
  Pallas kernels  7.76 us (22%)
  local copies, waits for them, and re-layouts  1.56 us (4%)
  between operations  1.38 us (4%)
    ppermute x8, starting transfers between devices, exchange(): lax.ppermute(value, AXES, [(index, partner(index)) for index in range(tot...  13.1 us
    ppermute x8, waiting for transfers between devices, exchange(): lax.ppermute(value, AXES, [(index, partner(index)) for index in range(tot...  11.2 us
    pallas_call x1, Pallas kernels, local(): kernel_call(lambda *refs: finish_kernel(total, *refs), (like((snapcount,...  3.81 us
    pallas_call x1, Pallas kernels, local(): kernel_call(lambda *refs: gram_kernel(bounds, *refs), (like((fold_rows, h...  2.46 us
    unnamed x10, local copies, waits for them, and re-layouts  1.56 us
    pallas_call x1, Pallas kernels, local(): kernel_call(lambda *refs: project_kernel(sources, total, *refs), (part, p...  1.32 us
  transfers between devices with their start and end apart: 8, of which 7 were waited for; matrix products, arithmetic and copies ran while one was open for 0% of the time, Pallas kernels for 7%

profile of v4, /device:TPU:0, one launch (start us, length us, event | category | flops | bytes accessed | tf_op | source)
XLA Modules:
  0.0 35.1 jit_solution(11027845984510716820)
XLA Ops:
  0.6 0.0 copy-start
  0.6 0.6 %collective-permute-start.5 = (bf16[4,8,2048]{2,1,0:T(8,128)(2,1)}, bf16[4,8,2048]{2,1,0:T(8,128)(2,1)S(1)}, u32[]{:S(2)}, u32[]{:S(2)}) collective-permute-start(bf16[4,8,2048]{2,1,0:T(8,128)(2,1)} %bitcast.25), channel_id=1, source_target_pairs={{0,1},{1,0},{2,3},{3,2},{4,5},{5,4},{6,7},{7,6},{8,9},{9,8},{10,11... | collective-permute-start | bytes 393224 | tf_op jit(solution)/shard_map/ppermute | solution.py:250
  1.2 0.0 copy-start.1
  1.2 0.9 %copy-done.1 = bf16[8,8192]{1,0:T(8,128)(2,1)S(1)} copy-done((bf16[8,8192]{1,0:T(8,128)(2,1)S(1)}, bf16[8,8192]{1,0:T(8,128)(2,1)}, u32[]{:S(2)}) %copy-start.1) | copy-done | bytes 131096
  2.1 0.0 copy-start.2
  2.1 0.2 shard_map.58.refs_0_
  2.3 0.1 collective-permute-done.5.refs_1_
  2.4 2.7 %collective-permute-start.6 = (bf16[2,1,8,2048]{3,2,0,1:T(8,128)(2,1)S(1)}, bf16[2,1,8,2048]{3,2,0,1:T(8,128)(2,1)S(1)}, u32[]{:S(2)}, u32[]{:S(2)}) collective-permute-start(bf16[2,1,8,2048]{3,2,0,1:T(8,128)(2,1)S(1)} %bitcast.27), channel_id=1, source_target_pairs={{0,3},{1,2},{2,1},{3,0},{4,7},{5,6},{6,5},{7,4},{8,11},{9,10},{10,... | collective-permute-start | bytes 196616 | tf_op jit(solution)/shard_map/ppermute | solution.py:250
  5.1 0.0 copy-done.2
  5.1 2.5 %shard_map.60 = (f32[320,128]{1,0:T(8,128)S(1)}, bf16[8192,256]{1,0:T(8,128)(2,1)S(1)}) custom-call(bf16[8192,256]{1,0:T(8,128)(2,1)S(1)} %copy-done.2), custom_call_target="tpu_custom_call" | custom-call | flops 1073741824 | bytes 4194304 | tf_op jit(solution)/shard_map/pallas_call | solution.py:326
  7.5 0.0 collective-permute-done.6
  7.5 0.0 copy-done
  7.6 1.3 %shard_map.61 = (f32[176,128]{1,0:T(8,128)S(1)}, f32[176,128]{1,0:T(8,128)S(1)}, bf16[8,8192]{1,0:T(8,128)(2,1)S(1)}) custom-call(s32[1,4,4]{2,1,0:T(4,128)S(1)} %copy-done, bf16[2,8,2048]{2,1,0:T(8,128)(2,1)S(1)} %bitcast.23, bf16[2,8,2048]{2,1,0:T(8,128)(2,1)S(1)} %bitcast.24, bf16[8192,256]{1,0:T(8,128)(2,1)S(1)} %get-tuple-element.31.refs_3_, ...), custom_call_target="tpu_custom_call" | custom-call | tf_op jit(solution)/shard_map/pallas_call | solution.py:337
  8.9 0.4 %collective-permute-start.7 = (f32[176,128]{1,0:T(8,128)S(1)}, f32[176,128]{1,0:T(8,128)S(1)}, u32[]{:S(2)}, u32[]{:S(2)}) collective-permute-start(f32[176,128]{1,0:T(8,128)S(1)} %get-tuple-element.34), channel_id=1, source_target_pairs={{0,1},{1,0},{2,3},{3,2},{4,5},{5,4},{6,7},{7,6},{8,9},{9,8},{10,11... | collective-permute-start | bytes 270344 | tf_op jit(solution)/shard_map/ppermute | solution.py:250
  9.3 0.9 %collective-permute-done.7 = f32[176,128]{1,0:T(8,128)S(1)} collective-permute-done((f32[176,128]{1,0:T(8,128)S(1)}, f32[176,128]{1,0:T(8,128)S(1)}, u32[]{:S(2)}, u32[]{:S(2)}) %collective-permute-start.7) | collective-permute-done | bytes 90144 | tf_op jit(solution)/shard_map/ppermute | solution.py:250
  10.3 1.9 %collective-permute-start.8 = (f32[176,128]{1,0:T(8,128)S(1)}, f32[176,128]{1,0:T(8,128)S(1)}, u32[]{:S(2)}, u32[]{:S(2)}) collective-permute-start(f32[176,128]{1,0:T(8,128)S(1)} %add.42), channel_id=1, source_target_pairs={{0,3},{1,4},{2,7},{3,0},{4,1},{5,6},{6,5},{7,2},{8,13},{9,10},{10,... | collective-permute-start | bytes 270344 | tf_op jit(solution)/shard_map/ppermute | solution.py:250
  12.1 2.2 %collective-permute-done.8 = f32[176,128]{1,0:T(8,128)S(1)} collective-permute-done((f32[176,128]{1,0:T(8,128)S(1)}, f32[176,128]{1,0:T(8,128)S(1)}, u32[]{:S(2)}, u32[]{:S(2)}) %collective-permute-start.8) | collective-permute-done | bytes 90144 | tf_op jit(solution)/shard_map/ppermute | solution.py:250
  14.4 1.8 %collective-permute-start.9 = (f32[176,128]{1,0:T(8,128)S(1)}, f32[176,128]{1,0:T(8,128)S(1)}, u32[]{:S(2)}, u32[]{:S(2)}) collective-permute-start(f32[176,128]{1,0:T(8,128)S(1)} %add.43), channel_id=1, source_target_pairs={{0,5},{1,2},{2,1},{3,6},{4,7},{5,0},{6,3},{7,4},{8,11},{9,12},{10,... | collective-permute-start | bytes 270344 | tf_op jit(solution)/shard_map/ppermute | solution.py:250
  16.2 2.2 %collective-permute-done.9 = f32[176,128]{1,0:T(8,128)S(1)} collective-permute-done((f32[176,128]{1,0:T(8,128)S(1)}, f32[176,128]{1,0:T(8,128)S(1)}, u32[]{:S(2)}, u32[]{:S(2)}) %collective-permute-start.9) | collective-permute-done | bytes 90144 | tf_op jit(solution)/shard_map/ppermute | solution.py:250
  18.4 1.9 %collective-permute-start.10 = (f32[176,128]{1,0:T(8,128)S(1)}, f32[176,128]{1,0:T(8,128)S(1)}, u32[]{:S(2)}, u32[]{:S(2)}) collective-permute-start(f32[176,128]{1,0:T(8,128)S(1)} %add.44), channel_id=1, source_target_pairs={{0,9},{1,16},{2,19},{3,10},{4,21},{5,12},{6,15},{7,22},{8,25},{9,0... | collective-permute-start | bytes 270344 | tf_op jit(solution)/shard_map/ppermute | solution.py:250
  20.3 2.5 %collective-permute-done.10 = f32[176,128]{1,0:T(8,128)S(1)} collective-permute-done((f32[176,128]{1,0:T(8,128)S(1)}, f32[176,128]{1,0:T(8,128)S(1)}, u32[]{:S(2)}, u32[]{:S(2)}) %collective-permute-start.10) | collective-permute-done | bytes 90144 | tf_op jit(solution)/shard_map/ppermute | solution.py:250
  22.8 3.1 %collective-permute-start.11 = (f32[176,128]{1,0:T(8,128)S(1)}, f32[176,128]{1,0:T(8,128)S(1)}, u32[]{:S(2)}, u32[]{:S(2)}) collective-permute-start(f32[176,128]{1,0:T(8,128)S(1)} %add.45), channel_id=1, source_target_pairs={{0,17},{1,8},{2,11},{3,18},{4,13},{5,20},{6,23},{7,14},{8,1},{9,24... | collective-permute-start | bytes 270344 | tf_op jit(solution)/shard_map/ppermute | solution.py:250
  26.0 2.3 %collective-permute-done.11 = f32[176,128]{1,0:T(8,128)S(1)} collective-permute-done((f32[176,128]{1,0:T(8,128)S(1)}, f32[176,128]{1,0:T(8,128)S(1)}, u32[]{:S(2)}, u32[]{:S(2)}) %collective-permute-start.11) | collective-permute-done | bytes 90144 | tf_op jit(solution)/shard_map/ppermute | solution.py:250
  28.2 0.8 %collective-permute-start.12 = (f32[176,128]{1,0:T(8,128)S(1)}, f32[176,128]{1,0:T(8,128)S(1)}, u32[]{:S(2)}, u32[]{:S(2)}) collective-permute-start(f32[176,128]{1,0:T(8,128)S(1)} %add.46.refs_0_), channel_id=1, source_target_pairs={{0,1},{1,0},{2,3},{3,2},{4,5},{5,4},{6,7},{7,6},{8,9},{9,8},{10,11... | collective-permute-start | bytes 270344 | tf_op jit(solution)/shard_map/ppermute | solution.py:250
  29.0 0.9 %collective-permute-done.12.refs_1_ = f32[176,128]{1,0:T(8,128)S(1)} collective-permute-done((f32[176,128]{1,0:T(8,128)S(1)}, f32[176,128]{1,0:T(8,128)S(1)}, u32[]{:S(2)}, u32[]{:S(2)}) %collective-permute-start.12) | collective-permute-done | bytes 90144 | tf_op jit(solution)/shard_map/ppermute | solution.py:250
  30.0 3.8 %shard_map.62 = (bf16[8,8192]{1,0:T(8,128)(2,1)S(1)}, f32[8,256]{1,0:T(8,128)}, f32[8,8]{1,0:T(8,128)S(1)}, f32[1]{0:T(128)}) custom-call(f32[176,128]{1,0:T(8,128)S(1)} %add.46.refs_0_, f32[176,128]{1,0:T(8,128)S(1)} %collective-permute-done.12.refs_1_, bf16[8,8192]{1,0:T(8,128)(2,1)S(1)} %get-tuple-element.35.refs_2_, ...), custom_call_target="tpu_custom_call" | custom-call | tf_op jit(solution)/shard_map/pallas_call | solution.py:358
  34.5 0.0 copy-start.3
  34.5 0.0 copy-start.4
  34.5 0.6 %copy-done.3 = bf16[8,8192]{1,0:T(8,128)(2,1)} copy-done((bf16[8,8192]{1,0:T(8,128)(2,1)}, bf16[8,8192]{1,0:T(8,128)(2,1)S(1)}, u32[]{:S(2)}) %copy-start.3) | copy-done | bytes 131096
  35.1 0.0 copy-done.4
  (7 shorter events, 0.1 us)
Async XLA Ops:
  0.6 6.9 %copy-start = (s32[1,4,4]{2,1,0:T(4,128)S(1)}, s32[1,4,4]{2,1,0:T(4,128)}, u32[]{:S(2)}) copy-start(s32[1,4,4]{2,1,0:T(4,128)} %refs_0_.3) | copy-start | bytes 196
  0.6 1.8 %collective-permute-start.5 = (bf16[4,8,2048]{2,1,0:T(8,128)(2,1)}, bf16[4,8,2048]{2,1,0:T(8,128)(2,1)S(1)}, u32[]{:S(2)}, u32[]{:S(2)}) collective-permute-start(bf16[4,8,2048]{2,1,0:T(8,128)(2,1)} %bitcast.25), channel_id=1, source_target_pairs={{0,1},{1,0},{2,3},{3,2},{4,5},{5,4},{6,7},{7,6},{8,9},{9,8},{10,11... | collective-permute-start | bytes 393224 | tf_op jit(solution)/shard_map/ppermute | solution.py:250
  1.2 0.9 %copy-start.1 = (bf16[8,8192]{1,0:T(8,128)(2,1)S(1)}, bf16[8,8192]{1,0:T(8,128)(2,1)}, u32[]{:S(2)}) copy-start(bf16[8,8192]{1,0:T(8,128)(2,1)} %param.5) | copy-start | bytes 393220
  2.1 3.0 %copy-start.2 = (bf16[8192,256]{1,0:T(8,128)(2,1)S(1)}, bf16[8192,256]{1,0:T(8,128)(2,1)}, u32[]{:S(2)}) copy-start(bf16[8192,256]{1,0:T(8,128)(2,1)} %refs_0_.2) | copy-start | bytes 12582916
  2.4 5.1 %collective-permute-start.6 = (bf16[2,1,8,2048]{3,2,0,1:T(8,128)(2,1)S(1)}, bf16[2,1,8,2048]{3,2,0,1:T(8,128)(2,1)S(1)}, u32[]{:S(2)}, u32[]{:S(2)}) collective-permute-start(bf16[2,1,8,2048]{3,2,0,1:T(8,128)(2,1)S(1)} %bitcast.27), channel_id=1, source_target_pairs={{0,3},{1,2},{2,1},{3,0},{4,7},{5,6},{6,5},{7,4},{8,11},{9,10},{10,... | collective-permute-start | bytes 196616 | tf_op jit(solution)/shard_map/ppermute | solution.py:250
  8.9 1.4 %collective-permute-start.7 = (f32[176,128]{1,0:T(8,128)S(1)}, f32[176,128]{1,0:T(8,128)S(1)}, u32[]{:S(2)}, u32[]{:S(2)}) collective-permute-start(f32[176,128]{1,0:T(8,128)S(1)} %get-tuple-element.34), channel_id=1, source_target_pairs={{0,1},{1,0},{2,3},{3,2},{4,5},{5,4},{6,7},{7,6},{8,9},{9,8},{10,11... | collective-permute-start | bytes 270344 | tf_op jit(solution)/shard_map/ppermute | solution.py:250
  10.3 4.1 %collective-permute-start.8 = (f32[176,128]{1,0:T(8,128)S(1)}, f32[176,128]{1,0:T(8,128)S(1)}, u32[]{:S(2)}, u32[]{:S(2)}) collective-permute-start(f32[176,128]{1,0:T(8,128)S(1)} %add.42), channel_id=1, source_target_pairs={{0,3},{1,4},{2,7},{3,0},{4,1},{5,6},{6,5},{7,2},{8,13},{9,10},{10,... | collective-permute-start | bytes 270344 | tf_op jit(solution)/shard_map/ppermute | solution.py:250
  14.4 4.0 %collective-permute-start.9 = (f32[176,128]{1,0:T(8,128)S(1)}, f32[176,128]{1,0:T(8,128)S(1)}, u32[]{:S(2)}, u32[]{:S(2)}) collective-permute-start(f32[176,128]{1,0:T(8,128)S(1)} %add.43), channel_id=1, source_target_pairs={{0,5},{1,2},{2,1},{3,6},{4,7},{5,0},{6,3},{7,4},{8,11},{9,12},{10,... | collective-permute-start | bytes 270344 | tf_op jit(solution)/shard_map/ppermute | solution.py:250
  18.4 4.4 %collective-permute-start.10 = (f32[176,128]{1,0:T(8,128)S(1)}, f32[176,128]{1,0:T(8,128)S(1)}, u32[]{:S(2)}, u32[]{:S(2)}) collective-permute-start(f32[176,128]{1,0:T(8,128)S(1)} %add.44), channel_id=1, source_target_pairs={{0,9},{1,16},{2,19},{3,10},{4,21},{5,12},{6,15},{7,22},{8,25},{9,0... | collective-permute-start | bytes 270344 | tf_op jit(solution)/shard_map/ppermute | solution.py:250
  22.8 5.4 %collective-permute-start.11 = (f32[176,128]{1,0:T(8,128)S(1)}, f32[176,128]{1,0:T(8,128)S(1)}, u32[]{:S(2)}, u32[]{:S(2)}) collective-permute-start(f32[176,128]{1,0:T(8,128)S(1)} %add.45), channel_id=1, source_target_pairs={{0,17},{1,8},{2,11},{3,18},{4,13},{5,20},{6,23},{7,14},{8,1},{9,24... | collective-permute-start | bytes 270344 | tf_op jit(solution)/shard_map/ppermute | solution.py:250
  28.2 1.7 %collective-permute-start.12 = (f32[176,128]{1,0:T(8,128)S(1)}, f32[176,128]{1,0:T(8,128)S(1)}, u32[]{:S(2)}, u32[]{:S(2)}) collective-permute-start(f32[176,128]{1,0:T(8,128)S(1)} %add.46.refs_0_), channel_id=1, source_target_pairs={{0,1},{1,0},{2,3},{3,2},{4,5},{5,4},{6,7},{7,6},{8,9},{9,8},{10,11... | collective-permute-start | bytes 270344 | tf_op jit(solution)/shard_map/ppermute | solution.py:250
  34.5 0.7 %copy-start.3 = (bf16[8,8192]{1,0:T(8,128)(2,1)}, bf16[8,8192]{1,0:T(8,128)(2,1)S(1)}, u32[]{:S(2)}) copy-start(bf16[8,8192]{1,0:T(8,128)(2,1)S(1)} %get-tuple-element.44) | copy-start | bytes 393220
  34.5 0.6 %copy-start.4 = (f32[8,8]{1,0:T(8,128)}, f32[8,8]{1,0:T(8,128)S(1)}, u32[]{:S(2)}) copy-start(f32[8,8]{1,0:T(8,128)S(1)} %get-tuple-element.47) | copy-start | bytes 772

commit v5 on v4

--- a/solution.py
+++ b/solution.py
@@ -7,7 +7,7 @@
 
 AXES = ("rows", "sub")
 HIGH = lax.Precision.HIGHEST
-LANES = 128
+LANES, SUBLANES = 128, 8
 GUARD = 1.0 / 64.0
 STRETCHES = 8
 HBM = pl.BlockSpec(memory_space=pltpu.HBM)
@@ -25,10 +25,6 @@
     )
 
 
-def lane_at_least(shape, bound):
-    return lax.broadcasted_iota(jnp.int32, shape, len(shape) - 1) >= bound
-
-
 def gram_of(part):
     return lax.dot_general(part, part, (((0,), (0,)), ((), ())), preferred_element_type=F32)
 
@@ -39,27 +35,62 @@
     copy.wait()
 
 
-def gram_kernel(bounds, basis_ref, fold_ref, near_ref, sems):
+def triangle(count):
+    shape = (count, count)
+    return (
+        lax.broadcasted_iota(jnp.int32, shape, 0),
+        lax.broadcasted_iota(jnp.int32, shape, 1),
+    )
+
+
+def place_of(order_ref, source):
+    position = lax.axis_index("sub")
+    order = order_ref[0].astype(F32)
+    rows = lax.broadcasted_iota(jnp.int32, order.shape, 0)
+    cols = lax.broadcasted_iota(jnp.int32, order.shape, 1)
+    wanted = (rows == position) & (cols == position ^ source)
+    return jnp.sum(jnp.where(wanted, order, 0.0)).astype(jnp.int32)
+
+
+def block_sums(sources, order_ref, blocks_ref, basis_ref, placed_ref):
+    _, snapcount, block_len = blocks_ref.shape
+    raw = jnp.zeros((snapcount, basis_ref.shape[1]), F32)
+    own = jnp.zeros((snapcount, snapcount), F32)
+    for index, source in enumerate(sources):
+        block = blocks_ref[index]
+        own += nt(block, block)
+        start = pl.multiple_of(place_of(order_ref, source) * block_len, block_len)
+        raw += jnp.dot(block, basis_ref[pl.ds(start, block_len), :], preferred_element_type=F32)
+        placed_ref[:, pl.ds(start, block_len)] = block
+    return raw, own
+
+
+def gram_kernel(
+    sources, order_ref, keep_ref, basis_ref, sums_ref, near_ref, placed_ref, sem
+):
+    move = pltpu.make_async_copy(basis_ref, near_ref, sem)
+    move.start()
+    move.wait()
+    snapcount = keep_ref.shape[1]
     rank = near_ref.shape[1]
-    half, quarter = rank // 2, rank // 4
-    moves = []
-    for index, (low, high) in enumerate(bounds):
-        part = pl.ds(low, high - low)
-        moves.append(
-            pltpu.make_async_copy(basis_ref.at[part], near_ref.at[part], sems.at[index])
-        )
-        moves[index].start()
-    total = jnp.zeros((rank, rank), F32)
-    for move, (low, high) in zip(moves, bounds):
-        move.wait()
-        total += gram_of(near_ref[low:high])
-    upper = lane_at_least((quarter, half), quarter)
-    fold_ref[0:quarter] = jnp.where(upper, 2.0, 1.0) * total[0:quarter, 0:half]
-    fold_ref[quarter : 2 * quarter] = jnp.where(
-        upper, total[quarter:half, 0:half], total[half : 3 * quarter, half:]
-    )
-    fold_ref[2 * quarter : 3 * quarter] = jnp.where(upper, 1.0, 2.0) * total[3 * quarter :, half:]
-    fold_ref[3 * quarter : 3 * quarter + half] = 2.0 * total[0:half, half:]
+    half = rank // 2
+    raw, own = block_sums(sources, order_ref, keep_ref, near_ref, placed_ref)
+    total = gram_of(near_ref[...])
+    row_id, col_id = triangle(half)
+    corner = total[half:, half:]
+    sums_ref[0:half] = jnp.where(row_id == col_id, 1.0, 2.0) * jnp.where(
+        row_id >= col_id, total[0:half, 0:half], corner
+    )
+    sums_ref[half:rank] = 2.0 * total[0:half, half:]
+    edge = jnp.sum(jnp.where(row_id == col_id, corner, 0.0), axis=0, keepdims=True)
+    at = rank
+    sums_ref[at : at + SUBLANES] = jnp.broadcast_to(edge, (SUBLANES, half))
+    at += SUBLANES
+    for part in range(rank // half):
+        sums_ref[at : at + snapcount] = raw[:, part * half : (part + 1) * half]
+        at += snapcount
+    sums_ref[at:] = jnp.zeros((sums_ref.shape[0] - at, half), F32)
+    sums_ref[at : at + snapcount, 0:snapcount] = own
 
 
 def device_index():
@@ -85,47 +116,30 @@
 def project_kernel(
     sources,
     total,
-    order_hbm,
-    keep_ref,
+    order_ref,
     far_ref,
     basis_ref,
-    fold_ref,
+    sums_ref,
+    placed_in,
     mine_ref,
     send_ref,
     placed_ref,
     out_ref,
-    order_ref,
-    sem,
 ):
-    table = pltpu.make_async_copy(order_hbm, order_ref, sem)
-    table.start()
-    near, snapcount, block_len = keep_ref.shape
+    snapcount = far_ref.shape[1]
+    rank = basis_ref.shape[1]
+    half = rank // 2
     share = mine_ref.shape[0]
-    fold_rows = fold_ref.shape[0]
-    rank = basis_ref.shape[1]
-    blocks = [keep_ref[index] for index in range(near)]
-    blocks += [far_ref[index] for index in range(len(sources) - near)]
-    out_ref[0:fold_rows] = fold_ref[...]
-    own = nt(blocks[0], blocks[0])
-    for block in blocks[1:]:
-        own += nt(block, block)
-    table.wait()
-    position = lax.axis_index("sub")
-    raw = jnp.zeros((snapcount, rank), F32)
-    for source, block in zip(sources, blocks):
-        start = order_ref[0, position, position ^ source] * block_len
-        start = pl.multiple_of(start, block_len)
-        raw += jnp.dot(block, basis_ref[pl.ds(start, block_len), :], preferred_element_type=F32)
-        placed_ref[:, pl.ds(start, block_len)] = block
-    at = fold_rows
-    for part in range(rank // LANES):
-        out_ref[at : at + snapcount] = raw[:, part * LANES : (part + 1) * LANES]
+    raw, own = block_sums(sources, order_ref, far_ref, basis_ref, placed_ref)
+    out_ref[...] = sums_ref[...]
+    at = rank + SUBLANES
+    for part in range(rank // half):
+        out_ref[at : at + snapcount] += raw[:, part * half : (part + 1) * half]
         at += snapcount
-    out_ref[at:] = jnp.zeros((out_ref.shape[0] - at, LANES), F32)
-    out_ref[at : at + snapcount, 0:snapcount] = own
+    out_ref[at : at + snapcount, 0:snapcount] += own
     side = parity(device_index(), total)
-    mine_ref[...] = out_ref[pl.ds(pl.multiple_of(side * share, 8), share)]
-    send_ref[...] = out_ref[pl.ds(pl.multiple_of((1 - side) * share, 8), share)]
+    mine_ref[...] = out_ref[pl.ds(pl.multiple_of(side * share, SUBLANES), share)]
+    send_ref[...] = out_ref[pl.ds(pl.multiple_of((1 - side) * share, SUBLANES), share)]
 
 
 def column(matrix, index):
@@ -155,55 +169,45 @@
     other_ref,
     placed_ref,
     basis_ref,
-    modes_hbm,
-    coeffs_hbm,
+    modes_ref,
+    coeffs_ref,
     upper_ref,
     weak_ref,
     sums_ref,
-    coeffs_ref,
     resid_ref,
-    modes_ref,
-    coeffs_sem,
-    modes_sems,
 ):
     snapcount, cells = placed_ref.shape
     rank = basis_ref.shape[1]
     cell_total = cells * total
-    half, quarter = rank // 2, rank // 4
+    half = rank // 2
     share = mine_ref.shape[0]
     first = parity(device_index(), total) == 0
     sums_ref[0:share] = jnp.where(first, mine_ref[...], other_ref[...])
     sums_ref[share:] = jnp.where(first, other_ref[...], mine_ref[...])
-    fold_rows = 3 * quarter + half
-    parts = rank // LANES
-    raw = jnp.concatenate(
-        [sums_ref[fold_rows + k * snapcount : fold_rows + (k + 1) * snapcount] for k in range(parts)],
-        axis=1,
-    )
-    at = fold_rows + parts * snapcount
+    at = rank + SUBLANES
+    parts = []
+    for _ in range(rank // half):
+        parts.append(sums_ref[at : at + snapcount])
+        at += snapcount
+    raw = jnp.concatenate(parts, axis=1)
     own = sums_ref[at : at + snapcount, 0:snapcount]
     coeffs = raw / cell_total
     coeffs_ref[...] = coeffs
-    coeffs_copy = pltpu.make_async_copy(coeffs_ref, coeffs_hbm, coeffs_sem)
-    coeffs_copy.start()
     narrow = coeffs.astype(jnp.bfloat16)
     rounded = narrow.astype(F32)
 
-    upper = lane_at_least((quarter, half), quarter)
-    middle = sums_ref[quarter : 2 * quarter]
-    left = jnp.concatenate([sums_ref[0:quarter], jnp.where(upper, middle, 0.0)], axis=0)
+    row_id, col_id = triangle(half)
+    square = sums_ref[0:half]
+    left = jnp.where(row_id >= col_id, square, 0.0)
     right = jnp.concatenate(
-        [
-            sums_ref[3 * quarter : fold_rows],
-            jnp.where(upper, 0.0, middle),
-            sums_ref[2 * quarter : 3 * quarter],
-        ],
-        axis=0,
-    )
+        [sums_ref[half:rank], jnp.where(row_id < col_id, square, 0.0)], axis=0
+    )
+    edge = sums_ref[rank : rank + 1]
     spread = jnp.concatenate(
         [
             jnp.dot(rounded[:, 0:half], left, precision=HIGH, preferred_element_type=F32),
-            jnp.dot(rounded, right, precision=HIGH, preferred_element_type=F32),
+            jnp.dot(rounded, right, precision=HIGH, preferred_element_type=F32)
+            + rounded[:, half:] * edge,
         ],
         axis=1,
     )
@@ -221,7 +225,6 @@
     columns = [jnp.broadcast_to(column(inverse, row), (snapcount, LANES)) for row in range(snapcount)]
 
     stretch = cells // STRETCHES
-    outgoing = []
     for index in range(STRETCHES):
         low = index * stretch
         fitted = nt(narrow, basis_ref[low : low + stretch])
@@ -233,14 +236,6 @@
             for row in range(1, snapcount):
                 modes += columns[row] * resid_ref[row : row + 1, lane : lane + LANES]
             modes_ref[:, lane : lane + LANES] = modes.astype(jnp.bfloat16)
-        part = pl.ds(low, stretch)
-        outgoing.append(
-            pltpu.make_async_copy(modes_ref.at[:, part], modes_hbm.at[:, part], modes_sems.at[index])
-        )
-        outgoing[index].start()
-    coeffs_copy.wait()
-    for copy in outgoing:
-        copy.wait()
 
 
 def exchange(value, total, masks):
@@ -319,32 +314,29 @@
     )(boxes)
     keep, far, sources = spread_boxes(own, peer, groups, total)
 
-    half, quarter = rank // 2, rank // 4
-    fold_rows = 3 * quarter + half
-    eighth = local_cells // 8
-    bounds = [(0, eighth), (eighth, 3 * eighth), (3 * eighth, local_cells)]
-    fold, near = kernel_call(
-        lambda *refs: gram_kernel(bounds, *refs),
-        (like((fold_rows, half), F32), like(basis.shape, basis.dtype)),
-        [HBM],
-        (VMEM, VMEM),
-        [DMA((len(bounds),))],
+    half = rank // 2
+    used = rank + SUBLANES + (rank // half + 1) * snapcount
+    share = -(-used // (2 * SUBLANES)) * SUBLANES
+    sums_shape = like((2 * share, half), F32)
+    placed_shape = like((snapcount, local_cells), snaps_box.dtype)
+    first = keep.shape[0]
+    sums, near, placed = kernel_call(
+        lambda *refs: gram_kernel(sources[:first], *refs),
+        (sums_shape, like(basis.shape, basis.dtype), placed_shape),
+        [VMEM, VMEM, HBM],
+        (VMEM, VMEM, VMEM),
+        [DMA(())],
         cost_estimate=gram_cost(local_cells, rank),
-    )(basis)
-    used = fold_rows + (rank // LANES + 1) * snapcount
-    share = -(-used // 16) * 8
-    part = like((share, LANES), F32)
+    )(box_order, keep, basis)
+    part = like((share, half), F32)
     mine, send, placed = kernel_call(
-        lambda *refs: project_kernel(sources, total, *refs),
-        (part, part, like((snapcount, local_cells), snaps_box.dtype)),
-        [ANY, VMEM, VMEM, VMEM, VMEM],
+        lambda *refs: project_kernel(sources[first:], total, *refs),
+        (part, part, placed_shape),
+        [VMEM, VMEM, VMEM, VMEM, VMEM],
         (VMEM, VMEM, VMEM),
-        [
-            pltpu.VMEM((2 * share, LANES), F32),
-            pltpu.SMEM(box_order.shape, box_order.dtype),
-            DMA(()),
-        ],
-    )(box_order, keep, far, near, fold)
+        [pltpu.VMEM(sums_shape.shape, F32)],
+        input_output_aliases={4: 2},
+    )(box_order, far, near, sums, placed)
 
     mine = mine + exchange(send, total, (1, 1))
     masks = flips(total)
@@ -364,14 +356,10 @@
             like((1,), F32),
         ),
         [VMEM, VMEM, VMEM, VMEM],
-        (HBM, HBM, VMEM, SMEM),
+        (VMEM, VMEM, VMEM, SMEM),
         [
-            pltpu.VMEM((2 * share, LANES), F32),
-            pltpu.VMEM((snapcount, rank), F32),
+            pltpu.VMEM(sums_shape.shape, F32),
             pltpu.VMEM((snapcount, local_cells), F32),
-            pltpu.VMEM((snapcount, local_cells), jnp.bfloat16),
-            DMA(()),
-            DMA((STRETCHES,)),
         ],
     )(mine, other, placed, near)
 

time: 35.3 us -> 31.2 us (0.88)
  Pallas kernels: 7.76 us -> 4.44 us
  waiting for transfers between devices: 11.2 us -> 10.4 us
    pallas_call x1, Pallas kernels: 3.81 us -> 1.75 us  [local(): kernel_call(lambda *refs: finish_kernel(total, *refs), (like((snapcount,...]
    pallas_call x2, Pallas kernels: 3.78 us -> 2.53 us  [the longest x1 2.01 us: local(): kernel_call(lambda *refs: gram_kernel(sources[:first], *refs), (sums_shap...]
    ppermute x8, waiting for transfers between devices: 11.2 us -> 10.4 us  [exchange(): lax.ppermute(value, AXES, [(index, partner(index)) for index in range(tot...]
  transfers between devices with their start and end apart: 8 -> 8, of which waited for: 7 -> 8; matrix products, arithmetic and copies ran while one was open for 0% -> 0% of each run, Pallas kernels for 7% -> 7%
where the time goes in v5:
time: 31.2 us; the launch traced here: 31.1 us
  starting transfers between devices  13.3 us (43%)
  waiting for transfers between devices  10.4 us (33%)
  Pallas kernels  4.44 us (14%)
  local copies, waits for them, and re-layouts  1.56 us (5%)
  between operations  1.37 us (4%)
    ppermute x8, starting transfers between devices, exchange(): lax.ppermute(value, AXES, [(index, partner(index)) for index in range(tot...  13.3 us
    ppermute x8, waiting for transfers between devices, exchange(): lax.ppermute(value, AXES, [(index, partner(index)) for index in range(tot...  10.4 us
    pallas_call x1, Pallas kernels, local(): kernel_call(lambda *refs: gram_kernel(sources[:first], *refs), (sums_shap...  2.01 us
    pallas_call x1, Pallas kernels, local(): kernel_call(lambda *refs: finish_kernel(total, *refs), (like((snapcount,...  1.75 us
    unnamed x10, local copies, waits for them, and re-layouts  1.56 us
  transfers between devices with their start and end apart: 8, of which 8 were waited for; matrix products, arithmetic and copies ran while one was open for 0% of the time, Pallas kernels for 7%

profile of v5, /device:TPU:0, one launch (start us, length us, event | category | flops | bytes accessed | tf_op | source)
XLA Modules:
  0.0 31.1 jit_solution(915680514182932048)
XLA Ops:
  0.6 0.0 copy-start
  0.6 0.6 %collective-permute-start.5 = (bf16[4,8,2048]{2,1,0:T(8,128)(2,1)}, bf16[4,8,2048]{2,1,0:T(8,128)(2,1)S(1)}, u32[]{:S(2)}, u32[]{:S(2)}) collective-permute-start(bf16[4,8,2048]{2,1,0:T(8,128)(2,1)} %bitcast.25), channel_id=1, source_target_pairs={{0,1},{1,0},{2,3},{3,2},{4,5},{5,4},{6,7},{7,6},{8,9},{9,8},{10,11... | collective-permute-start | bytes 393224 | tf_op jit(solution)/shard_map/ppermute | solution.py:245
  1.2 0.0 copy-start.1
  1.2 0.9 %copy-done.1 = bf16[8,8192]{1,0:T(8,128)(2,1)S(1)} copy-done((bf16[8,8192]{1,0:T(8,128)(2,1)S(1)}, bf16[8,8192]{1,0:T(8,128)(2,1)}, u32[]{:S(2)}) %copy-start.1) | copy-done | bytes 131096
  2.1 0.0 copy-start.2
  2.1 0.2 shard_map.58.refs_0_
  2.3 0.1 collective-permute-done.5.refs_1_
  2.4 2.7 %collective-permute-start.6 = (bf16[2,1,8,2048]{3,2,0,1:T(8,128)(2,1)S(1)}, bf16[2,1,8,2048]{3,2,0,1:T(8,128)(2,1)S(1)}, u32[]{:S(2)}, u32[]{:S(2)}) collective-permute-start(bf16[2,1,8,2048]{3,2,0,1:T(8,128)(2,1)S(1)} %bitcast.27), channel_id=1, source_target_pairs={{0,3},{1,2},{2,1},{3,0},{4,7},{5,6},{6,5},{7,4},{8,11},{9,10},{10,... | collective-permute-start | bytes 196616 | tf_op jit(solution)/shard_map/ppermute | solution.py:245
  5.1 0.0 copy-done
  5.1 0.0 copy-done.2
  5.1 2.0 %shard_map.60 = (f32[288,128]{1,0:T(8,128)S(1)}, bf16[8192,256]{1,0:T(8,128)(2,1)S(1)}, bf16[8,8192]{1,0:T(8,128)(2,1)S(1)}) custom-call(s32[1,4,4]{2,1,0:T(4,128)S(1)} %copy-done, bf16[2,8,2048]{2,1,0:T(8,128)(2,1)S(1)} %bitcast.24, bf16[8192,256]{1,0:T(8,128)(2,1)S(1)} %copy-done.2), custom_call_target="tpu_custom_call" | custom-call | flops 1073741824 | bytes 4194304 | tf_op jit(solution)/shard_map/pallas_call | solution.py:323
  7.1 0.1 collective-permute-done.6
  7.2 0.5 %shard_map.61 = (f32[144,128]{1,0:T(8,128)S(1)}, f32[144,128]{1,0:T(8,128)S(1)}, bf16[8,8192]{1,0:T(8,128)(2,1)S(1)}) custom-call(s32[1,4,4]{2,1,0:T(4,128)S(1)} %copy-done, bf16[2,8,2048]{2,1,0:T(8,128)(2,1)S(1)} %bitcast.23, bf16[8192,256]{1,0:T(8,128)(2,1)S(1)} %get-tuple-element.32.refs_2_.refs_3_, ...), custom_call_target="tpu_custom_call", output_to_operand_aliasing={{2}: (4, {})} | custom-call | tf_op jit(solution)/shard_map/pallas_call | solution.py:332
  7.7 0.3 %collective-permute-start.7 = (f32[144,128]{1,0:T(8,128)S(1)}, f32[144,128]{1,0:T(8,128)S(1)}, u32[]{:S(2)}, u32[]{:S(2)}) collective-permute-start(f32[144,128]{1,0:T(8,128)S(1)} %get-tuple-element.36), channel_id=1, source_target_pairs={{0,1},{1,0},{2,3},{3,2},{4,5},{5,4},{6,7},{7,6},{8,9},{9,8},{10,11... | collective-permute-start | bytes 221192 | tf_op jit(solution)/shard_map/ppermute | solution.py:245
  8.1 1.0 %collective-permute-done.7 = f32[144,128]{1,0:T(8,128)S(1)} collective-permute-done((f32[144,128]{1,0:T(8,128)S(1)}, f32[144,128]{1,0:T(8,128)S(1)}, u32[]{:S(2)}, u32[]{:S(2)}) %collective-permute-start.7) | collective-permute-done | bytes 73760 | tf_op jit(solution)/shard_map/ppermute | solution.py:245
  9.1 2.0 %collective-permute-start.8 = (f32[144,128]{1,0:T(8,128)S(1)}, f32[144,128]{1,0:T(8,128)S(1)}, u32[]{:S(2)}, u32[]{:S(2)}) collective-permute-start(f32[144,128]{1,0:T(8,128)S(1)} %add.42), channel_id=1, source_target_pairs={{0,3},{1,4},{2,7},{3,0},{4,1},{5,6},{6,5},{7,2},{8,13},{9,10},{10,... | collective-permute-start | bytes 221192 | tf_op jit(solution)/shard_map/ppermute | solution.py:245
  11.0 2.0 %collective-permute-done.8 = f32[144,128]{1,0:T(8,128)S(1)} collective-permute-done((f32[144,128]{1,0:T(8,128)S(1)}, f32[144,128]{1,0:T(8,128)S(1)}, u32[]{:S(2)}, u32[]{:S(2)}) %collective-permute-start.8) | collective-permute-done | bytes 73760 | tf_op jit(solution)/shard_map/ppermute | solution.py:245
  13.1 1.8 %collective-permute-start.9 = (f32[144,128]{1,0:T(8,128)S(1)}, f32[144,128]{1,0:T(8,128)S(1)}, u32[]{:S(2)}, u32[]{:S(2)}) collective-permute-start(f32[144,128]{1,0:T(8,128)S(1)} %add.43), channel_id=1, source_target_pairs={{0,5},{1,2},{2,1},{3,6},{4,7},{5,0},{6,3},{7,4},{8,11},{9,12},{10,... | collective-permute-start | bytes 221192 | tf_op jit(solution)/shard_map/ppermute | solution.py:245
  14.9 2.0 %collective-permute-done.9 = f32[144,128]{1,0:T(8,128)S(1)} collective-permute-done((f32[144,128]{1,0:T(8,128)S(1)}, f32[144,128]{1,0:T(8,128)S(1)}, u32[]{:S(2)}, u32[]{:S(2)}) %collective-permute-start.9) | collective-permute-done | bytes 73760 | tf_op jit(solution)/shard_map/ppermute | solution.py:245
  17.0 1.9 %collective-permute-start.10 = (f32[144,128]{1,0:T(8,128)S(1)}, f32[144,128]{1,0:T(8,128)S(1)}, u32[]{:S(2)}, u32[]{:S(2)}) collective-permute-start(f32[144,128]{1,0:T(8,128)S(1)} %add.44), channel_id=1, source_target_pairs={{0,9},{1,16},{2,19},{3,10},{4,21},{5,12},{6,15},{7,22},{8,25},{9,0... | collective-permute-start | bytes 221192 | tf_op jit(solution)/shard_map/ppermute | solution.py:245
  18.8 2.0 %collective-permute-done.10 = f32[144,128]{1,0:T(8,128)S(1)} collective-permute-done((f32[144,128]{1,0:T(8,128)S(1)}, f32[144,128]{1,0:T(8,128)S(1)}, u32[]{:S(2)}, u32[]{:S(2)}) %collective-permute-start.10) | collective-permute-done | bytes 73760 | tf_op jit(solution)/shard_map/ppermute | solution.py:245
  20.9 3.5 %collective-permute-start.11 = (f32[144,128]{1,0:T(8,128)S(1)}, f32[144,128]{1,0:T(8,128)S(1)}, u32[]{:S(2)}, u32[]{:S(2)}) collective-permute-start(f32[144,128]{1,0:T(8,128)S(1)} %add.45), channel_id=1, source_target_pairs={{0,17},{1,8},{2,11},{3,18},{4,13},{5,20},{6,23},{7,14},{8,1},{9,24... | collective-permute-start | bytes 221192 | tf_op jit(solution)/shard_map/ppermute | solution.py:245
  24.3 2.1 %collective-permute-done.11 = f32[144,128]{1,0:T(8,128)S(1)} collective-permute-done((f32[144,128]{1,0:T(8,128)S(1)}, f32[144,128]{1,0:T(8,128)S(1)}, u32[]{:S(2)}, u32[]{:S(2)}) %collective-permute-start.11) | collective-permute-done | bytes 73760 | tf_op jit(solution)/shard_map/ppermute | solution.py:245
  26.5 0.6 %collective-permute-start.12 = (f32[144,128]{1,0:T(8,128)S(1)}, f32[144,128]{1,0:T(8,128)S(1)}, u32[]{:S(2)}, u32[]{:S(2)}) collective-permute-start(f32[144,128]{1,0:T(8,128)S(1)} %add.46.refs_0_), channel_id=1, source_target_pairs={{0,1},{1,0},{2,3},{3,2},{4,5},{5,4},{6,7},{7,6},{8,9},{9,8},{10,11... | collective-permute-start | bytes 221192 | tf_op jit(solution)/shard_map/ppermute | solution.py:245
  27.1 0.9 %collective-permute-done.12.refs_1_ = f32[144,128]{1,0:T(8,128)S(1)} collective-permute-done((f32[144,128]{1,0:T(8,128)S(1)}, f32[144,128]{1,0:T(8,128)S(1)}, u32[]{:S(2)}, u32[]{:S(2)}) %collective-permute-start.12) | collective-permute-done | bytes 73760 | tf_op jit(solution)/shard_map/ppermute | solution.py:245
  28.0 1.7 %shard_map.62 = (bf16[8,8192]{1,0:T(8,128)(2,1)S(1)}, f32[8,256]{1,0:T(8,128)}, f32[8,8]{1,0:T(8,128)S(1)}, f32[1]{0:T(128)}) custom-call(f32[144,128]{1,0:T(8,128)S(1)} %add.46.refs_0_, f32[144,128]{1,0:T(8,128)S(1)} %collective-permute-done.12.refs_1_, bf16[8,8192]{1,0:T(8,128)(2,1)S(1)} %get-tuple-element.37.refs_2_, ...), custom_call_target="tpu_custom_call" | custom-call | tf_op jit(solution)/shard_map/pallas_call | solution.py:350
  30.4 0.0 copy-start.3
  30.4 0.0 copy-start.4
  30.4 0.6 %copy-done.3 = bf16[8,8192]{1,0:T(8,128)(2,1)} copy-done((bf16[8,8192]{1,0:T(8,128)(2,1)}, bf16[8,8192]{1,0:T(8,128)(2,1)S(1)}, u32[]{:S(2)}) %copy-start.3) | copy-done | bytes 131096
  31.1 0.0 copy-done.4
  (7 shorter events, 0.1 us)
Async XLA Ops:
  0.6 4.4 %copy-start = (s32[1,4,4]{2,1,0:T(4,128)S(1)}, s32[1,4,4]{2,1,0:T(4,128)}, u32[]{:S(2)}) copy-start(s32[1,4,4]{2,1,0:T(4,128)} %refs_0_.3) | copy-start | bytes 196
  0.6 1.8 %collective-permute-start.5 = (bf16[4,8,2048]{2,1,0:T(8,128)(2,1)}, bf16[4,8,2048]{2,1,0:T(8,128)(2,1)S(1)}, u32[]{:S(2)}, u32[]{:S(2)}) collective-permute-start(bf16[4,8,2048]{2,1,0:T(8,128)(2,1)} %bitcast.25), channel_id=1, source_target_pairs={{0,1},{1,0},{2,3},{3,2},{4,5},{5,4},{6,7},{7,6},{8,9},{9,8},{10,11... | collective-permute-start | bytes 393224 | tf_op jit(solution)/shard_map/ppermute | solution.py:245
  1.2 0.9 %copy-start.1 = (bf16[8,8192]{1,0:T(8,128)(2,1)S(1)}, bf16[8,8192]{1,0:T(8,128)(2,1)}, u32[]{:S(2)}) copy-start(bf16[8,8192]{1,0:T(8,128)(2,1)} %param.5) | copy-start | bytes 393220
  2.1 3.0 %copy-start.2 = (bf16[8192,256]{1,0:T(8,128)(2,1)S(1)}, bf16[8192,256]{1,0:T(8,128)(2,1)}, u32[]{:S(2)}) copy-start(bf16[8192,256]{1,0:T(8,128)(2,1)} %refs_2_.1) | copy-start | bytes 12582916
  2.4 4.8 %collective-permute-start.6 = (bf16[2,1,8,2048]{3,2,0,1:T(8,128)(2,1)S(1)}, bf16[2,1,8,2048]{3,2,0,1:T(8,128)(2,1)S(1)}, u32[]{:S(2)}, u32[]{:S(2)}) collective-permute-start(bf16[2,1,8,2048]{3,2,0,1:T(8,128)(2,1)S(1)} %bitcast.27), channel_id=1, source_target_pairs={{0,3},{1,2},{2,1},{3,0},{4,7},{5,6},{6,5},{7,4},{8,11},{9,10},{10,... | collective-permute-start | bytes 196616 | tf_op jit(solution)/shard_map/ppermute | solution.py:245
  7.7 1.3 %collective-permute-start.7 = (f32[144,128]{1,0:T(8,128)S(1)}, f32[144,128]{1,0:T(8,128)S(1)}, u32[]{:S(2)}, u32[]{:S(2)}) collective-permute-start(f32[144,128]{1,0:T(8,128)S(1)} %get-tuple-element.36), channel_id=1, source_target_pairs={{0,1},{1,0},{2,3},{3,2},{4,5},{5,4},{6,7},{7,6},{8,9},{9,8},{10,11... | collective-permute-start | bytes 221192 | tf_op jit(solution)/shard_map/ppermute | solution.py:245
  9.1 4.0 %collective-permute-start.8 = (f32[144,128]{1,0:T(8,128)S(1)}, f32[144,128]{1,0:T(8,128)S(1)}, u32[]{:S(2)}, u32[]{:S(2)}) collective-permute-start(f32[144,128]{1,0:T(8,128)S(1)} %add.42), channel_id=1, source_target_pairs={{0,3},{1,4},{2,7},{3,0},{4,1},{5,6},{6,5},{7,2},{8,13},{9,10},{10,... | collective-permute-start | bytes 221192 | tf_op jit(solution)/shard_map/ppermute | solution.py:245
  13.1 3.9 %collective-permute-start.9 = (f32[144,128]{1,0:T(8,128)S(1)}, f32[144,128]{1,0:T(8,128)S(1)}, u32[]{:S(2)}, u32[]{:S(2)}) collective-permute-start(f32[144,128]{1,0:T(8,128)S(1)} %add.43), channel_id=1, source_target_pairs={{0,5},{1,2},{2,1},{3,6},{4,7},{5,0},{6,3},{7,4},{8,11},{9,12},{10,... | collective-permute-start | bytes 221192 | tf_op jit(solution)/shard_map/ppermute | solution.py:245
  17.0 3.9 %collective-permute-start.10 = (f32[144,128]{1,0:T(8,128)S(1)}, f32[144,128]{1,0:T(8,128)S(1)}, u32[]{:S(2)}, u32[]{:S(2)}) collective-permute-start(f32[144,128]{1,0:T(8,128)S(1)} %add.44), channel_id=1, source_target_pairs={{0,9},{1,16},{2,19},{3,10},{4,21},{5,12},{6,15},{7,22},{8,25},{9,0... | collective-permute-start | bytes 221192 | tf_op jit(solution)/shard_map/ppermute | solution.py:245
  20.9 5.6 %collective-permute-start.11 = (f32[144,128]{1,0:T(8,128)S(1)}, f32[144,128]{1,0:T(8,128)S(1)}, u32[]{:S(2)}, u32[]{:S(2)}) collective-permute-start(f32[144,128]{1,0:T(8,128)S(1)} %add.45), channel_id=1, source_target_pairs={{0,17},{1,8},{2,11},{3,18},{4,13},{5,20},{6,23},{7,14},{8,1},{9,24... | collective-permute-start | bytes 221192 | tf_op jit(solution)/shard_map/ppermute | solution.py:245
  26.5 1.5 %collective-permute-start.12 = (f32[144,128]{1,0:T(8,128)S(1)}, f32[144,128]{1,0:T(8,128)S(1)}, u32[]{:S(2)}, u32[]{:S(2)}) collective-permute-start(f32[144,128]{1,0:T(8,128)S(1)} %add.46.refs_0_), channel_id=1, source_target_pairs={{0,1},{1,0},{2,3},{3,2},{4,5},{5,4},{6,7},{7,6},{8,9},{9,8},{10,11... | collective-permute-start | bytes 221192 | tf_op jit(solution)/shard_map/ppermute | solution.py:245
  30.4 0.7 %copy-start.3 = (bf16[8,8192]{1,0:T(8,128)(2,1)}, bf16[8,8192]{1,0:T(8,128)(2,1)S(1)}, u32[]{:S(2)}) copy-start(bf16[8,8192]{1,0:T(8,128)(2,1)S(1)} %get-tuple-element.46) | copy-start | bytes 393220
  30.4 0.6 %copy-start.4 = (f32[8,8]{1,0:T(8,128)}, f32[8,8]{1,0:T(8,128)S(1)}, u32[]{:S(2)}) copy-start(f32[8,8]{1,0:T(8,128)S(1)} %get-tuple-element.49) | copy-start | bytes 772

commit v6 on v5

--- a/solution.py
+++ b/solution.py
@@ -1,6 +1,7 @@
 import jax
 import jax.numpy as jnp
 from jax import lax
+from jax._src.lax.control_flow.conditionals import _switch_internal
 from jax.experimental import pallas as pl
 from jax.experimental.pallas import tpu as pltpu
 from jax.sharding import PartitionSpec as P
@@ -142,6 +143,26 @@
     send_ref[...] = out_ref[pl.ds(pl.multiple_of((1 - side) * share, SUBLANES), share)]
 
 
+def exact_dot(narrow, wide):
+    total = None
+    for _ in range(3):
+        part = wide.astype(jnp.bfloat16)
+        wide = wide - part.astype(F32)
+        term = jnp.dot(narrow, part, preferred_element_type=F32)
+        total = term if total is None else total + term
+    return total
+
+
+def left_exact_nt(wide, narrow):
+    parts = []
+    for _ in range(3):
+        parts.append(wide.astype(jnp.bfloat16))
+        wide = wide - parts[-1].astype(F32)
+    stacked = nt(jnp.concatenate(parts, axis=0), narrow)
+    count = wide.shape[0]
+    return stacked[0:count] + stacked[count : 2 * count] + stacked[2 * count :]
+
+
 def column(matrix, index):
     return matrix[:, index : index + 1]
 
@@ -158,7 +179,7 @@
         ratio = factors / factors[step : step + 1]
         both -= jnp.where(rows > step, ratio * both[step : step + 1], 0.0)
     pivots = jnp.sum(both[:, 0:count] * eye, axis=1, keepdims=True)
-    weak = jnp.sum(jnp.where(pivots >= GUARD * scale, 0.0, 1.0))
+    weak = jnp.sum(jnp.where(pivots >= GUARD * scale, 0.0, 1.0), axis=0, keepdims=True)
     both = both / jnp.sqrt(pivots)
     return jnp.where(row_id <= col_id, both[:, 0:count], 0.0), both[:, count:], weak
 
@@ -205,23 +226,24 @@
     edge = sums_ref[rank : rank + 1]
     spread = jnp.concatenate(
         [
-            jnp.dot(rounded[:, 0:half], left, precision=HIGH, preferred_element_type=F32),
-            jnp.dot(rounded, right, precision=HIGH, preferred_element_type=F32)
-            + rounded[:, half:] * edge,
+            exact_dot(narrow[:, 0:half], left),
+            exact_dot(narrow, right) + rounded[:, half:] * edge,
         ],
         axis=1,
     )
-    cross = nt(raw, rounded, HIGH)
-    quad = nt(spread, rounded, HIGH)
-    gram = (own - (cross + cross.T) + 0.5 * (quad + quad.T)) / cell_total
-    size = own + 2.0 * jnp.abs(cross) + jnp.abs(quad)
-    eye = lax.broadcasted_iota(jnp.int32, size.shape, 0) == lax.broadcasted_iota(
-        jnp.int32, size.shape, 1
-    )
-    scale = jnp.sum(jnp.where(eye, size, 0.0), axis=1, keepdims=True) / cell_total
+    pull = left_exact_nt(0.5 * spread - raw, narrow)
+    gram = (own + pull + pull.T) / cell_total
+    eye = lax.broadcasted_iota(jnp.int32, own.shape, 0) == lax.broadcasted_iota(
+        jnp.int32, own.shape, 1
+    )
+    scale = (
+        jnp.sum(jnp.where(eye, own, 0.0), axis=1, keepdims=True)
+        + 2.0 * jnp.abs(jnp.sum(raw * rounded, axis=1, keepdims=True))
+        + jnp.abs(jnp.sum(spread * rounded, axis=1, keepdims=True))
+    ) / cell_total
     upper_factor, inverse, weak = factor(gram, scale)
     upper_ref[...] = upper_factor
-    weak_ref[0] = weak
+    weak_ref[...] = (weak > 0.0).astype(jnp.int32)
     columns = [jnp.broadcast_to(column(inverse, row), (snapcount, LANES)) for row in range(snapcount)]
 
     stretch = cells // STRETCHES
@@ -340,10 +362,8 @@
 
     mine = mine + exchange(send, total, (1, 1))
     masks = flips(total)
-    swapped = list(masks)
-    for index in range(0, len(masks) - 1, 2):
-        swapped[index], swapped[index + 1] = masks[index + 1], masks[index]
-    for pair in zip(masks, swapped):
+    turn = len(masks) // 2
+    for pair in zip(masks, masks[turn:] + masks[:turn]):
         mine = mine + exchange(mine, total, pair)
     other = exchange(mine, total, (1, 1))
 
@@ -353,10 +373,10 @@
             like((snapcount, local_cells), jnp.bfloat16),
             like((snapcount, rank), F32),
             like((snapcount, snapcount), F32),
-            like((1,), F32),
+            like((1, 1), jnp.int32),
         ),
         [VMEM, VMEM, VMEM, VMEM],
-        (VMEM, VMEM, VMEM, SMEM),
+        (VMEM, VMEM, VMEM, VMEM),
         [
             pltpu.VMEM(sums_shape.shape, F32),
             pltpu.VMEM((snapcount, local_cells), F32),
@@ -370,7 +390,9 @@
         solved = jax.scipy.linalg.solve_triangular(lower, residual, lower=True)
         return solved.astype(jnp.bfloat16), lower.T
 
-    modes, r_factor = lax.cond(weak[0] > 0.0, direct, lambda ready: ready, (modes, r_factor))
+    modes, r_factor = _switch_internal(
+        weak.reshape(()), (lambda ready: ready, direct), ((modes, r_factor),), branches_platforms=None
+    )
     return modes, coeffs, r_factor
 
 

time: 31.2 us -> 30.7 us (0.984)
  between operations: 1.37 us -> 0.71 us
  loops' own time: 0.01 us -> 0.65 us
  starting transfers between devices: 13.3 us -> 12.8 us
    another operation x1, loops' own time: 0.01 us -> 0.65 us  [local(): _switch_internal(weak.reshape(()), (lambda ready: ready, direct), ((modes...]
    ppermute x8, starting transfers between devices: 13.3 us -> 12.8 us  [exchange(): lax.ppermute(value, AXES, [(index, partner(index)) for index in range(tot...]
where the time goes in v6:
time: 30.7 us; the launch traced here: 30.6 us
  starting transfers between devices  12.8 us (42%)
  waiting for transfers between devices  10.5 us (34%)
  Pallas kernels  4.28 us (14%)
  local copies, waits for them, and re-layouts  1.56 us (5%)
  between operations  0.71 us (2%)
  loops' own time  0.65 us (2%)
    ppermute x8, starting transfers between devices, exchange(): lax.ppermute(value, AXES, [(index, partner(index)) for index in range(tot...  12.8 us
    ppermute x8, waiting for transfers between devices, exchange(): lax.ppermute(value, AXES, [(index, partner(index)) for index in range(tot...  10.5 us
    pallas_call x1, Pallas kernels, local(): kernel_call(lambda *refs: gram_kernel(sources[:first], *refs), (sums_shap...  2.01 us
    pallas_call x1, Pallas kernels, local(): kernel_call(lambda *refs: finish_kernel(total, *refs), (like((snapcount,...  1.59 us
    unnamed x10, local copies, waits for them, and re-layouts  1.56 us
    another operation x1, loops' own time, local(): _switch_internal(weak.reshape(()), (lambda ready: ready, direct), ((modes...  0.65 us
  transfers between devices with their start and end apart: 8, of which 8 were waited for; matrix products, arithmetic and copies ran while one was open for 0% of the time, Pallas kernels for 7%

profile of v6, /device:TPU:0, one launch (start us, length us, event | category | flops | bytes accessed | tf_op | source)
XLA Modules:
  0.0 30.6 jit_solution(18325775012820428970)
XLA Ops:
  0.6 0.0 copy-start
  0.6 0.6 %collective-permute-start.5 = (bf16[4,8,2048]{2,1,0:T(8,128)(2,1)}, bf16[4,8,2048]{2,1,0:T(8,128)(2,1)S(1)}, u32[]{:S(2)}, u32[]{:S(2)}) collective-permute-start(bf16[4,8,2048]{2,1,0:T(8,128)(2,1)} %bitcast.25), channel_id=1, source_target_pairs={{0,1},{1,0},{2,3},{3,2},{4,5},{5,4},{6,7},{7,6},{8,9},{9,8},{10,11... | collective-permute-start | bytes 393224 | tf_op jit(solution)/shard_map/ppermute | solution.py:267
  1.2 0.0 copy-start.1
  1.2 0.9 %copy-done.1 = bf16[8,8192]{1,0:T(8,128)(2,1)S(1)} copy-done((bf16[8,8192]{1,0:T(8,128)(2,1)S(1)}, bf16[8,8192]{1,0:T(8,128)(2,1)}, u32[]{:S(2)}) %copy-start.1) | copy-done | bytes 131096
  2.1 0.0 copy-start.2
  2.1 0.2 shard_map.58.refs_0_
  2.3 0.1 collective-permute-done.5.refs_1_
  2.4 2.7 %collective-permute-start.6 = (bf16[2,1,8,2048]{3,2,0,1:T(8,128)(2,1)S(1)}, bf16[2,1,8,2048]{3,2,0,1:T(8,128)(2,1)S(1)}, u32[]{:S(2)}, u32[]{:S(2)}) collective-permute-start(bf16[2,1,8,2048]{3,2,0,1:T(8,128)(2,1)S(1)} %bitcast.27), channel_id=1, source_target_pairs={{0,3},{1,2},{2,1},{3,0},{4,7},{5,6},{6,5},{7,4},{8,11},{9,10},{10,... | collective-permute-start | bytes 196616 | tf_op jit(solution)/shard_map/ppermute | solution.py:267
  5.1 0.0 copy-done
  5.1 0.0 copy-done.2
  5.1 2.0 %shard_map.60 = (f32[288,128]{1,0:T(8,128)S(1)}, bf16[8192,256]{1,0:T(8,128)(2,1)S(1)}, bf16[8,8192]{1,0:T(8,128)(2,1)S(1)}) custom-call(s32[1,4,4]{2,1,0:T(4,128)S(1)} %copy-done, bf16[2,8,2048]{2,1,0:T(8,128)(2,1)S(1)} %bitcast.24, bf16[8192,256]{1,0:T(8,128)(2,1)S(1)} %copy-done.2), custom_call_target="tpu_custom_call" | custom-call | flops 1073741824 | bytes 4194304 | tf_op jit(solution)/shard_map/pallas_call | solution.py:345
  7.1 0.1 collective-permute-done.6
  7.2 0.5 %shard_map.61 = (f32[144,128]{1,0:T(8,128)S(1)}, f32[144,128]{1,0:T(8,128)S(1)}, bf16[8,8192]{1,0:T(8,128)(2,1)S(1)}) custom-call(s32[1,4,4]{2,1,0:T(4,128)S(1)} %copy-done, bf16[2,8,2048]{2,1,0:T(8,128)(2,1)S(1)} %bitcast.23, bf16[8192,256]{1,0:T(8,128)(2,1)S(1)} %get-tuple-element.32.refs_2_.refs_3_, ...), custom_call_target="tpu_custom_call", output_to_operand_aliasing={{2}: (4, {})} | custom-call | tf_op jit(solution)/shard_map/pallas_call | solution.py:354
  7.7 0.3 %collective-permute-start.7 = (f32[144,128]{1,0:T(8,128)S(1)}, f32[144,128]{1,0:T(8,128)S(1)}, u32[]{:S(2)}, u32[]{:S(2)}) collective-permute-start(f32[144,128]{1,0:T(8,128)S(1)} %get-tuple-element.36), channel_id=1, source_target_pairs={{0,1},{1,0},{2,3},{3,2},{4,5},{5,4},{6,7},{7,6},{8,9},{9,8},{10,11... | collective-permute-start | bytes 221192 | tf_op jit(solution)/shard_map/ppermute | solution.py:267
  8.1 1.0 %collective-permute-done.7 = f32[144,128]{1,0:T(8,128)S(1)} collective-permute-done((f32[144,128]{1,0:T(8,128)S(1)}, f32[144,128]{1,0:T(8,128)S(1)}, u32[]{:S(2)}, u32[]{:S(2)}) %collective-permute-start.7) | collective-permute-done | bytes 73760 | tf_op jit(solution)/shard_map/ppermute | solution.py:267
  9.1 2.0 %collective-permute-start.8 = (f32[144,128]{1,0:T(8,128)S(1)}, f32[144,128]{1,0:T(8,128)S(1)}, u32[]{:S(2)}, u32[]{:S(2)}) collective-permute-start(f32[144,128]{1,0:T(8,128)S(1)} %add.42), channel_id=1, source_target_pairs={{0,3},{1,8},{2,11},{3,0},{4,13},{5,6},{6,5},{7,14},{8,1},{9,10},{1... | collective-permute-start | bytes 221192 | tf_op jit(solution)/shard_map/ppermute | solution.py:267
  11.0 2.0 %collective-permute-done.8 = f32[144,128]{1,0:T(8,128)S(1)} collective-permute-done((f32[144,128]{1,0:T(8,128)S(1)}, f32[144,128]{1,0:T(8,128)S(1)}, u32[]{:S(2)}, u32[]{:S(2)}) %collective-permute-start.8) | collective-permute-done | bytes 73760 | tf_op jit(solution)/shard_map/ppermute | solution.py:267
  13.1 1.8 %collective-permute-start.9 = (f32[144,128]{1,0:T(8,128)S(1)}, f32[144,128]{1,0:T(8,128)S(1)}, u32[]{:S(2)}, u32[]{:S(2)}) collective-permute-start(f32[144,128]{1,0:T(8,128)S(1)} %add.43), channel_id=1, source_target_pairs={{0,5},{1,16},{2,19},{3,6},{4,21},{5,0},{6,3},{7,22},{8,25},{9,12},... | collective-permute-start | bytes 221192 | tf_op jit(solution)/shard_map/ppermute | solution.py:267
  14.9 2.0 %collective-permute-done.9 = f32[144,128]{1,0:T(8,128)S(1)} collective-permute-done((f32[144,128]{1,0:T(8,128)S(1)}, f32[144,128]{1,0:T(8,128)S(1)}, u32[]{:S(2)}, u32[]{:S(2)}) %collective-permute-start.9) | collective-permute-done | bytes 73760 | tf_op jit(solution)/shard_map/ppermute | solution.py:267
  17.0 2.2 %collective-permute-start.10 = (f32[144,128]{1,0:T(8,128)S(1)}, f32[144,128]{1,0:T(8,128)S(1)}, u32[]{:S(2)}, u32[]{:S(2)}) collective-permute-start(f32[144,128]{1,0:T(8,128)S(1)} %add.44), channel_id=1, source_target_pairs={{0,9},{1,2},{2,1},{3,10},{4,7},{5,12},{6,15},{7,4},{8,11},{9,0},{1... | collective-permute-start | bytes 221192 | tf_op jit(solution)/shard_map/ppermute | solution.py:267
  19.1 2.0 %collective-permute-done.10 = f32[144,128]{1,0:T(8,128)S(1)} collective-permute-done((f32[144,128]{1,0:T(8,128)S(1)}, f32[144,128]{1,0:T(8,128)S(1)}, u32[]{:S(2)}, u32[]{:S(2)}) %collective-permute-start.10) | collective-permute-done | bytes 73760 | tf_op jit(solution)/shard_map/ppermute | solution.py:267
  21.2 3.1 %collective-permute-start.11 = (f32[144,128]{1,0:T(8,128)S(1)}, f32[144,128]{1,0:T(8,128)S(1)}, u32[]{:S(2)}, u32[]{:S(2)}) collective-permute-start(f32[144,128]{1,0:T(8,128)S(1)} %add.45), channel_id=1, source_target_pairs={{0,17},{1,4},{2,7},{3,18},{4,1},{5,20},{6,23},{7,2},{8,13},{9,24},... | collective-permute-start | bytes 221192 | tf_op jit(solution)/shard_map/ppermute | solution.py:267
  24.3 2.0 %collective-permute-done.11 = f32[144,128]{1,0:T(8,128)S(1)} collective-permute-done((f32[144,128]{1,0:T(8,128)S(1)}, f32[144,128]{1,0:T(8,128)S(1)}, u32[]{:S(2)}, u32[]{:S(2)}) %collective-permute-start.11) | collective-permute-done | bytes 73760 | tf_op jit(solution)/shard_map/ppermute | solution.py:267
  26.3 0.2 collective-permute-start.12
  26.5 1.2 %collective-permute-done.12.refs_1_ = f32[144,128]{1,0:T(8,128)S(1)} collective-permute-done((f32[144,128]{1,0:T(8,128)S(1)}, f32[144,128]{1,0:T(8,128)S(1)}, u32[]{:S(2)}, u32[]{:S(2)}) %collective-permute-start.12) | collective-permute-done | bytes 73760 | tf_op jit(solution)/shard_map/ppermute | solution.py:267
  27.7 1.6 %shard_map.62 = (bf16[8,8192]{1,0:T(8,128)(2,1)S(1)}, f32[8,256]{1,0:T(8,128)}, f32[8,8]{1,0:T(8,128)S(1)}, s32[1,1]{1,0:T(1,128)}) custom-call(f32[144,128]{1,0:T(8,128)S(1)} %add.46.refs_0_, f32[144,128]{1,0:T(8,128)S(1)} %collective-permute-done.12.refs_1_, bf16[8,8192]{1,0:T(8,128)(2,1)S(1)} %get-tuple-element.37.refs_2_, ...), custom_call_target="tpu_custom_call" | custom-call | tf_op jit(solution)/shard_map/pallas_call | solution.py:370
  29.3 0.7 %conditional.1 = ((bf16[8,8192]{1,0:T(8,128)(2,1)S(1)}, f32[8,8]{1,0:T(8,128)S(1)})) conditional(s32[]{:T(128)} %bitcast.10, (bf16[8,8192]{1,0:T(8,128)(2,1)S(1)}, f32[8,8]{1,0:T(8,128)S(1)}) %tuple.15, (bf16[8,8192]{1,0:T(8,128)(2,1)S(1)}, f32[8,256]{1,0:T(8,128)}, bf16[8192,256]{1,0:T(8,128)(2,1)S(1)}) %tuple.27), branch_computations={%region_0.0_spmd, %region_1.0_spmd} | conditional | flops 46336968 | bytes 5263650 | solution.py:393
  29.9 0.0 copy-start.3
  29.9 0.0 copy-start.4
  29.9 0.6 %copy-done.3 = bf16[8,8192]{1,0:T(8,128)(2,1)} copy-done((bf16[8,8192]{1,0:T(8,128)(2,1)}, bf16[8,8192]{1,0:T(8,128)(2,1)S(1)}, u32[]{:S(2)}) %copy-start.3) | copy-done | bytes 131096
  30.6 0.0 copy-done.4
  (6 shorter events, 0.1 us)
Async XLA Ops:
  0.6 4.4 %copy-start = (s32[1,4,4]{2,1,0:T(4,128)S(1)}, s32[1,4,4]{2,1,0:T(4,128)}, u32[]{:S(2)}) copy-start(s32[1,4,4]{2,1,0:T(4,128)} %refs_0_.3) | copy-start | bytes 196
  0.6 1.8 %collective-permute-start.5 = (bf16[4,8,2048]{2,1,0:T(8,128)(2,1)}, bf16[4,8,2048]{2,1,0:T(8,128)(2,1)S(1)}, u32[]{:S(2)}, u32[]{:S(2)}) collective-permute-start(bf16[4,8,2048]{2,1,0:T(8,128)(2,1)} %bitcast.25), channel_id=1, source_target_pairs={{0,1},{1,0},{2,3},{3,2},{4,5},{5,4},{6,7},{7,6},{8,9},{9,8},{10,11... | collective-permute-start | bytes 393224 | tf_op jit(solution)/shard_map/ppermute | solution.py:267
  1.2 0.9 %copy-start.1 = (bf16[8,8192]{1,0:T(8,128)(2,1)S(1)}, bf16[8,8192]{1,0:T(8,128)(2,1)}, u32[]{:S(2)}) copy-start(bf16[8,8192]{1,0:T(8,128)(2,1)} %param.5) | copy-start | bytes 393220
  2.1 3.0 %copy-start.2 = (bf16[8192,256]{1,0:T(8,128)(2,1)S(1)}, bf16[8192,256]{1,0:T(8,128)(2,1)}, u32[]{:S(2)}) copy-start(bf16[8192,256]{1,0:T(8,128)(2,1)} %refs_2_.1) | copy-start | bytes 12582916
  2.4 4.8 %collective-permute-start.6 = (bf16[2,1,8,2048]{3,2,0,1:T(8,128)(2,1)S(1)}, bf16[2,1,8,2048]{3,2,0,1:T(8,128)(2,1)S(1)}, u32[]{:S(2)}, u32[]{:S(2)}) collective-permute-start(bf16[2,1,8,2048]{3,2,0,1:T(8,128)(2,1)S(1)} %bitcast.27), channel_id=1, source_target_pairs={{0,3},{1,2},{2,1},{3,0},{4,7},{5,6},{6,5},{7,4},{8,11},{9,10},{10,... | collective-permute-start | bytes 196616 | tf_op jit(solution)/shard_map/ppermute | solution.py:267
  7.7 1.3 %collective-permute-start.7 = (f32[144,128]{1,0:T(8,128)S(1)}, f32[144,128]{1,0:T(8,128)S(1)}, u32[]{:S(2)}, u32[]{:S(2)}) collective-permute-start(f32[144,128]{1,0:T(8,128)S(1)} %get-tuple-element.36), channel_id=1, source_target_pairs={{0,1},{1,0},{2,3},{3,2},{4,5},{5,4},{6,7},{7,6},{8,9},{9,8},{10,11... | collective-permute-start | bytes 221192 | tf_op jit(solution)/shard_map/ppermute | solution.py:267
  9.1 4.0 %collective-permute-start.8 = (f32[144,128]{1,0:T(8,128)S(1)}, f32[144,128]{1,0:T(8,128)S(1)}, u32[]{:S(2)}, u32[]{:S(2)}) collective-permute-start(f32[144,128]{1,0:T(8,128)S(1)} %add.42), channel_id=1, source_target_pairs={{0,3},{1,8},{2,11},{3,0},{4,13},{5,6},{6,5},{7,14},{8,1},{9,10},{1... | collective-permute-start | bytes 221192 | tf_op jit(solution)/shard_map/ppermute | solution.py:267
  13.1 3.9 %collective-permute-start.9 = (f32[144,128]{1,0:T(8,128)S(1)}, f32[144,128]{1,0:T(8,128)S(1)}, u32[]{:S(2)}, u32[]{:S(2)}) collective-permute-start(f32[144,128]{1,0:T(8,128)S(1)} %add.43), channel_id=1, source_target_pairs={{0,5},{1,16},{2,19},{3,6},{4,21},{5,0},{6,3},{7,22},{8,25},{9,12},... | collective-permute-start | bytes 221192 | tf_op jit(solution)/shard_map/ppermute | solution.py:267
  17.0 4.2 %collective-permute-start.10 = (f32[144,128]{1,0:T(8,128)S(1)}, f32[144,128]{1,0:T(8,128)S(1)}, u32[]{:S(2)}, u32[]{:S(2)}) collective-permute-start(f32[144,128]{1,0:T(8,128)S(1)} %add.44), channel_id=1, source_target_pairs={{0,9},{1,2},{2,1},{3,10},{4,7},{5,12},{6,15},{7,4},{8,11},{9,0},{1... | collective-permute-start | bytes 221192 | tf_op jit(solution)/shard_map/ppermute | solution.py:267
  21.2 5.2 %collective-permute-start.11 = (f32[144,128]{1,0:T(8,128)S(1)}, f32[144,128]{1,0:T(8,128)S(1)}, u32[]{:S(2)}, u32[]{:S(2)}) collective-permute-start(f32[144,128]{1,0:T(8,128)S(1)} %add.45), channel_id=1, source_target_pairs={{0,17},{1,4},{2,7},{3,18},{4,1},{5,20},{6,23},{7,2},{8,13},{9,24},... | collective-permute-start | bytes 221192 | tf_op jit(solution)/shard_map/ppermute | solution.py:267
  26.3 1.3 %collective-permute-start.12 = (f32[144,128]{1,0:T(8,128)S(1)}, f32[144,128]{1,0:T(8,128)S(1)}, u32[]{:S(2)}, u32[]{:S(2)}) collective-permute-start(f32[144,128]{1,0:T(8,128)S(1)} %add.46.refs_0_), channel_id=1, source_target_pairs={{0,1},{1,0},{2,3},{3,2},{4,5},{5,4},{6,7},{7,6},{8,9},{9,8},{10,11... | collective-permute-start | bytes 221192 | tf_op jit(solution)/shard_map/ppermute | solution.py:267
  29.9 0.7 %copy-start.3 = (bf16[8,8192]{1,0:T(8,128)(2,1)}, bf16[8,8192]{1,0:T(8,128)(2,1)S(1)}, u32[]{:S(2)}) copy-start(bf16[8,8192]{1,0:T(8,128)(2,1)S(1)} %get-tuple-element.46) | copy-start | bytes 393220
  29.9 0.6 %copy-start.4 = (f32[8,8]{1,0:T(8,128)}, f32[8,8]{1,0:T(8,128)S(1)}, u32[]{:S(2)}) copy-start(f32[8,8]{1,0:T(8,128)S(1)} %get-tuple-element.49) | copy-start | bytes 772

commit v7 on v6

--- a/solution.py
+++ b/solution.py
@@ -10,7 +10,7 @@
 HIGH = lax.Precision.HIGHEST
 LANES, SUBLANES = 128, 8
 GUARD = 1.0 / 64.0
-STRETCHES = 8
+STRETCHES = 4
 HBM = pl.BlockSpec(memory_space=pltpu.HBM)
 ANY = pl.BlockSpec(memory_space=pl.ANY)
 DMA = pltpu.SemaphoreType.DMA
@@ -131,6 +131,7 @@
     rank = basis_ref.shape[1]
     half = rank // 2
     share = mine_ref.shape[0]
+    placed_ref[...] = placed_in[...]
     raw, own = block_sums(sources, order_ref, far_ref, basis_ref, placed_ref)
     out_ref[...] = sums_ref[...]
     at = rank + SUBLANES
@@ -169,19 +170,27 @@
 
 def factor(gram, scale):
     count = gram.shape[0]
-    row_id = lax.broadcasted_iota(jnp.int32, (count, count), 0)
-    col_id = lax.broadcasted_iota(jnp.int32, (count, count), 1)
-    eye = (row_id == col_id).astype(F32)
-    both = jnp.concatenate([gram, eye], axis=1)
-    rows = lax.broadcasted_iota(jnp.int32, both.shape, 0)
+    shape = (count, LANES)
+    rows = lax.broadcasted_iota(jnp.int32, shape, 0)
+    lanes = lax.broadcasted_iota(jnp.int32, shape, 1)
+    columns = [jnp.broadcast_to(column(gram, index), shape) for index in range(count)]
+    inverse = [(rows == index).astype(F32) for index in range(count)]
     for step in range(count - 1):
-        factors = column(both, step)
-        ratio = factors / factors[step : step + 1]
-        both -= jnp.where(rows > step, ratio * both[step : step + 1], 0.0)
-    pivots = jnp.sum(both[:, 0:count] * eye, axis=1, keepdims=True)
-    weak = jnp.sum(jnp.where(pivots >= GUARD * scale, 0.0, 1.0), axis=0, keepdims=True)
-    both = both / jnp.sqrt(pivots)
-    return jnp.where(row_id <= col_id, both[:, 0:count], 0.0), both[:, count:], weak
+        ratio = columns[step] * (1.0 / columns[step][step : step + 1])
+        ratio = jnp.where(rows > step, ratio, 0.0)
+        for index in range(step + 1, count):
+            columns[index] -= ratio * columns[index][step : step + 1]
+        for index in range(step + 1):
+            inverse[index] -= ratio * inverse[index][step : step + 1]
+    pivots = jnp.zeros(shape, F32)
+    upper = jnp.zeros(shape, F32)
+    for index in range(count):
+        pivots = jnp.where(rows == index, columns[index], pivots)
+        upper = jnp.where((lanes == index) & (rows <= index), columns[index], upper)
+    sound = pivots[:, 0:1] >= GUARD * scale
+    weak = jnp.sum(jnp.where(sound, 0.0, 1.0), axis=0, keepdims=True)
+    root = 1.0 / jnp.sqrt(pivots)
+    return (upper * root)[:, 0:count], [part * root for part in inverse], weak
 
 
 def finish_kernel(
@@ -241,23 +250,21 @@
         + 2.0 * jnp.abs(jnp.sum(raw * rounded, axis=1, keepdims=True))
         + jnp.abs(jnp.sum(spread * rounded, axis=1, keepdims=True))
     ) / cell_total
-    upper_factor, inverse, weak = factor(gram, scale)
+    upper_factor, columns, weak = factor(gram, scale)
     upper_ref[...] = upper_factor
     weak_ref[...] = (weak > 0.0).astype(jnp.int32)
-    columns = [jnp.broadcast_to(column(inverse, row), (snapcount, LANES)) for row in range(snapcount)]
 
     stretch = cells // STRETCHES
-    for index in range(STRETCHES):
-        low = index * stretch
+    for low in range(0, cells, stretch):
         fitted = nt(narrow, basis_ref[low : low + stretch])
         resid_ref[:, low : low + stretch] = (
             placed_ref[:, low : low + stretch].astype(F32) - fitted
         )
-        for lane in range(low, low + stretch, LANES):
-            modes = columns[0] * resid_ref[0:1, lane : lane + LANES]
-            for row in range(1, snapcount):
-                modes += columns[row] * resid_ref[row : row + 1, lane : lane + LANES]
-            modes_ref[:, lane : lane + LANES] = modes.astype(jnp.bfloat16)
+    for lane in range(0, cells, LANES):
+        modes = columns[0] * resid_ref[0:1, lane : lane + LANES]
+        for row in range(1, snapcount):
+            modes += columns[row] * resid_ref[row : row + 1, lane : lane + LANES]
+        modes_ref[:, lane : lane + LANES] = modes.astype(jnp.bfloat16)
 
 
 def exchange(value, total, masks):
@@ -357,7 +364,6 @@
         [VMEM, VMEM, VMEM, VMEM, VMEM],
         (VMEM, VMEM, VMEM),
         [pltpu.VMEM(sums_shape.shape, F32)],
-        input_output_aliases={4: 2},
     )(box_order, far, near, sums, placed)
 
     mine = mine + exchange(send, total, (1, 1))

time: 30.7 us -> 30.7 us (level)
  no operation moved by 1% of the time
where the time goes in v7:
time: 30.7 us; the launch traced here: 30.5 us
  starting transfers between devices  12.8 us (42%)
  waiting for transfers between devices  10.5 us (34%)
  Pallas kernels  4.18 us (14%)
  local copies, waits for them, and re-layouts  1.56 us (5%)
  between operations  0.72 us (2%)
  loops' own time  0.66 us (2%)
    ppermute x8, starting transfers between devices, exchange(): lax.ppermute(value, AXES, [(index, partner(index)) for index in range(tot...  12.8 us
    ppermute x8, waiting for transfers between devices, exchange(): lax.ppermute(value, AXES, [(index, partner(index)) for index in range(tot...  10.5 us
    pallas_call x1, Pallas kernels, local(): kernel_call(lambda *refs: gram_kernel(sources[:first], *refs), (sums_shap...  2.01 us
    unnamed x10, local copies, waits for them, and re-layouts  1.56 us
    pallas_call x1, Pallas kernels, local(): kernel_call(lambda *refs: finish_kernel(total, *refs), (like((snapcount,...  1.48 us
    another operation x1, loops' own time, local(): _switch_internal(weak.reshape(()), (lambda ready: ready, direct), ((modes...  0.66 us
  transfers between devices with their start and end apart: 8, of which 8 were waited for; matrix products, arithmetic and copies ran while one was open for 0% of the time, Pallas kernels for 7%

profile of v7, /device:TPU:0, one launch (start us, length us, event | category | flops | bytes accessed | tf_op | source)
XLA Modules:
  0.0 30.5 jit_solution(6553447080893259189)
XLA Ops:
  0.6 0.0 copy-start
  0.6 0.6 %collective-permute-start.5 = (bf16[4,8,2048]{2,1,0:T(8,128)(2,1)}, bf16[4,8,2048]{2,1,0:T(8,128)(2,1)S(1)}, u32[]{:S(2)}, u32[]{:S(2)}) collective-permute-start(bf16[4,8,2048]{2,1,0:T(8,128)(2,1)} %bitcast.25), channel_id=1, source_target_pairs={{0,1},{1,0},{2,3},{3,2},{4,5},{5,4},{6,7},{7,6},{8,9},{9,8},{10,11... | collective-permute-start | bytes 393224 | tf_op jit(solution)/shard_map/ppermute | solution.py:274
  1.2 0.0 copy-start.1
  1.2 0.9 %copy-done.1 = bf16[8,8192]{1,0:T(8,128)(2,1)S(1)} copy-done((bf16[8,8192]{1,0:T(8,128)(2,1)S(1)}, bf16[8,8192]{1,0:T(8,128)(2,1)}, u32[]{:S(2)}) %copy-start.1) | copy-done | bytes 131096
  2.1 0.0 copy-start.2
  2.1 0.2 shard_map.58.refs_0_
  2.3 0.1 collective-permute-done.5.refs_1_
  2.4 2.7 %collective-permute-start.6 = (bf16[2,1,8,2048]{3,2,0,1:T(8,128)(2,1)S(1)}, bf16[2,1,8,2048]{3,2,0,1:T(8,128)(2,1)S(1)}, u32[]{:S(2)}, u32[]{:S(2)}) collective-permute-start(bf16[2,1,8,2048]{3,2,0,1:T(8,128)(2,1)S(1)} %bitcast.27), channel_id=1, source_target_pairs={{0,3},{1,2},{2,1},{3,0},{4,7},{5,6},{6,5},{7,4},{8,11},{9,10},{10,... | collective-permute-start | bytes 196616 | tf_op jit(solution)/shard_map/ppermute | solution.py:274
  5.1 0.0 copy-done
  5.1 0.0 copy-done.2
  5.1 2.0 %shard_map.60 = (f32[288,128]{1,0:T(8,128)S(1)}, bf16[8192,256]{1,0:T(8,128)(2,1)S(1)}, bf16[8,8192]{1,0:T(8,128)(2,1)S(1)}) custom-call(s32[1,4,4]{2,1,0:T(4,128)S(1)} %copy-done, bf16[2,8,2048]{2,1,0:T(8,128)(2,1)S(1)} %bitcast.24, bf16[8192,256]{1,0:T(8,128)(2,1)S(1)} %copy-done.2), custom_call_target="tpu_custom_call" | custom-call | flops 1073741824 | bytes 4194304 | tf_op jit(solution)/shard_map/pallas_call | solution.py:352
  7.1 0.1 collective-permute-done.6
  7.2 0.5 %shard_map.61 = (f32[144,128]{1,0:T(8,128)S(1)}, f32[144,128]{1,0:T(8,128)S(1)}, bf16[8,8192]{1,0:T(8,128)(2,1)S(1)}) custom-call(s32[1,4,4]{2,1,0:T(4,128)S(1)} %copy-done, bf16[2,8,2048]{2,1,0:T(8,128)(2,1)S(1)} %bitcast.23, bf16[8192,256]{1,0:T(8,128)(2,1)S(1)} %get-tuple-element.32.refs_2_.refs_3_, f32[288,128]{1,0:T(8,128)S(1)} %get-tuple-element.33.refs_3_, ...), custom_call_target="tpu_custom_call" | custom-call | tf_op jit(solution)/shard_map/pallas_call | solution.py:361
  7.8 0.3 %collective-permute-start.7 = (f32[144,128]{1,0:T(8,128)S(1)}, f32[144,128]{1,0:T(8,128)S(1)}, u32[]{:S(2)}, u32[]{:S(2)}) collective-permute-start(f32[144,128]{1,0:T(8,128)S(1)} %get-tuple-element.36), channel_id=1, source_target_pairs={{0,1},{1,0},{2,3},{3,2},{4,5},{5,4},{6,7},{7,6},{8,9},{9,8},{10,11... | collective-permute-start | bytes 221192 | tf_op jit(solution)/shard_map/ppermute | solution.py:274
  8.1 1.0 %collective-permute-done.7 = f32[144,128]{1,0:T(8,128)S(1)} collective-permute-done((f32[144,128]{1,0:T(8,128)S(1)}, f32[144,128]{1,0:T(8,128)S(1)}, u32[]{:S(2)}, u32[]{:S(2)}) %collective-permute-start.7) | collective-permute-done | bytes 73760 | tf_op jit(solution)/shard_map/ppermute | solution.py:274
  9.1 2.0 %collective-permute-start.8 = (f32[144,128]{1,0:T(8,128)S(1)}, f32[144,128]{1,0:T(8,128)S(1)}, u32[]{:S(2)}, u32[]{:S(2)}) collective-permute-start(f32[144,128]{1,0:T(8,128)S(1)} %add.42), channel_id=1, source_target_pairs={{0,3},{1,8},{2,11},{3,0},{4,13},{5,6},{6,5},{7,14},{8,1},{9,10},{1... | collective-permute-start | bytes 221192 | tf_op jit(solution)/shard_map/ppermute | solution.py:274
  11.0 2.0 %collective-permute-done.8 = f32[144,128]{1,0:T(8,128)S(1)} collective-permute-done((f32[144,128]{1,0:T(8,128)S(1)}, f32[144,128]{1,0:T(8,128)S(1)}, u32[]{:S(2)}, u32[]{:S(2)}) %collective-permute-start.8) | collective-permute-done | bytes 73760 | tf_op jit(solution)/shard_map/ppermute | solution.py:274
  13.1 1.8 %collective-permute-start.9 = (f32[144,128]{1,0:T(8,128)S(1)}, f32[144,128]{1,0:T(8,128)S(1)}, u32[]{:S(2)}, u32[]{:S(2)}) collective-permute-start(f32[144,128]{1,0:T(8,128)S(1)} %add.43), channel_id=1, source_target_pairs={{0,5},{1,16},{2,19},{3,6},{4,21},{5,0},{6,3},{7,22},{8,25},{9,12},... | collective-permute-start | bytes 221192 | tf_op jit(solution)/shard_map/ppermute | solution.py:274
  14.9 2.0 %collective-permute-done.9 = f32[144,128]{1,0:T(8,128)S(1)} collective-permute-done((f32[144,128]{1,0:T(8,128)S(1)}, f32[144,128]{1,0:T(8,128)S(1)}, u32[]{:S(2)}, u32[]{:S(2)}) %collective-permute-start.9) | collective-permute-done | bytes 73760 | tf_op jit(solution)/shard_map/ppermute | solution.py:274
  17.0 2.2 %collective-permute-start.10 = (f32[144,128]{1,0:T(8,128)S(1)}, f32[144,128]{1,0:T(8,128)S(1)}, u32[]{:S(2)}, u32[]{:S(2)}) collective-permute-start(f32[144,128]{1,0:T(8,128)S(1)} %add.44), channel_id=1, source_target_pairs={{0,9},{1,2},{2,1},{3,10},{4,7},{5,12},{6,15},{7,4},{8,11},{9,0},{1... | collective-permute-start | bytes 221192 | tf_op jit(solution)/shard_map/ppermute | solution.py:274
  19.1 2.0 %collective-permute-done.10 = f32[144,128]{1,0:T(8,128)S(1)} collective-permute-done((f32[144,128]{1,0:T(8,128)S(1)}, f32[144,128]{1,0:T(8,128)S(1)}, u32[]{:S(2)}, u32[]{:S(2)}) %collective-permute-start.10) | collective-permute-done | bytes 73760 | tf_op jit(solution)/shard_map/ppermute | solution.py:274
  21.2 3.1 %collective-permute-start.11 = (f32[144,128]{1,0:T(8,128)S(1)}, f32[144,128]{1,0:T(8,128)S(1)}, u32[]{:S(2)}, u32[]{:S(2)}) collective-permute-start(f32[144,128]{1,0:T(8,128)S(1)} %add.45), channel_id=1, source_target_pairs={{0,17},{1,4},{2,7},{3,18},{4,1},{5,20},{6,23},{7,2},{8,13},{9,24},... | collective-permute-start | bytes 221192 | tf_op jit(solution)/shard_map/ppermute | solution.py:274
  24.3 2.0 %collective-permute-done.11 = f32[144,128]{1,0:T(8,128)S(1)} collective-permute-done((f32[144,128]{1,0:T(8,128)S(1)}, f32[144,128]{1,0:T(8,128)S(1)}, u32[]{:S(2)}, u32[]{:S(2)}) %collective-permute-start.11) | collective-permute-done | bytes 73760 | tf_op jit(solution)/shard_map/ppermute | solution.py:274
  26.3 0.2 collective-permute-start.12
  26.5 1.2 %collective-permute-done.12.refs_1_ = f32[144,128]{1,0:T(8,128)S(1)} collective-permute-done((f32[144,128]{1,0:T(8,128)S(1)}, f32[144,128]{1,0:T(8,128)S(1)}, u32[]{:S(2)}, u32[]{:S(2)}) %collective-permute-start.12) | collective-permute-done | bytes 73760 | tf_op jit(solution)/shard_map/ppermute | solution.py:274
  27.7 1.5 %shard_map.62 = (bf16[8,8192]{1,0:T(8,128)(2,1)S(1)}, f32[8,256]{1,0:T(8,128)}, f32[8,8]{1,0:T(8,128)S(1)}, s32[1,1]{1,0:T(1,128)}) custom-call(f32[144,128]{1,0:T(8,128)S(1)} %add.46.refs_0_, f32[144,128]{1,0:T(8,128)S(1)} %collective-permute-done.12.refs_1_, bf16[8,8192]{1,0:T(8,128)(2,1)S(1)} %get-tuple-element.37.refs_2_, ...), custom_call_target="tpu_custom_call" | custom-call | tf_op jit(solution)/shard_map/pallas_call | solution.py:376
  29.2 0.7 %conditional.1 = ((bf16[8,8192]{1,0:T(8,128)(2,1)S(1)}, f32[8,8]{1,0:T(8,128)S(1)})) conditional(s32[]{:T(128)} %bitcast.10, (bf16[8,8192]{1,0:T(8,128)(2,1)S(1)}, f32[8,8]{1,0:T(8,128)S(1)}) %tuple.15, (bf16[8,8192]{1,0:T(8,128)(2,1)S(1)}, f32[8,256]{1,0:T(8,128)}, bf16[8192,256]{1,0:T(8,128)(2,1)S(1)}) %tuple.27), branch_computations={%region_0.0_spmd, %region_1.0_spmd} | conditional | flops 46336968 | bytes 5263650 | solution.py:399
  29.8 0.0 copy-start.3
  29.8 0.0 copy-start.4
  29.9 0.6 %copy-done.3 = bf16[8,8192]{1,0:T(8,128)(2,1)} copy-done((bf16[8,8192]{1,0:T(8,128)(2,1)}, bf16[8,8192]{1,0:T(8,128)(2,1)S(1)}, u32[]{:S(2)}) %copy-start.3) | copy-done | bytes 131096
  30.5 0.0 copy-done.4
  (6 shorter events, 0.1 us)
Async XLA Ops:
  0.6 4.4 %copy-start = (s32[1,4,4]{2,1,0:T(4,128)S(1)}, s32[1,4,4]{2,1,0:T(4,128)}, u32[]{:S(2)}) copy-start(s32[1,4,4]{2,1,0:T(4,128)} %refs_0_.3) | copy-start | bytes 196
  0.6 1.8 %collective-permute-start.5 = (bf16[4,8,2048]{2,1,0:T(8,128)(2,1)}, bf16[4,8,2048]{2,1,0:T(8,128)(2,1)S(1)}, u32[]{:S(2)}, u32[]{:S(2)}) collective-permute-start(bf16[4,8,2048]{2,1,0:T(8,128)(2,1)} %bitcast.25), channel_id=1, source_target_pairs={{0,1},{1,0},{2,3},{3,2},{4,5},{5,4},{6,7},{7,6},{8,9},{9,8},{10,11... | collective-permute-start | bytes 393224 | tf_op jit(solution)/shard_map/ppermute | solution.py:274
  1.2 0.9 %copy-start.1 = (bf16[8,8192]{1,0:T(8,128)(2,1)S(1)}, bf16[8,8192]{1,0:T(8,128)(2,1)}, u32[]{:S(2)}) copy-start(bf16[8,8192]{1,0:T(8,128)(2,1)} %param.5) | copy-start | bytes 393220
  2.1 3.0 %copy-start.2 = (bf16[8192,256]{1,0:T(8,128)(2,1)S(1)}, bf16[8192,256]{1,0:T(8,128)(2,1)}, u32[]{:S(2)}) copy-start(bf16[8192,256]{1,0:T(8,128)(2,1)} %refs_2_.1) | copy-start | bytes 12582916
  2.4 4.8 %collective-permute-start.6 = (bf16[2,1,8,2048]{3,2,0,1:T(8,128)(2,1)S(1)}, bf16[2,1,8,2048]{3,2,0,1:T(8,128)(2,1)S(1)}, u32[]{:S(2)}, u32[]{:S(2)}) collective-permute-start(bf16[2,1,8,2048]{3,2,0,1:T(8,128)(2,1)S(1)} %bitcast.27), channel_id=1, source_target_pairs={{0,3},{1,2},{2,1},{3,0},{4,7},{5,6},{6,5},{7,4},{8,11},{9,10},{10,... | collective-permute-start | bytes 196616 | tf_op jit(solution)/shard_map/ppermute | solution.py:274
  7.8 1.3 %collective-permute-start.7 = (f32[144,128]{1,0:T(8,128)S(1)}, f32[144,128]{1,0:T(8,128)S(1)}, u32[]{:S(2)}, u32[]{:S(2)}) collective-permute-start(f32[144,128]{1,0:T(8,128)S(1)} %get-tuple-element.36), channel_id=1, source_target_pairs={{0,1},{1,0},{2,3},{3,2},{4,5},{5,4},{6,7},{7,6},{8,9},{9,8},{10,11... | collective-permute-start | bytes 221192 | tf_op jit(solution)/shard_map/ppermute | solution.py:274
  9.1 4.0 %collective-permute-start.8 = (f32[144,128]{1,0:T(8,128)S(1)}, f32[144,128]{1,0:T(8,128)S(1)}, u32[]{:S(2)}, u32[]{:S(2)}) collective-permute-start(f32[144,128]{1,0:T(8,128)S(1)} %add.42), channel_id=1, source_target_pairs={{0,3},{1,8},{2,11},{3,0},{4,13},{5,6},{6,5},{7,14},{8,1},{9,10},{1... | collective-permute-start | bytes 221192 | tf_op jit(solution)/shard_map/ppermute | solution.py:274
  13.1 3.9 %collective-permute-start.9 = (f32[144,128]{1,0:T(8,128)S(1)}, f32[144,128]{1,0:T(8,128)S(1)}, u32[]{:S(2)}, u32[]{:S(2)}) collective-permute-start(f32[144,128]{1,0:T(8,128)S(1)} %add.43), channel_id=1, source_target_pairs={{0,5},{1,16},{2,19},{3,6},{4,21},{5,0},{6,3},{7,22},{8,25},{9,12},... | collective-permute-start | bytes 221192 | tf_op jit(solution)/shard_map/ppermute | solution.py:274
  17.0 4.2 %collective-permute-start.10 = (f32[144,128]{1,0:T(8,128)S(1)}, f32[144,128]{1,0:T(8,128)S(1)}, u32[]{:S(2)}, u32[]{:S(2)}) collective-permute-start(f32[144,128]{1,0:T(8,128)S(1)} %add.44), channel_id=1, source_target_pairs={{0,9},{1,2},{2,1},{3,10},{4,7},{5,12},{6,15},{7,4},{8,11},{9,0},{1... | collective-permute-start | bytes 221192 | tf_op jit(solution)/shard_map/ppermute | solution.py:274
  21.2 5.2 %collective-permute-start.11 = (f32[144,128]{1,0:T(8,128)S(1)}, f32[144,128]{1,0:T(8,128)S(1)}, u32[]{:S(2)}, u32[]{:S(2)}) collective-permute-start(f32[144,128]{1,0:T(8,128)S(1)} %add.45), channel_id=1, source_target_pairs={{0,17},{1,4},{2,7},{3,18},{4,1},{5,20},{6,23},{7,2},{8,13},{9,24},... | collective-permute-start | bytes 221192 | tf_op jit(solution)/shard_map/ppermute | solution.py:274
  26.3 1.3 %collective-permute-start.12 = (f32[144,128]{1,0:T(8,128)S(1)}, f32[144,128]{1,0:T(8,128)S(1)}, u32[]{:S(2)}, u32[]{:S(2)}) collective-permute-start(f32[144,128]{1,0:T(8,128)S(1)} %add.46.refs_0_), channel_id=1, source_target_pairs={{0,1},{1,0},{2,3},{3,2},{4,5},{5,4},{6,7},{7,6},{8,9},{9,8},{10,11... | collective-permute-start | bytes 221192 | tf_op jit(solution)/shard_map/ppermute | solution.py:274
  29.8 0.7 %copy-start.3 = (bf16[8,8192]{1,0:T(8,128)(2,1)}, bf16[8,8192]{1,0:T(8,128)(2,1)S(1)}, u32[]{:S(2)}) copy-start(bf16[8,8192]{1,0:T(8,128)(2,1)S(1)} %get-tuple-element.46) | copy-start | bytes 393220
  29.8 0.6 %copy-start.4 = (f32[8,8]{1,0:T(8,128)}, f32[8,8]{1,0:T(8,128)S(1)}, u32[]{:S(2)}) copy-start(f32[8,8]{1,0:T(8,128)S(1)} %get-tuple-element.49) | copy-start | bytes 772

commit v8 on v7

--- a/solution.py
+++ b/solution.py
@@ -125,7 +125,6 @@
     mine_ref,
     send_ref,
     placed_ref,
-    out_ref,
 ):
     snapcount = far_ref.shape[1]
     rank = basis_ref.shape[1]
@@ -133,15 +132,18 @@
     share = mine_ref.shape[0]
     placed_ref[...] = placed_in[...]
     raw, own = block_sums(sources, order_ref, far_ref, basis_ref, placed_ref)
-    out_ref[...] = sums_ref[...]
-    at = rank + SUBLANES
+    side = parity(device_index(), total)
+    mine_ref[...] = sums_ref[pl.ds(pl.multiple_of(side * share, SUBLANES), share)]
+    send_ref[...] = sums_ref[pl.ds(pl.multiple_of((1 - side) * share, SUBLANES), share)]
+    keeps = side == 1
+    at = rank + SUBLANES - share
     for part in range(rank // half):
-        out_ref[at : at + snapcount] += raw[:, part * half : (part + 1) * half]
+        term = raw[:, part * half : (part + 1) * half]
+        mine_ref[at : at + snapcount] += jnp.where(keeps, term, 0.0)
+        send_ref[at : at + snapcount] += jnp.where(keeps, 0.0, term)
         at += snapcount
-    out_ref[at : at + snapcount, 0:snapcount] += own
-    side = parity(device_index(), total)
-    mine_ref[...] = out_ref[pl.ds(pl.multiple_of(side * share, SUBLANES), share)]
-    send_ref[...] = out_ref[pl.ds(pl.multiple_of((1 - side) * share, SUBLANES), share)]
+    mine_ref[at : at + snapcount, 0:snapcount] += jnp.where(keeps, own, 0.0)
+    send_ref[at : at + snapcount, 0:snapcount] += jnp.where(keeps, 0.0, own)
 
 
 def exact_dot(narrow, wide):
@@ -363,7 +365,6 @@
         (part, part, placed_shape),
         [VMEM, VMEM, VMEM, VMEM, VMEM],
         (VMEM, VMEM, VMEM),
-        [pltpu.VMEM(sums_shape.shape, F32)],
     )(box_order, far, near, sums, placed)
 
     mine = mine + exchange(send, total, (1, 1))

time: 30.7 us -> 30.7 us (level)
  no operation moved by 1% of the time
where the time goes in v8:
time: 30.7 us; the launch traced here: 30.5 us
  starting transfers between devices  12.8 us (42%)
  waiting for transfers between devices  10.5 us (34%)
  Pallas kernels  4.15 us (14%)
  local copies, waits for them, and re-layouts  1.56 us (5%)
  between operations  0.72 us (2%)
  loops' own time  0.66 us (2%)
    ppermute x8, starting transfers between devices, exchange(): lax.ppermute(value, AXES, [(index, partner(index)) for index in range(tot...  12.8 us
    ppermute x8, waiting for transfers between devices, exchange(): lax.ppermute(value, AXES, [(index, partner(index)) for index in range(tot...  10.5 us
    pallas_call x1, Pallas kernels, local(): kernel_call(lambda *refs: gram_kernel(sources[:first], *refs), (sums_shap...  2.01 us
    unnamed x10, local copies, waits for them, and re-layouts  1.56 us
    pallas_call x1, Pallas kernels, local(): kernel_call(lambda *refs: finish_kernel(total, *refs), (like((snapcount,...  1.48 us
    another operation x1, loops' own time, local(): _switch_internal(weak.reshape(()), (lambda ready: ready, direct), ((modes...  0.66 us
  transfers between devices with their start and end apart: 8, of which 8 were waited for; matrix products, arithmetic and copies ran while one was open for 0% of the time, Pallas kernels for 7%

profile of v8, /device:TPU:0, one launch (start us, length us, event | category | flops | bytes accessed | tf_op | source)
XLA Modules:
  0.0 30.5 jit_solution(17937612289996574702)
XLA Ops:
  0.6 0.0 copy-start
  0.6 0.6 %collective-permute-start.5 = (bf16[4,8,2048]{2,1,0:T(8,128)(2,1)}, bf16[4,8,2048]{2,1,0:T(8,128)(2,1)S(1)}, u32[]{:S(2)}, u32[]{:S(2)}) collective-permute-start(bf16[4,8,2048]{2,1,0:T(8,128)(2,1)} %bitcast.25), channel_id=1, source_target_pairs={{0,1},{1,0},{2,3},{3,2},{4,5},{5,4},{6,7},{7,6},{8,9},{9,8},{10,11... | collective-permute-start | bytes 393224 | tf_op jit(solution)/shard_map/ppermute | solution.py:276
  1.2 0.0 copy-start.1
  1.2 0.9 %copy-done.1 = bf16[8,8192]{1,0:T(8,128)(2,1)S(1)} copy-done((bf16[8,8192]{1,0:T(8,128)(2,1)S(1)}, bf16[8,8192]{1,0:T(8,128)(2,1)}, u32[]{:S(2)}) %copy-start.1) | copy-done | bytes 131096
  2.1 0.0 copy-start.2
  2.1 0.2 shard_map.58.refs_0_
  2.3 0.1 collective-permute-done.5.refs_1_
  2.4 2.7 %collective-permute-start.6 = (bf16[2,1,8,2048]{3,2,0,1:T(8,128)(2,1)S(1)}, bf16[2,1,8,2048]{3,2,0,1:T(8,128)(2,1)S(1)}, u32[]{:S(2)}, u32[]{:S(2)}) collective-permute-start(bf16[2,1,8,2048]{3,2,0,1:T(8,128)(2,1)S(1)} %bitcast.27), channel_id=1, source_target_pairs={{0,3},{1,2},{2,1},{3,0},{4,7},{5,6},{6,5},{7,4},{8,11},{9,10},{10,... | collective-permute-start | bytes 196616 | tf_op jit(solution)/shard_map/ppermute | solution.py:276
  5.1 0.0 copy-done
  5.1 0.0 copy-done.2
  5.1 2.0 %shard_map.60 = (f32[288,128]{1,0:T(8,128)S(1)}, bf16[8192,256]{1,0:T(8,128)(2,1)S(1)}, bf16[8,8192]{1,0:T(8,128)(2,1)S(1)}) custom-call(s32[1,4,4]{2,1,0:T(4,128)S(1)} %copy-done, bf16[2,8,2048]{2,1,0:T(8,128)(2,1)S(1)} %bitcast.24, bf16[8192,256]{1,0:T(8,128)(2,1)S(1)} %copy-done.2), custom_call_target="tpu_custom_call" | custom-call | flops 1073741824 | bytes 4194304 | tf_op jit(solution)/shard_map/pallas_call | solution.py:354
  7.1 0.1 collective-permute-done.6
  7.2 0.5 %shard_map.61 = (f32[144,128]{1,0:T(8,128)S(1)}, f32[144,128]{1,0:T(8,128)S(1)}, bf16[8,8192]{1,0:T(8,128)(2,1)S(1)}) custom-call(s32[1,4,4]{2,1,0:T(4,128)S(1)} %copy-done, bf16[2,8,2048]{2,1,0:T(8,128)(2,1)S(1)} %bitcast.23, bf16[8192,256]{1,0:T(8,128)(2,1)S(1)} %get-tuple-element.32.refs_2_.refs_3_, f32[288,128]{1,0:T(8,128)S(1)} %get-tuple-element.33.refs_3_, ...), custom_call_target="tpu_custom_call" | custom-call | tf_op jit(solution)/shard_map/pallas_call | solution.py:363
  7.7 0.4 %collective-permute-start.7 = (f32[144,128]{1,0:T(8,128)S(1)}, f32[144,128]{1,0:T(8,128)S(1)}, u32[]{:S(2)}, u32[]{:S(2)}) collective-permute-start(f32[144,128]{1,0:T(8,128)S(1)} %get-tuple-element.36), channel_id=1, source_target_pairs={{0,1},{1,0},{2,3},{3,2},{4,5},{5,4},{6,7},{7,6},{8,9},{9,8},{10,11... | collective-permute-start | bytes 221192 | tf_op jit(solution)/shard_map/ppermute | solution.py:276
  8.1 0.9 %collective-permute-done.7 = f32[144,128]{1,0:T(8,128)S(1)} collective-permute-done((f32[144,128]{1,0:T(8,128)S(1)}, f32[144,128]{1,0:T(8,128)S(1)}, u32[]{:S(2)}, u32[]{:S(2)}) %collective-permute-start.7) | collective-permute-done | bytes 73760 | tf_op jit(solution)/shard_map/ppermute | solution.py:276
  9.1 2.0 %collective-permute-start.8 = (f32[144,128]{1,0:T(8,128)S(1)}, f32[144,128]{1,0:T(8,128)S(1)}, u32[]{:S(2)}, u32[]{:S(2)}) collective-permute-start(f32[144,128]{1,0:T(8,128)S(1)} %add.42), channel_id=1, source_target_pairs={{0,3},{1,8},{2,11},{3,0},{4,13},{5,6},{6,5},{7,14},{8,1},{9,10},{1... | collective-permute-start | bytes 221192 | tf_op jit(solution)/shard_map/ppermute | solution.py:276
  11.0 2.0 %collective-permute-done.8 = f32[144,128]{1,0:T(8,128)S(1)} collective-permute-done((f32[144,128]{1,0:T(8,128)S(1)}, f32[144,128]{1,0:T(8,128)S(1)}, u32[]{:S(2)}, u32[]{:S(2)}) %collective-permute-start.8) | collective-permute-done | bytes 73760 | tf_op jit(solution)/shard_map/ppermute | solution.py:276
  13.1 1.8 %collective-permute-start.9 = (f32[144,128]{1,0:T(8,128)S(1)}, f32[144,128]{1,0:T(8,128)S(1)}, u32[]{:S(2)}, u32[]{:S(2)}) collective-permute-start(f32[144,128]{1,0:T(8,128)S(1)} %add.43), channel_id=1, source_target_pairs={{0,5},{1,16},{2,19},{3,6},{4,21},{5,0},{6,3},{7,22},{8,25},{9,12},... | collective-permute-start | bytes 221192 | tf_op jit(solution)/shard_map/ppermute | solution.py:276
  14.9 2.0 %collective-permute-done.9 = f32[144,128]{1,0:T(8,128)S(1)} collective-permute-done((f32[144,128]{1,0:T(8,128)S(1)}, f32[144,128]{1,0:T(8,128)S(1)}, u32[]{:S(2)}, u32[]{:S(2)}) %collective-permute-start.9) | collective-permute-done | bytes 73760 | tf_op jit(solution)/shard_map/ppermute | solution.py:276
  17.0 2.2 %collective-permute-start.10 = (f32[144,128]{1,0:T(8,128)S(1)}, f32[144,128]{1,0:T(8,128)S(1)}, u32[]{:S(2)}, u32[]{:S(2)}) collective-permute-start(f32[144,128]{1,0:T(8,128)S(1)} %add.44), channel_id=1, source_target_pairs={{0,9},{1,2},{2,1},{3,10},{4,7},{5,12},{6,15},{7,4},{8,11},{9,0},{1... | collective-permute-start | bytes 221192 | tf_op jit(solution)/shard_map/ppermute | solution.py:276
  19.1 2.0 %collective-permute-done.10 = f32[144,128]{1,0:T(8,128)S(1)} collective-permute-done((f32[144,128]{1,0:T(8,128)S(1)}, f32[144,128]{1,0:T(8,128)S(1)}, u32[]{:S(2)}, u32[]{:S(2)}) %collective-permute-start.10) | collective-permute-done | bytes 73760 | tf_op jit(solution)/shard_map/ppermute | solution.py:276
  21.2 3.1 %collective-permute-start.11 = (f32[144,128]{1,0:T(8,128)S(1)}, f32[144,128]{1,0:T(8,128)S(1)}, u32[]{:S(2)}, u32[]{:S(2)}) collective-permute-start(f32[144,128]{1,0:T(8,128)S(1)} %add.45), channel_id=1, source_target_pairs={{0,17},{1,4},{2,7},{3,18},{4,1},{5,20},{6,23},{7,2},{8,13},{9,24},... | collective-permute-start | bytes 221192 | tf_op jit(solution)/shard_map/ppermute | solution.py:276
  24.3 2.0 %collective-permute-done.11 = f32[144,128]{1,0:T(8,128)S(1)} collective-permute-done((f32[144,128]{1,0:T(8,128)S(1)}, f32[144,128]{1,0:T(8,128)S(1)}, u32[]{:S(2)}, u32[]{:S(2)}) %collective-permute-start.11) | collective-permute-done | bytes 73760 | tf_op jit(solution)/shard_map/ppermute | solution.py:276
  26.3 0.2 collective-permute-start.12
  26.5 1.2 %collective-permute-done.12.refs_1_ = f32[144,128]{1,0:T(8,128)S(1)} collective-permute-done((f32[144,128]{1,0:T(8,128)S(1)}, f32[144,128]{1,0:T(8,128)S(1)}, u32[]{:S(2)}, u32[]{:S(2)}) %collective-permute-start.12) | collective-permute-done | bytes 73760 | tf_op jit(solution)/shard_map/ppermute | solution.py:276
  27.7 1.5 %shard_map.62 = (bf16[8,8192]{1,0:T(8,128)(2,1)S(1)}, f32[8,256]{1,0:T(8,128)}, f32[8,8]{1,0:T(8,128)S(1)}, s32[1,1]{1,0:T(1,128)}) custom-call(f32[144,128]{1,0:T(8,128)S(1)} %add.46.refs_0_, f32[144,128]{1,0:T(8,128)S(1)} %collective-permute-done.12.refs_1_, bf16[8,8192]{1,0:T(8,128)(2,1)S(1)} %get-tuple-element.37.refs_2_, ...), custom_call_target="tpu_custom_call" | custom-call | tf_op jit(solution)/shard_map/pallas_call | solution.py:377
  29.2 0.7 %conditional.1 = ((bf16[8,8192]{1,0:T(8,128)(2,1)S(1)}, f32[8,8]{1,0:T(8,128)S(1)})) conditional(s32[]{:T(128)} %bitcast.10, (bf16[8,8192]{1,0:T(8,128)(2,1)S(1)}, f32[8,8]{1,0:T(8,128)S(1)}) %tuple.15, (bf16[8,8192]{1,0:T(8,128)(2,1)S(1)}, f32[8,256]{1,0:T(8,128)}, bf16[8192,256]{1,0:T(8,128)(2,1)S(1)}) %tuple.27), branch_computations={%region_0.0_spmd, %region_1.0_spmd} | conditional | flops 46336968 | bytes 5263650 | solution.py:400
  29.8 0.0 copy-start.3
  29.8 0.0 copy-start.4
  29.9 0.6 %copy-done.3 = bf16[8,8192]{1,0:T(8,128)(2,1)} copy-done((bf16[8,8192]{1,0:T(8,128)(2,1)}, bf16[8,8192]{1,0:T(8,128)(2,1)S(1)}, u32[]{:S(2)}) %copy-start.3) | copy-done | bytes 131096
  30.5 0.0 copy-done.4
  (6 shorter events, 0.1 us)
Async XLA Ops:
  0.6 4.4 %copy-start = (s32[1,4,4]{2,1,0:T(4,128)S(1)}, s32[1,4,4]{2,1,0:T(4,128)}, u32[]{:S(2)}) copy-start(s32[1,4,4]{2,1,0:T(4,128)} %refs_0_.3) | copy-start | bytes 196
  0.6 1.8 %collective-permute-start.5 = (bf16[4,8,2048]{2,1,0:T(8,128)(2,1)}, bf16[4,8,2048]{2,1,0:T(8,128)(2,1)S(1)}, u32[]{:S(2)}, u32[]{:S(2)}) collective-permute-start(bf16[4,8,2048]{2,1,0:T(8,128)(2,1)} %bitcast.25), channel_id=1, source_target_pairs={{0,1},{1,0},{2,3},{3,2},{4,5},{5,4},{6,7},{7,6},{8,9},{9,8},{10,11... | collective-permute-start | bytes 393224 | tf_op jit(solution)/shard_map/ppermute | solution.py:276
  1.2 0.9 %copy-start.1 = (bf16[8,8192]{1,0:T(8,128)(2,1)S(1)}, bf16[8,8192]{1,0:T(8,128)(2,1)}, u32[]{:S(2)}) copy-start(bf16[8,8192]{1,0:T(8,128)(2,1)} %param.5) | copy-start | bytes 393220
  2.1 3.0 %copy-start.2 = (bf16[8192,256]{1,0:T(8,128)(2,1)S(1)}, bf16[8192,256]{1,0:T(8,128)(2,1)}, u32[]{:S(2)}) copy-start(bf16[8192,256]{1,0:T(8,128)(2,1)} %refs_2_.1) | copy-start | bytes 12582916
  2.4 4.8 %collective-permute-start.6 = (bf16[2,1,8,2048]{3,2,0,1:T(8,128)(2,1)S(1)}, bf16[2,1,8,2048]{3,2,0,1:T(8,128)(2,1)S(1)}, u32[]{:S(2)}, u32[]{:S(2)}) collective-permute-start(bf16[2,1,8,2048]{3,2,0,1:T(8,128)(2,1)S(1)} %bitcast.27), channel_id=1, source_target_pairs={{0,3},{1,2},{2,1},{3,0},{4,7},{5,6},{6,5},{7,4},{8,11},{9,10},{10,... | collective-permute-start | bytes 196616 | tf_op jit(solution)/shard_map/ppermute | solution.py:276
  7.7 1.3 %collective-permute-start.7 = (f32[144,128]{1,0:T(8,128)S(1)}, f32[144,128]{1,0:T(8,128)S(1)}, u32[]{:S(2)}, u32[]{:S(2)}) collective-permute-start(f32[144,128]{1,0:T(8,128)S(1)} %get-tuple-element.36), channel_id=1, source_target_pairs={{0,1},{1,0},{2,3},{3,2},{4,5},{5,4},{6,7},{7,6},{8,9},{9,8},{10,11... | collective-permute-start | bytes 221192 | tf_op jit(solution)/shard_map/ppermute | solution.py:276
  9.1 4.0 %collective-permute-start.8 = (f32[144,128]{1,0:T(8,128)S(1)}, f32[144,128]{1,0:T(8,128)S(1)}, u32[]{:S(2)}, u32[]{:S(2)}) collective-permute-start(f32[144,128]{1,0:T(8,128)S(1)} %add.42), channel_id=1, source_target_pairs={{0,3},{1,8},{2,11},{3,0},{4,13},{5,6},{6,5},{7,14},{8,1},{9,10},{1... | collective-permute-start | bytes 221192 | tf_op jit(solution)/shard_map/ppermute | solution.py:276
  13.1 3.9 %collective-permute-start.9 = (f32[144,128]{1,0:T(8,128)S(1)}, f32[144,128]{1,0:T(8,128)S(1)}, u32[]{:S(2)}, u32[]{:S(2)}) collective-permute-start(f32[144,128]{1,0:T(8,128)S(1)} %add.43), channel_id=1, source_target_pairs={{0,5},{1,16},{2,19},{3,6},{4,21},{5,0},{6,3},{7,22},{8,25},{9,12},... | collective-permute-start | bytes 221192 | tf_op jit(solution)/shard_map/ppermute | solution.py:276
  17.0 4.2 %collective-permute-start.10 = (f32[144,128]{1,0:T(8,128)S(1)}, f32[144,128]{1,0:T(8,128)S(1)}, u32[]{:S(2)}, u32[]{:S(2)}) collective-permute-start(f32[144,128]{1,0:T(8,128)S(1)} %add.44), channel_id=1, source_target_pairs={{0,9},{1,2},{2,1},{3,10},{4,7},{5,12},{6,15},{7,4},{8,11},{9,0},{1... | collective-permute-start | bytes 221192 | tf_op jit(solution)/shard_map/ppermute | solution.py:276
  21.2 5.2 %collective-permute-start.11 = (f32[144,128]{1,0:T(8,128)S(1)}, f32[144,128]{1,0:T(8,128)S(1)}, u32[]{:S(2)}, u32[]{:S(2)}) collective-permute-start(f32[144,128]{1,0:T(8,128)S(1)} %add.45), channel_id=1, source_target_pairs={{0,17},{1,4},{2,7},{3,18},{4,1},{5,20},{6,23},{7,2},{8,13},{9,24},... | collective-permute-start | bytes 221192 | tf_op jit(solution)/shard_map/ppermute | solution.py:276
  26.3 1.3 %collective-permute-start.12 = (f32[144,128]{1,0:T(8,128)S(1)}, f32[144,128]{1,0:T(8,128)S(1)}, u32[]{:S(2)}, u32[]{:S(2)}) collective-permute-start(f32[144,128]{1,0:T(8,128)S(1)} %add.46.refs_0_), channel_id=1, source_target_pairs={{0,1},{1,0},{2,3},{3,2},{4,5},{5,4},{6,7},{7,6},{8,9},{9,8},{10,11... | collective-permute-start | bytes 221192 | tf_op jit(solution)/shard_map/ppermute | solution.py:276
  29.8 0.7 %copy-start.3 = (bf16[8,8192]{1,0:T(8,128)(2,1)}, bf16[8,8192]{1,0:T(8,128)(2,1)S(1)}, u32[]{:S(2)}) copy-start(bf16[8,8192]{1,0:T(8,128)(2,1)S(1)} %get-tuple-element.46) | copy-start | bytes 393220
  29.8 0.6 %copy-start.4 = (f32[8,8]{1,0:T(8,128)}, f32[8,8]{1,0:T(8,128)S(1)}, u32[]{:S(2)}) copy-start(f32[8,8]{1,0:T(8,128)S(1)} %get-tuple-element.49) | copy-start | bytes 772
